TPU v7x, 256 devices: a whole 4x4x8 slice. The times are simulated.
256 devices in a mesh: tx: 16 (over z, core), gx: 8 (over x, y_lo), gy: 2 (over y_hi).
Axes of the slice: x: 4, y: 4 (y_hi: 2, y_lo: 2; y = y_hi * 2 + y_lo), z: 8, core: 2. Of those that a mesh axis runs over, the one named last changes fastest.
Arguments:
- cond_h: float32 [128, 32, 128], P('gx', 'gy'), may hold values from 0.1 to 1.5
- cond_v: float32 [128, 32, 128], P('gx', 'gy'), may hold values from 0.1 to 1.5
- fwd_init: float32 [16, 6, 128, 32, 128], P('tx', None, 'gx', 'gy'), may hold values from -6 to 6
- adj_init: float32 [16, 6, 128, 32, 128], P('tx', None, 'gx', 'gy'), may hold values from -6 to 6
- observed: float32 [16, 4, 8, 2, 2, 32], P('tx', None, 'gx', 'gy'), may hold values from -6 to 6
- footprint: int32 [16, 8, 2], P('tx', 'gx', 'gy'), may hold values 0 or 1
- owner: int32 [8, 2, 16], P('gx', 'gy'), may hold values from 0 to 15, each once within a row
- rec_cells: int32 [8, 2, 32], P('gx', 'gy'), may hold values from 0 to 255
Outputs:
- owned_gradient: float32 [8, 16, 2, 1, 32, 128], P('gx', 'tx', None, None, 'gy')
- misfit: float32 [], replicated
Inputs may be any that keep to these rules, and one draw needn't show every extreme that they name: `owner`: each tile's row is a permutation of 0 to 15. `rec_cells`: cell index x * 16 + y within the tile; receivers may share a cell. `footprint`: 1 where the group's gradient counts in the tile.
All inputs are finite; a program needn't handle non-finite values.
Results may differ from a plain program's by a relative error of at most 0.00028.
Values sent between devices are 32-bit elements; how exact they have to be, the bound alone decides.
No kernel may reach another device: no remote copies, remote signals or barrier semaphores. Data moves between devices by JAX's collectives and lax.ppermute only.
A program may use at most 64 MiB of HBM per device.

v0:
```python
import jax
import jax.numpy as jnp
from jax import lax
from jax.sharding import PartitionSpec as P

STEPS = 4
ZREC = 32


STEP_DT = 0.5


def shifted(x, axis, by):
    size = lax.axis_size(axis)
    pairs = [(i, i + by) for i in range(size) if 0 <= i + by < size]
    return lax.ppermute(x, axis, pairs)


def coefficients(conduct):
    half_rate = 0.25 * conduct
    return ((1.0 - half_rate) / (1.0 + half_rate), STEP_DT / (1.0 + half_rate))


def ahead_of(values, tail_plane, axis_num):
    extent = values.shape[axis_num]
    return jnp.concatenate(
        [lax.slice_in_dim(values, 1, extent, axis=axis_num), tail_plane], axis=axis_num
    )


def before(values, head_plane, axis_num):
    extent = values.shape[axis_num]
    return jnp.concatenate(
        [head_plane, lax.slice_in_dim(values, 0, extent - 1, axis=axis_num)], axis=axis_num
    )


def zero_plane(values, axis_num):
    return jnp.zeros_like(lax.slice_in_dim(values, 0, 1, axis=axis_num))


def curl_ahead(field, next_x, next_y):
    comp_x, comp_y, comp_z = (field[0], field[1], field[2])
    out_x = (
        ahead_of(comp_z, next_y[1], 1)
        - comp_z
        - (ahead_of(comp_y, zero_plane(comp_y, 2), 2) - comp_y)
    )
    out_y = (
        ahead_of(comp_x, zero_plane(comp_x, 2), 2)
        - comp_x
        - (ahead_of(comp_z, next_x[1], 0) - comp_z)
    )
    out_z = ahead_of(comp_y, next_x[0], 0) - comp_y - (ahead_of(comp_x, next_y[0], 1) - comp_x)
    return jnp.stack([out_x, out_y, out_z])


def curl_before(field, prev_x, prev_y):
    comp_x, comp_y, comp_z = (field[0], field[1], field[2])
    out_x = (
        comp_z - before(comp_z, prev_y[1], 1) - (comp_y - before(comp_y, zero_plane(comp_y, 2), 2))
    )
    out_y = (
        comp_x - before(comp_x, zero_plane(comp_x, 2), 2) - (comp_z - before(comp_z, prev_x[1], 0))
    )
    out_z = comp_y - before(comp_y, prev_x[0], 0) - (comp_x - before(comp_x, prev_y[0], 1))
    return jnp.stack([out_x, out_y, out_z])


def electric_rims(electric):
    next_x = shifted(electric[1:3, 0:1], "gx", -1)
    next_y = shifted(electric[0::2, :, 0:1], "gy", -1)
    return (next_x, next_y)


def magnetic_rims(magnetic):
    size_x = magnetic.shape[1]
    size_y = magnetic.shape[2]
    prev_x = shifted(magnetic[1:3, size_x - 1 : size_x], "gx", 1)
    prev_y = shifted(magnetic[0::2, :, size_y - 1 : size_y], "gy", 1)
    return (prev_x, prev_y)


def advance(electric, magnetic, decay, drive):
    next_x, next_y = electric_rims(electric)
    magnetic = magnetic - STEP_DT * curl_ahead(electric, next_x, next_y)
    prev_x, prev_y = magnetic_rims(magnetic)
    electric = decay * electric + drive * curl_before(magnetic, prev_x, prev_y)
    return (electric, magnetic)


def on_device(cond_h, cond_v, fwd_init, adj_init, observed, footprint, owner, rec_cells):
    size_x, size_y, depth = cond_h.shape
    decay_h, drive_h = coefficients(cond_h)
    decay_v, drive_v = coefficients(cond_v)
    highest = lax.Precision.HIGHEST
    cell_ids = jnp.arange(size_x * size_y, dtype=jnp.int32)
    onehot = (rec_cells[0, 0][:, None] == cell_ids[None, :]).astype(jnp.float32)
    observe = observed[0, :, 0, 0]
    grad_h = jnp.zeros((size_x, size_y, depth), jnp.float32)
    grad_v = jnp.zeros((size_x, size_y, depth), jnp.float32)
    residuals = []
    decay = jnp.stack([decay_h, decay_h, decay_v])
    drive = jnp.stack([drive_h, drive_h, drive_v])
    electric, magnetic = (fwd_init[0, 0:3], fwd_init[0, 3:6])
    stored = []
    for step_idx in range(STEPS):
        electric, magnetic = advance(electric, magnetic, decay, drive)
        stored.append(electric)
        planes = electric[0:2, :, :, ZREC].reshape(2, size_x * size_y)
        residuals.append(jnp.dot(planes, onehot.T, precision=highest) - observe[step_idx])
    adj_e, adj_h = (adj_init[0, 0:3], adj_init[0, 3:6])
    for step_idx in reversed(range(STEPS)):
        adj_e = adj_e.at[0:2, :, :, ZREC].add(
            jnp.dot(residuals[step_idx], onehot, precision=highest).reshape(2, size_x, size_y)
        )
        adj_e, adj_h = advance(adj_e, adj_h, decay, drive)
        kept = stored[step_idx]
        grad_h = grad_h + adj_e[0] * kept[0] + adj_e[1] * kept[1]
        grad_v = grad_v + adj_e[2] * kept[2]
    local_misfit = jnp.float32(0.0)
    for step_idx in range(STEPS):
        local_misfit = local_misfit + 0.5 * jnp.sum(residuals[step_idx] * residuals[step_idx])
    misfit = lax.psum(local_misfit, ("tx", "gx", "gy"))
    tile_flag = footprint[0, 0, 0].astype(jnp.float32)
    gradient = jnp.stack([grad_h, grad_v]) * tile_flag
    groups_count = lax.axis_size("tx")
    block_rows = size_x // groups_count
    blocked = gradient.reshape(2, groups_count, block_rows, size_y, depth)
    ordered = jnp.take(blocked, owner[0, 0], axis=1)
    summed = lax.psum_scatter(ordered, "tx", scatter_dimension=1, tiled=True)
    owned_part = summed.reshape(1, 1, 2, block_rows, size_y, depth)
    return (owned_part, misfit)


def solution(mesh):
    placed = (
        P("gx", "gy", None),
        P("gx", "gy", None),
        P("tx", None, "gx", "gy", None),
        P("tx", None, "gx", "gy", None),
        P("tx", None, "gx", "gy", None, None),
        P("tx", "gx", "gy"),
        P("gx", "gy", None),
        P("gx", "gy", None),
    )
    return jax.shard_map(
        on_device,
        mesh=mesh,
        in_specs=placed,
        out_specs=(P("gx", "tx", None, None, "gy", None), P()),
        check_vma=False,
    )
```

profile of v0, /device:TPU:1, one launch (start us, length us, event | category | flops | bytes accessed | tf_op | source)
XLA Modules:
  0.0 326.6 jit_solution(11279298193173657843)
XLA Ops:
  19.2 5.6 %collective-permute-start.2 = (f32[2,16,1,128]{3,1,2,0:T(8,128)S(1)}, f32[2,16,1,128]{3,1,2,0:T(8,128)S(1)}, u32[]{:S(2)}, u32[]{:S(2)}) collective-permute-start(f32[2,16,1,128]{3,1,2,0:T(8,128)S(1)} %bitcast.592), channel_id=1, source_target_pairs={{0,1},{2,3},{4,5},{6,7},{8,9},{10,11},{12,13},{14,15},{16,17},{18,... | collective-permute-start | bytes 49160 | tf_op jit(solution)/shard_map/ppermute | solution.py:16
  24.9 4.5 %collective-permute-start.3 = (f32[2,1,16,128]{3,2,1,0:T(8,128)S(1)}, f32[2,1,16,128]{3,2,1,0:T(8,128)S(1)}, u32[]{:S(2)}, u32[]{:S(2)}) collective-permute-start(f32[2,1,16,128]{3,2,1,0:T(8,128)S(1)} %slice.1340), channel_id=1, source_target_pairs={{0,2},{2,4},{4,6},{6,8},{8,10},{10,12},{12,14},{1,3},{3,5},{5,7},{... | collective-permute-start | bytes 49160 | tf_op jit(solution)/shard_map/ppermute | solution.py:16
  41.6 6.1 %collective-permute-start.6 = (f32[2,16,1,128]{3,1,2,0:T(8,128)S(1)}, f32[2,16,1,128]{3,1,2,0:T(8,128)S(1)}, u32[]{:S(2)}, u32[]{:S(2)}) collective-permute-start(f32[2,16,1,128]{3,1,2,0:T(8,128)S(1)} %bitcast.593), channel_id=1, source_target_pairs={{0,1},{2,3},{4,5},{6,7},{8,9},{10,11},{12,13},{14,15},{16,17},{18,... | collective-permute-start | bytes 49160 | tf_op jit(solution)/shard_map/ppermute | solution.py:16
  47.8 3.7 %collective-permute-start.7 = (f32[2,1,16,128]{3,2,1,0:T(8,128)S(1)}, f32[2,1,16,128]{3,2,1,0:T(8,128)S(1)}, u32[]{:S(2)}, u32[]{:S(2)}) collective-permute-start(f32[2,1,16,128]{3,2,1,0:T(8,128)S(1)} %slice.1368), channel_id=1, source_target_pairs={{0,2},{2,4},{4,6},{6,8},{8,10},{10,12},{12,14},{1,3},{3,5},{5,7},{... | collective-permute-start | bytes 49160 | tf_op jit(solution)/shard_map/ppermute | solution.py:16
  68.3 6.1 %collective-permute-start.10 = (f32[2,16,1,128]{3,1,2,0:T(8,128)S(1)}, f32[2,16,1,128]{3,1,2,0:T(8,128)S(1)}, u32[]{:S(2)}, u32[]{:S(2)}) collective-permute-start(f32[2,16,1,128]{3,1,2,0:T(8,128)S(1)} %bitcast.594), channel_id=1, source_target_pairs={{0,1},{2,3},{4,5},{6,7},{8,9},{10,11},{12,13},{14,15},{16,17},{18,... | collective-permute-start | bytes 49160 | tf_op jit(solution)/shard_map/ppermute | solution.py:16
  74.5 3.7 %collective-permute-start.11 = (f32[2,1,16,128]{3,2,1,0:T(8,128)S(1)}, f32[2,1,16,128]{3,2,1,0:T(8,128)S(1)}, u32[]{:S(2)}, u32[]{:S(2)}) collective-permute-start(f32[2,1,16,128]{3,2,1,0:T(8,128)S(1)} %slice.1396), channel_id=1, source_target_pairs={{0,2},{2,4},{4,6},{6,8},{8,10},{10,12},{12,14},{1,3},{3,5},{5,7},{... | collective-permute-start | bytes 49160 | tf_op jit(solution)/shard_map/ppermute | solution.py:16
  97.4 5.9 %collective-permute-start.14 = (f32[2,16,1,128]{3,1,2,0:T(8,128)S(1)}, f32[2,16,1,128]{3,1,2,0:T(8,128)S(1)}, u32[]{:S(2)}, u32[]{:S(2)}) collective-permute-start(f32[2,16,1,128]{3,1,2,0:T(8,128)S(1)} %bitcast.595), channel_id=1, source_target_pairs={{0,1},{2,3},{4,5},{6,7},{8,9},{10,11},{12,13},{14,15},{16,17},{18,... | collective-permute-start | bytes 49160 | tf_op jit(solution)/shard_map/ppermute | solution.py:16
  103.3 3.7 %collective-permute-start.15 = (f32[2,1,16,128]{3,2,1,0:T(8,128)S(1)}, f32[2,1,16,128]{3,2,1,0:T(8,128)S(1)}, u32[]{:S(2)}, u32[]{:S(2)}) collective-permute-start(f32[2,1,16,128]{3,2,1,0:T(8,128)S(1)} %slice.1424), channel_id=1, source_target_pairs={{0,2},{2,4},{4,6},{6,8},{8,10},{10,12},{12,14},{1,3},{3,5},{5,7},{... | collective-permute-start | bytes 49160 | tf_op jit(solution)/shard_map/ppermute | solution.py:16
  114.3 3.6 %scatter-add.14 = f32[3,16,16,128]{3,2,1,0:T(8,128)S(1)} dynamic-update-slice(f32[3,16,16,128]{3,2,1,0:T(8,128)S(1)} %get-tuple-element.51, f32[2,16,16,1]{3,2,1,0:T(8,128)S(1)} %add_select_fusion.3, s32[]{:T(128)} %bitcast.4, s32[]{:T(128)} %constant.106.clone.1, s32[]{:T(128)} %constant.106.clone.1, s32[]{:T(128)} %bitcast.5) | dynamic-update-slice | bytes 4100 | tf_op jit(solution)/shard_map/scatter-add | solution.py:114
  120.7 3.3 collective-permute-done.16
  126.3 6.1 %collective-permute-start.18 = (f32[2,16,1,128]{3,1,2,0:T(8,128)S(1)}, f32[2,16,1,128]{3,1,2,0:T(8,128)S(1)}, u32[]{:S(2)}, u32[]{:S(2)}) collective-permute-start(f32[2,16,1,128]{3,1,2,0:T(8,128)S(1)} %bitcast.596), channel_id=1, source_target_pairs={{0,1},{2,3},{4,5},{6,7},{8,9},{10,11},{12,13},{14,15},{16,17},{18,... | collective-permute-start | bytes 49160 | tf_op jit(solution)/shard_map/ppermute | solution.py:16
  132.4 3.7 %collective-permute-start.19 = (f32[2,1,16,128]{3,2,1,0:T(8,128)S(1)}, f32[2,1,16,128]{3,2,1,0:T(8,128)S(1)}, u32[]{:S(2)}, u32[]{:S(2)}) collective-permute-start(f32[2,1,16,128]{3,2,1,0:T(8,128)S(1)} %slice.1453), channel_id=1, source_target_pairs={{0,2},{2,4},{4,6},{6,8},{8,10},{10,12},{12,14},{1,3},{3,5},{5,7},{... | collective-permute-start | bytes 49160 | tf_op jit(solution)/shard_map/ppermute | solution.py:16
  140.3 3.6 %scatter-add.15 = f32[3,16,16,128]{3,2,1,0:T(8,128)S(1)} dynamic-update-slice(f32[3,16,16,128]{3,2,1,0:T(8,128)S(1)} %copy.87, f32[2,16,16,1]{3,2,1,0:T(8,128)S(1)} %add_select_fusion.2, s32[]{:T(128)} %bitcast.4, s32[]{:T(128)} %constant.106.clone.1, s32[]{:T(128)} %constant.106.clone.1, s32[]{:T(128)} %bitcast.5) | dynamic-update-slice | bytes 4100 | tf_op jit(solution)/shard_map/scatter-add | solution.py:114
  146.7 3.3 collective-permute-done.20
  151.7 6.1 %collective-permute-start.22 = (f32[2,16,1,128]{3,1,2,0:T(8,128)S(1)}, f32[2,16,1,128]{3,1,2,0:T(8,128)S(1)}, u32[]{:S(2)}, u32[]{:S(2)}) collective-permute-start(f32[2,16,1,128]{3,1,2,0:T(8,128)S(1)} %bitcast.597), channel_id=1, source_target_pairs={{0,1},{2,3},{4,5},{6,7},{8,9},{10,11},{12,13},{14,15},{16,17},{18,... | collective-permute-start | bytes 49160 | tf_op jit(solution)/shard_map/ppermute | solution.py:16
  157.8 3.7 %collective-permute-start.23 = (f32[2,1,16,128]{3,2,1,0:T(8,128)S(1)}, f32[2,1,16,128]{3,2,1,0:T(8,128)S(1)}, u32[]{:S(2)}, u32[]{:S(2)}) collective-permute-start(f32[2,1,16,128]{3,2,1,0:T(8,128)S(1)} %slice.1486), channel_id=1, source_target_pairs={{0,2},{2,4},{4,6},{6,8},{8,10},{10,12},{12,14},{1,3},{3,5},{5,7},{... | collective-permute-start | bytes 49160 | tf_op jit(solution)/shard_map/ppermute | solution.py:16
  165.6 3.6 %scatter-add.16 = f32[3,16,16,128]{3,2,1,0:T(8,128)S(1)} dynamic-update-slice(f32[3,16,16,128]{3,2,1,0:T(8,128)S(1)} %copy.88, f32[2,16,16,1]{3,2,1,0:T(8,128)S(1)} %add_select_fusion.1, s32[]{:T(128)} %bitcast.4, s32[]{:T(128)} %constant.106.clone.1, s32[]{:T(128)} %constant.106.clone.1, s32[]{:T(128)} %bitcast.5) | dynamic-update-slice | bytes 4100 | tf_op jit(solution)/shard_map/scatter-add | solution.py:114
  177.5 6.1 %collective-permute-start.26 = (f32[2,16,1,128]{3,1,2,0:T(8,128)S(1)}, f32[2,16,1,128]{3,1,2,0:T(8,128)S(1)}, u32[]{:S(2)}, u32[]{:S(2)}) collective-permute-start(f32[2,16,1,128]{3,1,2,0:T(8,128)S(1)} %bitcast.598), channel_id=1, source_target_pairs={{0,1},{2,3},{4,5},{6,7},{8,9},{10,11},{12,13},{14,15},{16,17},{18,... | collective-permute-start | bytes 49160 | tf_op jit(solution)/shard_map/ppermute | solution.py:16
  183.6 3.7 %collective-permute-start.27 = (f32[2,1,16,128]{3,2,1,0:T(8,128)S(1)}, f32[2,1,16,128]{3,2,1,0:T(8,128)S(1)}, u32[]{:S(2)}, u32[]{:S(2)}) collective-permute-start(f32[2,1,16,128]{3,2,1,0:T(8,128)S(1)} %slice.1517), channel_id=1, source_target_pairs={{0,2},{2,4},{4,6},{6,8},{8,10},{10,12},{12,14},{1,3},{3,5},{5,7},{... | collective-permute-start | bytes 49160 | tf_op jit(solution)/shard_map/ppermute | solution.py:16
  191.6 3.6 %scatter-add.19 = f32[3,16,16,128]{3,2,1,0:T(8,128)S(1)} dynamic-update-slice(f32[3,16,16,128]{3,2,1,0:T(8,128)S(1)} %copy.89, f32[2,16,16,1]{3,2,1,0:T(8,128)S(1)} %add_select_fusion, s32[]{:T(128)} %bitcast.4, s32[]{:T(128)} %constant.106.clone.1, s32[]{:T(128)} %constant.106.clone.1, s32[]{:T(128)} %bitcast.5) | dynamic-update-slice | bytes 4100 | tf_op jit(solution)/shard_map/scatter-add | solution.py:114
  198.0 3.3 collective-permute-done.28
  203.1 6.1 %collective-permute-start.30 = (f32[2,16,1,128]{3,1,2,0:T(8,128)S(1)}, f32[2,16,1,128]{3,1,2,0:T(8,128)S(1)}, u32[]{:S(2)}, u32[]{:S(2)}) collective-permute-start(f32[2,16,1,128]{3,1,2,0:T(8,128)S(1)} %bitcast.599), channel_id=1, source_target_pairs={{0,1},{2,3},{4,5},{6,7},{8,9},{10,11},{12,13},{14,15},{16,17},{18,... | collective-permute-start | bytes 49160 | tf_op jit(solution)/shard_map/ppermute | solution.py:16
  209.3 3.7 %collective-permute-start.31 = (f32[2,1,16,128]{3,2,1,0:T(8,128)S(1)}, f32[2,1,16,128]{3,2,1,0:T(8,128)S(1)}, u32[]{:S(2)}, u32[]{:S(2)}) collective-permute-start(f32[2,1,16,128]{3,2,1,0:T(8,128)S(1)} %slice.1548), channel_id=1, source_target_pairs={{0,2},{2,4},{4,6},{6,8},{8,10},{10,12},{12,14},{1,3},{3,5},{5,7},{... | collective-permute-start | bytes 49160 | tf_op jit(solution)/shard_map/ppermute | solution.py:16
  219.5 100.3 %psum.7 = f32[]{:T(128)} all-reduce(f32[]{:T(128)S(6)} %add.229), channel_id=1, replica_groups=mesh['tx'=16,'gx'=8,'gy'=2] {'tx','gx','gy'}, use_global_device_ids=true, to_apply=%region_6.0 | all-reduce | flops 1 | bytes 8 | tf_op jit(solution)/shard_map/psum | solution.py:124
  (437 shorter events, 104.6 us)
Async XLA Ops:
  7.2 312.6 %reduce-scatter.2.cloned.1.call-start = ((), (), s32[]{:S(2)}) async-start(), calls=%async_computation.1 | async-start | bytes 278528 | tf_op jit(solution)/shard_map/reduce_scatter | solution.py:131
  8.3 10.5 %collective-permute-start = (f32[2,16,1,128]{3,2,1,0:T(1,128)S(1)}, f32[2,16,1,128]{3,2,1,0:T(1,128)S(1)}, u32[]{:S(2)}, u32[]{:S(2)}) collective-permute-start(f32[2,16,1,128]{3,2,1,0:T(1,128)S(1)} %slice.1044), channel_id=1, source_target_pairs={{1,0},{3,2},{5,4},{7,6},{9,8},{11,10},{13,12},{15,14},{17,16},{19,... | collective-permute-start | bytes 49160 | tf_op jit(solution)/shard_map/ppermute | solution.py:16
  9.6 9.2 %collective-permute-start.1 = (f32[2,1,16,128]{3,2,1,0:T(8,128)S(1)}, f32[2,1,16,128]{3,2,1,0:T(8,128)S(1)}, u32[]{:S(2)}, u32[]{:S(2)}) collective-permute-start(f32[2,1,16,128]{3,2,1,0:T(8,128)S(1)} %slice.1328), channel_id=1, source_target_pairs={{2,0},{4,2},{6,4},{8,6},{10,8},{12,10},{14,12},{3,1},{5,3},{7,5},{... | collective-permute-start | bytes 49160 | tf_op jit(solution)/shard_map/ppermute | solution.py:16
  19.2 10.2 %collective-permute-start.2 = (f32[2,16,1,128]{3,1,2,0:T(8,128)S(1)}, f32[2,16,1,128]{3,1,2,0:T(8,128)S(1)}, u32[]{:S(2)}, u32[]{:S(2)}) collective-permute-start(f32[2,16,1,128]{3,1,2,0:T(8,128)S(1)} %bitcast.592), channel_id=1, source_target_pairs={{0,1},{2,3},{4,5},{6,7},{8,9},{10,11},{12,13},{14,15},{16,17},{18,... | collective-permute-start | bytes 49160 | tf_op jit(solution)/shard_map/ppermute | solution.py:16
  24.9 5.4 %collective-permute-start.3 = (f32[2,1,16,128]{3,2,1,0:T(8,128)S(1)}, f32[2,1,16,128]{3,2,1,0:T(8,128)S(1)}, u32[]{:S(2)}, u32[]{:S(2)}) collective-permute-start(f32[2,1,16,128]{3,2,1,0:T(8,128)S(1)} %slice.1340), channel_id=1, source_target_pairs={{0,2},{2,4},{4,6},{6,8},{8,10},{10,12},{12,14},{1,3},{3,5},{5,7},{... | collective-permute-start | bytes 49160 | tf_op jit(solution)/shard_map/ppermute | solution.py:16
  32.5 6.0 %collective-permute-start.4 = (f32[2,16,1,128]{3,2,1,0:T(1,128)S(1)}, f32[2,16,1,128]{3,2,1,0:T(1,128)S(1)}, u32[]{:S(2)}, u32[]{:S(2)}) collective-permute-start(f32[2,16,1,128]{3,2,1,0:T(1,128)S(1)} %slice.1076), channel_id=1, source_target_pairs={{1,0},{3,2},{5,4},{7,6},{9,8},{11,10},{13,12},{15,14},{17,16},{19,... | collective-permute-start | bytes 49160 | tf_op jit(solution)/shard_map/ppermute | solution.py:16
  33.8 6.0 %collective-permute-start.5 = (f32[2,1,16,128]{3,2,1,0:T(8,128)S(1)}, f32[2,1,16,128]{3,2,1,0:T(8,128)S(1)}, u32[]{:S(2)}, u32[]{:S(2)}) collective-permute-start(f32[2,1,16,128]{3,2,1,0:T(8,128)S(1)} %slice.1355), channel_id=1, source_target_pairs={{2,0},{4,2},{6,4},{8,6},{10,8},{12,10},{14,12},{3,1},{5,3},{7,5},{... | collective-permute-start | bytes 49160 | tf_op jit(solution)/shard_map/ppermute | solution.py:16
  41.6 9.8 %collective-permute-start.6 = (f32[2,16,1,128]{3,1,2,0:T(8,128)S(1)}, f32[2,16,1,128]{3,1,2,0:T(8,128)S(1)}, u32[]{:S(2)}, u32[]{:S(2)}) collective-permute-start(f32[2,16,1,128]{3,1,2,0:T(8,128)S(1)} %bitcast.593), channel_id=1, source_target_pairs={{0,1},{2,3},{4,5},{6,7},{8,9},{10,11},{12,13},{14,15},{16,17},{18,... | collective-permute-start | bytes 49160 | tf_op jit(solution)/shard_map/ppermute | solution.py:16
  57.8 6.0 %collective-permute-start.8 = (f32[2,16,1,128]{3,2,1,0:T(1,128)S(1)}, f32[2,16,1,128]{3,2,1,0:T(1,128)S(1)}, u32[]{:S(2)}, u32[]{:S(2)}) collective-permute-start(f32[2,16,1,128]{3,2,1,0:T(1,128)S(1)} %copy-done.74), channel_id=1, source_target_pairs={{1,0},{3,2},{5,4},{7,6},{9,8},{11,10},{13,12},{15,14},{17,16},{19,... | collective-permute-start | bytes 49160 | tf_op jit(solution)/shard_map/ppermute | solution.py:16
  59.1 5.9 %collective-permute-start.9 = (f32[2,1,16,128]{3,2,1,0:T(8,128)S(1)}, f32[2,1,16,128]{3,2,1,0:T(8,128)S(1)}, u32[]{:S(2)}, u32[]{:S(2)}) collective-permute-start(f32[2,1,16,128]{3,2,1,0:T(8,128)S(1)} %copy-done.72), channel_id=1, source_target_pairs={{2,0},{4,2},{6,4},{8,6},{10,8},{12,10},{14,12},{3,1},{5,3},{7,5},{... | collective-permute-start | bytes 49160 | tf_op jit(solution)/shard_map/ppermute | solution.py:16
  68.3 9.8 %collective-permute-start.10 = (f32[2,16,1,128]{3,1,2,0:T(8,128)S(1)}, f32[2,16,1,128]{3,1,2,0:T(8,128)S(1)}, u32[]{:S(2)}, u32[]{:S(2)}) collective-permute-start(f32[2,16,1,128]{3,1,2,0:T(8,128)S(1)} %bitcast.594), channel_id=1, source_target_pairs={{0,1},{2,3},{4,5},{6,7},{8,9},{10,11},{12,13},{14,15},{16,17},{18,... | collective-permute-start | bytes 49160 | tf_op jit(solution)/shard_map/ppermute | solution.py:16
  86.1 6.4 %collective-permute-start.12 = (f32[2,16,1,128]{3,1,2,0:T(8,128)}, f32[2,16,1,128]{3,1,2,0:T(8,128)}, u32[]{:S(2)}, u32[]{:S(2)}) collective-permute-start(f32[2,16,1,128]{3,1,2,0:T(8,128)} %bitcast.197), channel_id=1, source_target_pairs={{1,0},{3,2},{5,4},{7,6},{9,8},{11,10},{13,12},{15,14},{17,16},{19,... | collective-permute-start | bytes 49160 | tf_op jit(solution)/shard_map/ppermute | solution.py:16
  87.5 5.7 %collective-permute-start.13 = (f32[2,1,16,128]{3,2,1,0:T(8,128)S(1)}, f32[2,1,16,128]{3,2,1,0:T(8,128)}, u32[]{:S(2)}, u32[]{:S(2)}) collective-permute-start(f32[2,1,16,128]{3,2,1,0:T(8,128)S(1)} %copy-done.73), channel_id=1, source_target_pairs={{2,0},{4,2},{6,4},{8,6},{10,8},{12,10},{14,12},{3,1},{5,3},{7,5},{... | collective-permute-start | bytes 49160 | tf_op jit(solution)/shard_map/ppermute | solution.py:16
  97.4 9.6 %collective-permute-start.14 = (f32[2,16,1,128]{3,1,2,0:T(8,128)S(1)}, f32[2,16,1,128]{3,1,2,0:T(8,128)S(1)}, u32[]{:S(2)}, u32[]{:S(2)}) collective-permute-start(f32[2,16,1,128]{3,1,2,0:T(8,128)S(1)} %bitcast.595), channel_id=1, source_target_pairs={{0,1},{2,3},{4,5},{6,7},{8,9},{10,11},{12,13},{14,15},{16,17},{18,... | collective-permute-start | bytes 49160 | tf_op jit(solution)/shard_map/ppermute | solution.py:16
  118.0 6.0 %collective-permute-start.16 = (f32[2,16,1,128]{3,1,2,0:T(8,128)S(1)}, f32[2,16,1,128]{3,1,2,0:T(8,128)S(1)}, u32[]{:S(2)}, u32[]{:S(2)}) collective-permute-start(f32[2,16,1,128]{3,1,2,0:T(8,128)S(1)} %bitcast.589), channel_id=1, source_target_pairs={{1,0},{3,2},{5,4},{7,6},{9,8},{11,10},{13,12},{15,14},{17,16},{19,... | collective-permute-start | bytes 49160 | tf_op jit(solution)/shard_map/ppermute | solution.py:16
  119.4 5.5 %collective-permute-start.17 = (f32[2,1,16,128]{3,2,1,0:T(8,128)S(1)}, f32[2,1,16,128]{3,2,1,0:T(8,128)S(1)}, u32[]{:S(2)}, u32[]{:S(2)}) collective-permute-start(f32[2,1,16,128]{3,2,1,0:T(8,128)S(1)} %slice.1440), channel_id=1, source_target_pairs={{2,0},{4,2},{6,4},{8,6},{10,8},{12,10},{14,12},{3,1},{5,3},{7,5},{... | collective-permute-start | bytes 49160 | tf_op jit(solution)/shard_map/ppermute | solution.py:16
  126.3 9.8 %collective-permute-start.18 = (f32[2,16,1,128]{3,1,2,0:T(8,128)S(1)}, f32[2,16,1,128]{3,1,2,0:T(8,128)S(1)}, u32[]{:S(2)}, u32[]{:S(2)}) collective-permute-start(f32[2,16,1,128]{3,1,2,0:T(8,128)S(1)} %bitcast.596), channel_id=1, source_target_pairs={{0,1},{2,3},{4,5},{6,7},{8,9},{10,11},{12,13},{14,15},{16,17},{18,... | collective-permute-start | bytes 49160 | tf_op jit(solution)/shard_map/ppermute | solution.py:16
  143.9 6.0 %collective-permute-start.20 = (f32[2,16,1,128]{3,1,2,0:T(8,128)S(1)}, f32[2,16,1,128]{3,1,2,0:T(8,128)S(1)}, u32[]{:S(2)}, u32[]{:S(2)}) collective-permute-start(f32[2,16,1,128]{3,1,2,0:T(8,128)S(1)} %bitcast.590), channel_id=1, source_target_pairs={{1,0},{3,2},{5,4},{7,6},{9,8},{11,10},{13,12},{15,14},{17,16},{19,... | collective-permute-start | bytes 49160 | tf_op jit(solution)/shard_map/ppermute | solution.py:16
  151.7 9.8 %collective-permute-start.22 = (f32[2,16,1,128]{3,1,2,0:T(8,128)S(1)}, f32[2,16,1,128]{3,1,2,0:T(8,128)S(1)}, u32[]{:S(2)}, u32[]{:S(2)}) collective-permute-start(f32[2,16,1,128]{3,1,2,0:T(8,128)S(1)} %bitcast.597), channel_id=1, source_target_pairs={{0,1},{2,3},{4,5},{6,7},{8,9},{10,11},{12,13},{14,15},{16,17},{18,... | collective-permute-start | bytes 49160 | tf_op jit(solution)/shard_map/ppermute | solution.py:16
  169.3 6.0 %collective-permute-start.24 = (f32[2,16,1,128]{3,1,2,0:T(8,128)S(1)}, f32[2,16,1,128]{3,1,2,0:T(8,128)S(1)}, u32[]{:S(2)}, u32[]{:S(2)}) collective-permute-start(f32[2,16,1,128]{3,1,2,0:T(8,128)S(1)} %bitcast.591), channel_id=1, source_target_pairs={{1,0},{3,2},{5,4},{7,6},{9,8},{11,10},{13,12},{15,14},{17,16},{19,... | collective-permute-start | bytes 49160 | tf_op jit(solution)/shard_map/ppermute | solution.py:16
  170.7 5.0 %collective-permute-start.25 = (f32[2,1,16,128]{3,2,1,0:T(8,128)S(1)}, f32[2,1,16,128]{3,2,1,0:T(8,128)S(1)}, u32[]{:S(2)}, u32[]{:S(2)}) collective-permute-start(f32[2,1,16,128]{3,2,1,0:T(8,128)S(1)} %slice.1504), channel_id=1, source_target_pairs={{2,0},{4,2},{6,4},{8,6},{10,8},{12,10},{14,12},{3,1},{5,3},{7,5},{... | collective-permute-start | bytes 49160 | tf_op jit(solution)/shard_map/ppermute | solution.py:16
  177.5 9.8 %collective-permute-start.26 = (f32[2,16,1,128]{3,1,2,0:T(8,128)S(1)}, f32[2,16,1,128]{3,1,2,0:T(8,128)S(1)}, u32[]{:S(2)}, u32[]{:S(2)}) collective-permute-start(f32[2,16,1,128]{3,1,2,0:T(8,128)S(1)} %bitcast.598), channel_id=1, source_target_pairs={{0,1},{2,3},{4,5},{6,7},{8,9},{10,11},{12,13},{14,15},{16,17},{18,... | collective-permute-start | bytes 49160 | tf_op jit(solution)/shard_map/ppermute | solution.py:16
  195.3 6.0 %collective-permute-start.28 = (f32[2,16,1,128]{3,2,1,0:T(1,128)S(1)}, f32[2,16,1,128]{3,2,1,0:T(1,128)S(1)}, u32[]{:S(2)}, u32[]{:S(2)}) collective-permute-start(f32[2,16,1,128]{3,2,1,0:T(1,128)S(1)} %slice.1285), channel_id=1, source_target_pairs={{1,0},{3,2},{5,4},{7,6},{9,8},{11,10},{13,12},{15,14},{17,16},{19,... | collective-permute-start | bytes 49160 | tf_op jit(solution)/shard_map/ppermute | solution.py:16
  203.1 9.8 %collective-permute-start.30 = (f32[2,16,1,128]{3,1,2,0:T(8,128)S(1)}, f32[2,16,1,128]{3,1,2,0:T(8,128)S(1)}, u32[]{:S(2)}, u32[]{:S(2)}) collective-permute-start(f32[2,16,1,128]{3,1,2,0:T(8,128)S(1)} %bitcast.599), channel_id=1, source_target_pairs={{0,1},{2,3},{4,5},{6,7},{8,9},{10,11},{12,13},{14,15},{16,17},{18,... | collective-permute-start | bytes 49160 | tf_op jit(solution)/shard_map/ppermute | solution.py:16
  (91 other events, 157.7 us)
Sparse Core Ops, SparseCore 0:
  217.1 75.4 reduce-scatter.1
where the time goes:
time: 329 us; the launch traced here: 327 us
  blocking collectives  100 us (30%)
  starting transfers between devices  99.3 us (30%)
  local copies, waits for them, and re-layouts  54.1 us (16%)
  waiting for transfers between devices  27.5 us (8%)
  between operations  19.4 us (6%)
  other arithmetic  18.6 us (6%)
  matrix products  7.47 us (2%)
    psum x1, blocking collectives, on_device(): misfit = lax.psum(local_misfit, ('tx', 'gx', 'gy'))  100 us
    ppermute x32, starting transfers between devices, shifted(): return lax.ppermute(x, axis, pairs)  99.2 us
    ppermute x32, waiting for transfers between devices, shifted(): return lax.ppermute(x, axis, pairs)  27.5 us
    unnamed x167, local copies, waits for them, and re-layouts  21.2 us
    scatter-add x4, local copies, waits for them, and re-layouts, on_device(): adj_e.at[0:2, :, :, ZREC]  14.4 us
    another operation x6, other arithmetic  10.1 us
  transfers between devices with their start and end apart: 33, of which 20 were waited for; matrix products, arithmetic and copies ran while one was open for 4% of the time, Pallas kernels for 0%

commit v1 on v0

v1 whole, which is shorter than its diff:
```python
import jax
import jax.numpy as jnp
from jax import lax
from jax.experimental import pallas as pl
from jax.experimental.pallas import tpu as pltpu
from jax.sharding import PartitionSpec as P

STEPS = 4
ZREC = 32
STEP_DT = 0.5
HALO = 4
CX = 16
CY = 16
NZ = 128
EX = CX + 2 * HALO
EY = CY + 2 * HALO
F32 = jnp.float32
HIGHEST = lax.Precision.HIGHEST

LOW = [(c, x) for c in range(6) for x in range(CX - HALO + (c == 3), CX)]
HIGH = [(c, x) for c in range(6) for x in range(HALO - (c in (0, 3, 4, 5)))]
LOW_COND = [(c, x) for c in (6, 7) for x in range(CX - HALO + 1, CX)]
HIGH_COND = [(c, x) for c in (6, 7) for x in range(HALO - 1)]
VMEM = pl.BlockSpec(memory_space=pltpu.VMEM)
SMEM = pl.BlockSpec(memory_space=pltpu.SMEM)


def shape(*dims):
    return jax.ShapeDtypeStruct(dims, F32)


def params():
    return pltpu.CompilerParams(vmem_limit_bytes=16 * 1024 * 1024)


def plane_of(refs, comp, x):
    return refs[0][0, comp, x] if comp < 6 else refs[comp - 5][x]


def pack_kernel(low, high, n_in, *refs):
    ins, (to_next, to_prev, to_side, side_next, side_prev) = refs[:n_in], refs[n_in:]
    second = lax.axis_index("gy") == 1
    comps = 6 + n_in - 1

    def edge(plane):
        return jnp.where(second, plane[0:HALO], plane[CY - HALO : CY])

    for k, (c, x) in enumerate(low):
        plane = plane_of(ins, c, x)
        to_next[k] = plane
        side_next[k] = edge(plane)
    for k, (c, x) in enumerate(high):
        plane = plane_of(ins, c, x)
        to_prev[k] = plane
        side_prev[k] = edge(plane)
    for c in range(comps):
        for x in range(CX):
            to_side[c, x] = edge(plane_of(ins, c, x))


def pack(low, high, *arrays):
    comps = 6 + len(arrays) - 1
    return pl.pallas_call(
        lambda *refs: pack_kernel(low, high, len(arrays), *refs),
        out_shape=[
            shape(len(low), CY, NZ),
            shape(len(high), CY, NZ),
            shape(comps, CX, HALO, NZ),
            shape(len(low), HALO, NZ),
            shape(len(high), HALO, NZ),
        ],
        in_specs=[VMEM] * len(arrays),
        out_specs=[VMEM] * 5,
        compiler_params=params(),
        name="pack",
    )(*arrays)


def exchange(to_next, to_prev, to_side, side_next, side_prev):
    size_x = lax.axis_size("gx")
    size_y = lax.axis_size("gy")

    def pairs(dx, swap):
        return [
            (x * size_y + y, (x + dx) * size_y + (1 - y if swap else y))
            for x in range(size_x)
            for y in range(size_y)
            if 0 <= x + dx < size_x
        ]

    both = ("gx", "gy")
    return (
        lax.ppermute(to_next, both, pairs(1, False)),
        lax.ppermute(to_prev, both, pairs(-1, False)),
        lax.ppermute(to_side, both, pairs(0, True)),
        lax.ppermute(side_next, both, pairs(1, True)),
        lax.ppermute(side_prev, both, pairs(-1, True)),
    )


def assemble(low, high, ins, halos, dest, first):
    from_prev, from_next, from_side, side_prev, side_next = halos
    zero_rows = jnp.zeros((HALO, NZ), F32)
    zero_plane = jnp.zeros((EY, NZ), F32)

    def put_side(ref, index, i, rows):
        ref[index, i, CY : CY + HALO] = jnp.where(first, rows, zero_rows)
        ref[index, i, CY + HALO : EY] = jnp.where(first, zero_rows, rows)

    comps = 6 + len(ins) - 1
    for c in range(comps):
        ref, index = dest(c)
        filled = set()
        for x in range(CX):
            ref[index, HALO + x, 0:CY] = plane_of(ins, c, x)
            put_side(ref, index, HALO + x, from_side[c, x])
            filled.add(HALO + x)
        for k, (comp, x) in enumerate(low):
            if comp == c:
                i = x - (CX - HALO)
                ref[index, i, 0:CY] = from_prev[k]
                put_side(ref, index, i, side_prev[k])
                filled.add(i)
        for k, (comp, x) in enumerate(high):
            if comp == c:
                i = x + HALO + CX
                ref[index, i, 0:CY] = from_next[k]
                put_side(ref, index, i, side_next[k])
                filled.add(i)
        for i in range(EX):
            if i not in filled:
                ref[index, i] = zero_plane


def helpers(gy):
    lane = lax.broadcasted_iota(jnp.int32, (EY, NZ), 1)
    row = lax.broadcasted_iota(jnp.int32, (EY, NZ), 0)
    y = jnp.where(row < CY + HALO, row, row - EY) + gy * CY
    inside = (y >= 0) & (y < 2 * CY)
    last, start = lane == NZ - 1, lane == 0

    def z_up(f):
        return jnp.where(last, 0.0, pltpu.roll(f, NZ - 1, 1))

    def z_down(f):
        return jnp.where(start, 0.0, pltpu.roll(f, 1, 1))

    def y_up(f):
        return pltpu.roll(f, EY - 1, 0)

    def y_down(f):
        return pltpu.roll(f, 1, 0)

    return lane, inside, z_up, z_down, y_up, y_down


def in_grid(gx, i):
    x = gx * CX + i - HALO
    return (x >= 0) & (x < 8 * CX)


def sweep(step, gx, elec, mag, coef, tools, load):
    _, inside, z_up, z_down, y_up, y_down = tools
    half = jnp.where(inside, STEP_DT, 0.0)
    zero = jnp.zeros((EY, NZ), F32)

    def body(i, carry):
        ex, ey, ez, hy_before, hz_before = carry
        ex_next, ey_next, ez_next = load(i + 1)
        rate = jnp.where(in_grid(gx, i), half, zero)
        hx = mag[0, i] - rate * ((y_up(ez) - ez) - (z_up(ey) - ey))
        hy = mag[1, i] - rate * ((z_up(ex) - ex) - (ez_next - ez))
        hz = mag[2, i] - rate * ((ey_next - ey) - (y_up(ex) - ex))
        mag[0, i] = hx
        mag[1, i] = hy
        mag[2, i] = hz
        decay_h, drive_h, decay_v, drive_v = (coef[k, i] for k in range(4))
        elec[0, i] = decay_h * ex + drive_h * ((hz - y_down(hz)) - (hy - z_down(hy)))
        elec[1, i] = decay_h * ey + drive_h * ((hx - z_down(hx)) - (hz - hz_before))
        elec[2, i] = decay_v * ez + drive_v * ((hy - hy_before) - (hx - y_down(hx)))
        return (ex_next, ey_next, ez_next, hy, hz)

    lax.fori_loop(step, EX - 1 - step, body, (*load(step), zero, zero))


def forward_kernel(fwd, cond_h, cond_v, *refs):
    halos, refs = refs[:5], refs[5:]
    observed, rec_vec, rec, coef, stored, spread, block, elec, mag, rows = refs
    gx, gy = lax.axis_index("gx"), lax.axis_index("gy")
    tools = helpers(gy)
    lane, inside = tools[0], tools[1]

    def dest(c):
        return ((elec, c) if c < 3 else (mag, c - 3)) if c < 6 else (coef, 2 * (c - 6))

    assemble(LOW + LOW_COND, HIGH + HIGH_COND, (fwd, cond_h, cond_v), halos, dest, gy == 0)

    def coefficients(i, carry):
        keep = inside & in_grid(gx, i)
        for k in (0, 2):
            half_rate = 0.25 * coef[k, i]
            coef[k, i] = jnp.where(keep, (1.0 - half_rate) / (1.0 + half_rate), 0.0)
            coef[k + 1, i] = jnp.where(keep, STEP_DT / (1.0 + half_rate), 0.0)
        return carry

    lax.fori_loop(0, EX, coefficients, 0)

    def load(i):
        return elec[0, i], elec[1, i], elec[2, i]

    for step in range(STEPS):
        sweep(step, gx, elec, mag, coef, tools, load)
        stored[step] = elec[:, HALO : HALO + CX, 0:CY]

    for r in range(rec.shape[0]):
        x, y = rec[r] // CY, rec[r] % CY
        for step in range(STEPS):
            for c in range(2):
                rows[pl.ds((2 * step + c) * 32 + r, 1), :] = stored[step, c, x, pl.ds(y, 1), :]
    pick = (lax.broadcasted_iota(jnp.int32, (8, NZ), 1) == ZREC).astype(F32)
    picked = lax.dot_general(
        pick, rows[...], (((1,), (1,)), ((), ())), precision=HIGHEST, preferred_element_type=F32
    )
    lane8 = lax.broadcasted_iota(jnp.int32, (8, NZ), 1)
    row8 = lax.broadcasted_iota(jnp.int32, (8, NZ), 0)
    own = jnp.where(lane8 // 32 == row8, picked[:, 0:NZ], 0.0)
    own = own + jnp.where(lane8 // 32 + 4 == row8, picked[:, NZ : 2 * NZ], 0.0)
    own = own + pltpu.roll(own, 64, 1)
    own = own + pltpu.roll(own, 32, 1)
    residual = own[:, 0:32] - observed[...]
    misfit = 0.5 * jnp.sum(residual * residual)
    cells = rec_vec[...]
    at_y = (cells % CY == lax.broadcasted_iota(jnp.int32, (CY, 32), 0)).astype(F32)
    at_x = cells // CY == lax.broadcasted_iota(jnp.int32, (NZ, 32), 0) // 8
    weighted = jnp.where(at_x, jnp.tile(residual, (16, 1)), 0.0)
    spread_now = lax.dot_general(
        at_y, weighted, (((1,), (1,)), ((), ())), precision=HIGHEST, preferred_element_type=F32
    )
    spread[...] = spread_now
    low_rows, high_rows = spread_now[0:8], spread_now[8:16]
    edges = jnp.where((lane8 < 32) | (lane8 >= 96), low_rows, pltpu.roll(high_rows, 64, 1))
    is_first = gy == 0
    side = jnp.where(is_first, high_rows, low_rows)
    used = row8 // HALO == 1 - gy
    side = jnp.where(used, side, misfit)
    for t in range(16):
        block[t, 0:8] = edges
        block[t, 8:16] = side


def adjoint_kernel(adj, *refs):
    halos, refs = refs[:5], refs[5:]
    coef, stored, spread, blocks, foot, owner, out, elec, mag, inject, grad = refs
    gx, gy = lax.axis_index("gx"), lax.axis_index("gy")
    tools = helpers(gy)
    lane, inside = tools[0], tools[1]

    def dest(c):
        return (elec, c) if c < 3 else (mag, c - 3)

    assemble(LOW, HIGH, (adj,), halos, dest, gy == 0)

    row8 = lax.broadcasted_iota(jnp.int32, (8, NZ), 0)
    used = row8 // HALO == gy
    for k, dx in enumerate((-1, 0, 1)):
        there = (gx + dx >= 0) & (gx + dx < 8)
        near = jnp.clip(gx + dx, 0, 7)
        if dx == 0:
            inject[k, 0:16] = spread[...]
        else:
            edges = jnp.where(there, blocks[2 * near + gy, 0:8], 0.0)
            inject[k, 0:8] = edges
            inject[k, 8:16] = pltpu.roll(edges, 64, 1)
        side = blocks[2 * near + 1 - gy, 8:16]
        inject[k, 16:24] = jnp.where(used & there, side, 0.0)

    at_depth = lane == ZREC

    for step in range(STEPS):
        when = STEPS - 1 - step

        def load(i, when=when):
            tile = jnp.where(i < HALO, 0, jnp.where(i < HALO + CX, 1, 2))
            x = (i + CX - HALO) % CX
            source = inject[tile]
            shift = (ZREC + NZ - (x * 8 + 2 * when)) % NZ
            add_x = jnp.where(at_depth, pltpu.roll(source, shift, 1), 0.0)
            add_y = jnp.where(at_depth, pltpu.roll(source, (shift + NZ - 1) % NZ, 1), 0.0)
            return elec[0, i] + add_x, elec[1, i] + add_y, elec[2, i]

        sweep(step, gx, elec, mag, coef, tools, load)

        def accumulate(x, carry, when=when, step=step):
            ax, ay, az = (elec[c, HALO + x, 0:CY] for c in range(3))
            horizontal = ax * stored[when, 0, x] + ay * stored[when, 1, x]
            vertical = az * stored[when, 2, x]
            if step:
                horizontal = grad[0, x] + horizontal
                vertical = grad[1, x] + vertical
            grad[0, x] = horizontal
            grad[1, x] = vertical
            return carry

        lax.fori_loop(0, CX, accumulate, 0)

    flag = foot[0].astype(F32)
    misfit = blocks[0, 8:16][0:1]
    for t in range(1, 16):
        top = 0 if t % 2 == 0 else HALO
        misfit = misfit + blocks[t, 8:16][top : top + 1]
    misfit = jnp.broadcast_to(misfit, (8, NZ))
    for t in range(16):
        out[t, 0:16] = grad[0, owner[t]] * flag
        out[t, 16:32] = grad[1, owner[t]] * flag
        out[t, 32:40] = misfit


def sum_kernel(blocks, part, misfit):
    total = blocks[0]
    for t in range(1, 16):
        total = total + blocks[t]
    part[0, 0, 0, 0] = total[0:16]
    part[0, 0, 1, 0] = total[16:32]
    misfit[...] = total[32:33, 0:1]


def on_device(cond_h, cond_v, fwd_init, adj_init, observed, footprint, owner, rec_cells):
    sent = pack(LOW + LOW_COND, HIGH + HIGH_COND, fwd_init, cond_h, cond_v)
    adj_sent = pack(LOW, HIGH, adj_init)
    halos = exchange(*sent)
    adj_halos = exchange(*adj_sent)
    rec = rec_cells.reshape(32)
    coef, stored, spread, block = pl.pallas_call(
        forward_kernel,
        out_shape=[
            shape(4, EX, EY, NZ),
            shape(STEPS, 3, CX, CY, NZ),
            shape(CY, NZ),
            shape(16, 16, NZ),
        ],
        in_specs=[VMEM] * 10 + [SMEM],
        out_specs=[VMEM] * 4,
        scratch_shapes=[
            pltpu.VMEM((3, EX, EY, NZ), F32),
            pltpu.VMEM((3, EX, EY, NZ), F32),
            pltpu.VMEM((256, NZ), F32),
        ],
        compiler_params=params(),
        name="forward",
    )(fwd_init, cond_h, cond_v, *halos, observed.reshape(8, 32), rec.reshape(1, 32), rec)
    blocks = lax.all_to_all(block, ("gx", "gy"), 0, 0, tiled=True)
    ordered = pl.pallas_call(
        adjoint_kernel,
        out_shape=shape(16, 40, NZ),
        in_specs=[VMEM] * 10 + [SMEM, SMEM],
        out_specs=VMEM,
        scratch_shapes=[
            pltpu.VMEM((3, EX, EY, NZ), F32),
            pltpu.VMEM((3, EX, EY, NZ), F32),
            pltpu.VMEM((3, EY, NZ), F32),
            pltpu.VMEM((2, CX, CY, NZ), F32),
        ],
        compiler_params=params(),
        name="adjoint",
    )(
        adj_init,
        *adj_halos,
        coef,
        stored,
        spread,
        blocks,
        footprint.reshape(1),
        owner.reshape(16),
    )
    summed = lax.all_to_all(ordered, "tx", 0, 0, tiled=True)
    part, misfit = pl.pallas_call(
        sum_kernel,
        out_shape=[shape(1, 1, 2, 1, CY, NZ), shape(1, 1)],
        in_specs=[VMEM],
        out_specs=[VMEM, VMEM],
        compiler_params=params(),
        name="total",
    )(summed)
    return part, misfit.reshape(())


def solution(mesh):
    placed = (
        P("gx", "gy", None),
        P("gx", "gy", None),
        P("tx", None, "gx", "gy", None),
        P("tx", None, "gx", "gy", None),
        P("tx", None, "gx", "gy", None, None),
        P("tx", "gx", "gy"),
        P("gx", "gy", None),
        P("gx", "gy", None),
    )
    return jax.shard_map(
        on_device,
        mesh=mesh,
        in_specs=placed,
        out_specs=(P("gx", "tx", None, None, "gy", None), P()),
        check_vma=False,
    )
```

time: 329 us -> 106 us (0.32)
  blocking collectives: 100 us -> 26 us
  starting transfers between devices: 99.3 us -> 34.4 us
  local copies, waits for them, and re-layouts: 54.1 us -> 7.55 us
  Pallas kernels: 0 us -> 30.5 us
  waiting for transfers between devices: 27.5 us -> 4.82 us
  other arithmetic: 18.6 us -> 0 us
  between operations: 19.4 us -> 1.51 us
  matrix products: 7.47 us -> 0 us
    psum x1 -> x0, blocking collectives: 100 us -> none  [on_device(): misfit = lax.psum(local_misfit, ('tx', 'gx', 'gy'))]
    ppermute x32 -> x10, starting transfers between devices: 99.2 us -> 28.4 us  [the longest x2 9.62 us: exchange(): lax.ppermute(side_next, both, pairs(1, True))]
    pallas_call x0 -> x5, Pallas kernels: none -> 30.5 us  [the longest x1 14.5 us: on_device(): pl.pallas_call(forward_kernel, out_shape=[shape(4, EX, EY, NZ), shape(STE...]
    all_to_all x0 -> x1, blocking collectives: none -> 26 us  [on_device(): summed = lax.all_to_all(ordered, 'tx', 0, 0, tiled=True)]
    ppermute x32 -> x10, waiting for transfers between devices: 27.5 us -> 4.82 us  [the longest x2 4.8 us: exchange(): lax.ppermute(side_prev, both, pairs(-1, True))]
    scatter-add x4 -> x0, local copies, waits for them, and re-layouts: 14.4 us -> none  [on_device(): adj_e.at[0:2, :, :, ZREC]]
    unnamed x167 -> x36, local copies, waits for them, and re-layouts: 21.2 us -> 7.55 us
    another operation x25 -> x0, other arithmetic: 12.3 us -> none
  transfers between devices with their start and end apart: 33 -> 11, of which waited for: 20 -> 1; matrix products, arithmetic and copies ran while one was open for 4% -> 0% of each run, Pallas kernels for 0% -> 15%
where the time goes in v1:
time: 106 us; the launch traced here: 105 us
  starting transfers between devices  34.4 us (32%)
  Pallas kernels  30.5 us (29%)
  blocking collectives  26 us (25%)
  local copies, waits for them, and re-layouts  7.55 us (7%)
  waiting for transfers between devices  4.82 us (5%)
  between operations  1.51 us (1%)
    all_to_all x1, blocking collectives, on_device(): summed = lax.all_to_all(ordered, 'tx', 0, 0, tiled=True)  26 us
    pallas_call x1, Pallas kernels, on_device(): pl.pallas_call(forward_kernel, out_shape=[shape(4, EX, EY, NZ), shape(STE...  14.5 us
    pallas_call x1, Pallas kernels, on_device(): pl.pallas_call(adjoint_kernel, out_shape=shape(16, 40, NZ), in_specs=[VME...  14.4 us
    ppermute x2, starting transfers between devices, exchange(): lax.ppermute(side_next, both, pairs(1, True))  9.62 us
    ppermute x2, starting transfers between devices, exchange(): lax.ppermute(to_next, both, pairs(1, False))  9.32 us
    unnamed x36, local copies, waits for them, and re-layouts  7.55 us
    all_to_all x1, starting transfers between devices, on_device(): blocks = lax.all_to_all(block, ('gx', 'gy'), 0, 0, tiled=True)  6.03 us
    ppermute x2, waiting for transfers between devices, exchange(): lax.ppermute(side_prev, both, pairs(-1, True))  4.8 us
  transfers between devices with their start and end apart: 11, of which 1 were waited for; matrix products, arithmetic and copies ran while one was open for 0% of the time, Pallas kernels for 15%

profile of v1, /device:TPU:1, one launch (start us, length us, event | category | flops | bytes accessed | tf_op | source)
XLA Modules:
  0.0 104.9 jit_solution(17715565791207941153)
XLA Ops:
  0.6 1.1 %copy-done = f32[1,6,16,16,128]{4,3,2,1,0:T(8,128)S(1)} copy-done((f32[1,6,16,16,128]{4,3,2,1,0:T(8,128)S(1)}, f32[1,6,16,16,128]{4,3,2,1,0:T(8,128)}, u32[]{:S(2)}) %copy-start) | copy-done | bytes 786456
  1.8 0.9 copy-done.4
  2.7 0.9 copy-done.6
  3.7 3.8 %collective-permute-start.7 = (f32[8,16,4,128]{3,2,1,0:T(4,128)S(1)}, f32[8,16,4,128]{3,2,1,0:T(4,128)S(1)}, u32[]{:S(2)}, u32[]{:S(2)}) collective-permute-start(f32[8,16,4,128]{3,2,1,0:T(4,128)S(1)} %get-tuple-element.25), channel_id=1, source_target_pairs={{0,1},{1,0},{2,3},{3,2},{4,5},{5,4},{6,7},{7,6},{8,9},{9,8},{10,11... | collective-permute-start | bytes 786440 | tf_op jit(solution)/shard_map/ppermute | solution.py:95
  7.5 1.3 %collective-permute-start.6 = (f32[26,16,128]{2,1,0:T(8,128)S(1)}, f32[26,16,128]{2,1,0:T(8,128)S(1)}, u32[]{:S(2)}, u32[]{:S(2)}) collective-permute-start(f32[26,16,128]{2,1,0:T(8,128)S(1)} %get-tuple-element.24), channel_id=1, source_target_pairs={{2,0},{3,1},{4,2},{5,3},{6,4},{7,5},{8,6},{9,7},{10,8},{11,9},{12,... | collective-permute-start | bytes 638984 | tf_op jit(solution)/shard_map/ppermute | solution.py:94
  8.8 4.0 %collective-permute-start.5 = (f32[29,16,128]{2,1,0:T(8,128)S(1)}, f32[29,16,128]{2,1,0:T(8,128)S(1)}, u32[]{:S(2)}, u32[]{:S(2)}) collective-permute-start(f32[29,16,128]{2,1,0:T(8,128)S(1)} %get-tuple-element.23), channel_id=1, source_target_pairs={{0,2},{1,3},{2,4},{3,5},{4,6},{5,7},{6,8},{7,9},{8,10},{9,11},{10,... | collective-permute-start | bytes 712712 | tf_op jit(solution)/shard_map/ppermute | solution.py:93
  12.8 1.3 %collective-permute-start.9 = (f32[26,4,128]{2,1,0:T(4,128)S(1)}, f32[26,4,128]{2,1,0:T(4,128)S(1)}, u32[]{:S(2)}, u32[]{:S(2)}) collective-permute-start(f32[26,4,128]{2,1,0:T(4,128)S(1)} %get-tuple-element.27), channel_id=1, source_target_pairs={{2,1},{3,0},{4,3},{5,2},{6,5},{7,4},{8,7},{9,6},{10,9},{11,8},{12,... | collective-permute-start | bytes 159752 | tf_op jit(solution)/shard_map/ppermute | solution.py:97
  14.1 5.2 %collective-permute-start.8 = (f32[29,4,128]{2,1,0:T(4,128)S(1)}, f32[29,4,128]{2,1,0:T(4,128)S(1)}, u32[]{:S(2)}, u32[]{:S(2)}) collective-permute-start(f32[29,4,128]{2,1,0:T(4,128)S(1)} %get-tuple-element.26), channel_id=1, source_target_pairs={{0,3},{1,2},{2,5},{3,4},{4,7},{5,6},{6,9},{7,8},{8,11},{9,10},{10,... | collective-permute-start | bytes 178184 | tf_op jit(solution)/shard_map/ppermute | solution.py:96
  19.4 1.1 %copy-done.2 = f32[1,6,16,16,128]{4,3,2,1,0:T(8,128)S(1)} copy-done((f32[1,6,16,16,128]{4,3,2,1,0:T(8,128)S(1)}, f32[1,6,16,16,128]{4,3,2,1,0:T(8,128)}, u32[]{:S(2)}) %copy-start.2) | copy-done | bytes 786456
  20.5 0.9 pack.2
  21.9 5.3 %collective-permute-start = (f32[23,16,128]{2,1,0:T(8,128)}, f32[23,16,128]{2,1,0:T(8,128)}, u32[]{:S(2)}, u32[]{:S(2)}) collective-permute-start(f32[23,16,128]{2,1,0:T(8,128)} %get-tuple-element.18), channel_id=1, source_target_pairs={{0,2},{1,3},{2,4},{3,5},{4,6},{5,7},{6,8},{7,9},{8,10},{9,11},{10,... | collective-permute-start | bytes 565256 | tf_op jit(solution)/shard_map/ppermute | solution.py:93
  27.2 1.3 %collective-permute-start.1 = (f32[20,16,128]{2,1,0:T(8,128)}, f32[20,16,128]{2,1,0:T(8,128)}, u32[]{:S(2)}, u32[]{:S(2)}) collective-permute-start(f32[20,16,128]{2,1,0:T(8,128)} %get-tuple-element.19), channel_id=1, source_target_pairs={{2,0},{3,1},{4,2},{5,3},{6,4},{7,5},{8,6},{9,7},{10,8},{11,9},{12,... | collective-permute-start | bytes 491528 | tf_op jit(solution)/shard_map/ppermute | solution.py:94
  28.5 14.5 %forward.1 = (f32[4,24,24,128]{3,2,1,0:T(8,128)S(1)}, f32[4,3,16,16,128]{4,3,2,1,0:T(8,128)S(1)}, f32[16,128]{1,0:T(8,128)S(1)}, f32[16,16,128]{2,1,0:T(8,128)S(1)}) custom-call(f32[1,6,16,16,128]{4,3,2,1,0:T(8,128)S(1)} %copy-done.1, f32[16,16,128]{2,1,0:T(8,128)S(1)} %copy-done.5, f32[16,16,128]{2,1,0:T(8,128)S(1)} %copy-done.7, ...), custom_call_target="tpu_custom_call" | custom-call | tf_op jit(solution)/shard_map/forward/pallas_call | solution.py:333
  43.1 0.6 copy-done.8
  43.8 6.0 %all-to-all-start = ((f32[16,16,128]{2,1,0:T(8,128)}), f32[16,16,128]{2,1,0:T(8,128)}, u32[]{:S(2)}, u32[]{:S(2)}) async-start(f32[16,16,128]{2,1,0:T(8,128)} %copy-done.8), calls=%async_computation | async-start | bytes 262144 | tf_op jit(solution)/shard_map/all_to_all | solution.py:351
  49.8 4.4 %collective-permute-start.3 = (f32[23,4,128]{2,1,0:T(4,128)}, f32[23,4,128]{2,1,0:T(4,128)S(1)}, u32[]{:S(2)}, u32[]{:S(2)}) collective-permute-start(f32[23,4,128]{2,1,0:T(4,128)} %copy-done.16), channel_id=1, source_target_pairs={{0,3},{1,2},{2,5},{3,4},{4,7},{5,6},{6,9},{7,8},{8,11},{9,10},{10,... | collective-permute-start | bytes 141320 | tf_op jit(solution)/shard_map/ppermute | solution.py:96
  54.2 1.3 %collective-permute-start.4 = (f32[20,4,128]{2,1,0:T(4,128)}, f32[20,4,128]{2,1,0:T(4,128)S(1)}, u32[]{:S(2)}, u32[]{:S(2)}) collective-permute-start(f32[20,4,128]{2,1,0:T(4,128)} %copy-done.17), channel_id=1, source_target_pairs={{2,1},{3,0},{4,3},{5,2},{6,5},{7,4},{8,7},{9,6},{10,9},{11,8},{12,... | collective-permute-start | bytes 122888 | tf_op jit(solution)/shard_map/ppermute | solution.py:97
  56.2 4.8 %collective-permute-done.4.refs_4_ = f32[20,4,128]{2,1,0:T(4,128)S(1)} collective-permute-done((f32[20,4,128]{2,1,0:T(4,128)}, f32[20,4,128]{2,1,0:T(4,128)S(1)}, u32[]{:S(2)}, u32[]{:S(2)}) %collective-permute-start.4) | collective-permute-done | bytes 40992 | tf_op jit(solution)/shard_map/ppermute | solution.py:97
  61.0 0.6 copy-done.11
  62.3 0.8 copy-done.10
  63.1 0.8 copy-done.12
  63.8 14.4 %adjoint.1 = f32[16,40,128]{2,1,0:T(8,128)S(1)} custom-call(f32[1,6,16,16,128]{4,3,2,1,0:T(8,128)S(1)} %copy-done.3, f32[23,16,128]{2,1,0:T(8,128)} %collective-permute-done.refs_0_, f32[20,16,128]{2,1,0:T(8,128)} %collective-permute-done.1.refs_1_, f32[6,16,4,128]{3,2,1,0:T(4,128)} %collective-permute-done.2.refs_2_, f32[23,4,128]{2,1,0:T(4,128)S(1)} %copy-done.10, ...), custom_call_target="tpu_custom_call" | custom-call | tf_op jit(solution)/shard_map/adjoint/pallas_call | solution.py:352
  78.2 26.0 %all_to_all.10.blocks = f32[16,40,128]{2,1,0:T(8,128)S(1)} all-to-all(f32[16,40,128]{2,1,0:T(8,128)S(1)} %adjoint.1), channel_id=1, replica_groups=mesh['tx'=16,'gx'=8,'gy'=2] {'tx'}, dimensions={0} | all-to-all | bytes 655360 | tf_op jit(solution)/shard_map/all_to_all | solution.py:375
  104.2 0.6 total.1
  (40 shorter events, 1.3 us)
Async XLA Ops:
  0.6 1.1 %copy-start = (f32[1,6,16,16,128]{4,3,2,1,0:T(8,128)S(1)}, f32[1,6,16,16,128]{4,3,2,1,0:T(8,128)}, u32[]{:S(2)}) copy-start(f32[1,6,16,16,128]{4,3,2,1,0:T(8,128)} %fwd.1) | copy-start | bytes 2359300
  1.8 0.9 copy-start.4
  2.7 0.9 copy-start.6
  3.6 24.9 %copy-start.1 = (f32[1,6,16,16,128]{4,3,2,1,0:T(8,128)S(1)}, f32[1,6,16,16,128]{4,3,2,1,0:T(8,128)}, u32[]{:S(2)}) copy-start(f32[1,6,16,16,128]{4,3,2,1,0:T(8,128)} %fwd.1) | copy-start | bytes 2359300
  3.6 24.9 %copy-start.5 = (f32[16,16,128]{2,1,0:T(8,128)S(1)}, f32[16,16,128]{2,1,0:T(8,128)}, u32[]{:S(2)}) copy-start(f32[16,16,128]{2,1,0:T(8,128)} %cond_h.1) | copy-start | bytes 393220
  3.6 24.9 %copy-start.7 = (f32[16,16,128]{2,1,0:T(8,128)S(1)}, f32[16,16,128]{2,1,0:T(8,128)}, u32[]{:S(2)}) copy-start(f32[16,16,128]{2,1,0:T(8,128)} %cond_v.1) | copy-start | bytes 393220
  3.6 24.9 %copy-start.13 = (f32[1,4,1,1,2,32]{5,4,3,2,1,0:T(2,128)S(1)}, f32[1,4,1,1,2,32]{5,4,3,2,1,0:T(2,128)}, u32[]{:S(2)}) copy-start(f32[1,4,1,1,2,32]{5,4,3,2,1,0:T(2,128)} %param.12) | copy-start | bytes 3076
  3.6 24.9 %copy-start.14 = (s32[1,1,32]{2,1,0:T(1,128)S(1)}, s32[1,1,32]{2,1,0:T(1,128)}, u32[]{:S(2)}) copy-start(s32[1,1,32]{2,1,0:T(1,128)} %param.15) | copy-start | bytes 388
  3.7 58.5 %copy-start.15 = (s32[1,1,16]{2,1,0:T(1,128)S(1)}, s32[1,1,16]{2,1,0:T(1,128)}, u32[]{:S(2)}) copy-start(s32[1,1,16]{2,1,0:T(1,128)} %param.14) | copy-start | bytes 196
  3.7 24.8 %collective-permute-start.7 = (f32[8,16,4,128]{3,2,1,0:T(4,128)S(1)}, f32[8,16,4,128]{3,2,1,0:T(4,128)S(1)}, u32[]{:S(2)}, u32[]{:S(2)}) collective-permute-start(f32[8,16,4,128]{3,2,1,0:T(4,128)S(1)} %get-tuple-element.25), channel_id=1, source_target_pairs={{0,1},{1,0},{2,3},{3,2},{4,5},{5,4},{6,7},{7,6},{8,9},{9,8},{10,11... | collective-permute-start | bytes 786440 | tf_op jit(solution)/shard_map/ppermute | solution.py:95
  7.5 19.6 %collective-permute-start.6 = (f32[26,16,128]{2,1,0:T(8,128)S(1)}, f32[26,16,128]{2,1,0:T(8,128)S(1)}, u32[]{:S(2)}, u32[]{:S(2)}) collective-permute-start(f32[26,16,128]{2,1,0:T(8,128)S(1)} %get-tuple-element.24), channel_id=1, source_target_pairs={{2,0},{3,1},{4,2},{5,3},{6,4},{7,5},{8,6},{9,7},{10,8},{11,9},{12,... | collective-permute-start | bytes 638984 | tf_op jit(solution)/shard_map/ppermute | solution.py:94
  8.8 19.6 %collective-permute-start.5 = (f32[29,16,128]{2,1,0:T(8,128)S(1)}, f32[29,16,128]{2,1,0:T(8,128)S(1)}, u32[]{:S(2)}, u32[]{:S(2)}) collective-permute-start(f32[29,16,128]{2,1,0:T(8,128)S(1)} %get-tuple-element.23), channel_id=1, source_target_pairs={{0,2},{1,3},{2,4},{3,5},{4,6},{5,7},{6,8},{7,9},{8,10},{9,11},{10,... | collective-permute-start | bytes 712712 | tf_op jit(solution)/shard_map/ppermute | solution.py:93
  12.8 8.5 %collective-permute-start.9 = (f32[26,4,128]{2,1,0:T(4,128)S(1)}, f32[26,4,128]{2,1,0:T(4,128)S(1)}, u32[]{:S(2)}, u32[]{:S(2)}) collective-permute-start(f32[26,4,128]{2,1,0:T(4,128)S(1)} %get-tuple-element.27), channel_id=1, source_target_pairs={{2,1},{3,0},{4,3},{5,2},{6,5},{7,4},{8,7},{9,6},{10,9},{11,8},{12,... | collective-permute-start | bytes 159752 | tf_op jit(solution)/shard_map/ppermute | solution.py:97
  14.1 7.7 %collective-permute-start.8 = (f32[29,4,128]{2,1,0:T(4,128)S(1)}, f32[29,4,128]{2,1,0:T(4,128)S(1)}, u32[]{:S(2)}, u32[]{:S(2)}) collective-permute-start(f32[29,4,128]{2,1,0:T(4,128)S(1)} %get-tuple-element.26), channel_id=1, source_target_pairs={{0,3},{1,2},{2,5},{3,4},{4,7},{5,6},{6,9},{7,8},{8,11},{9,10},{10,... | collective-permute-start | bytes 178184 | tf_op jit(solution)/shard_map/ppermute | solution.py:96
  19.3 1.1 %copy-start.2 = (f32[1,6,16,16,128]{4,3,2,1,0:T(8,128)S(1)}, f32[1,6,16,16,128]{4,3,2,1,0:T(8,128)}, u32[]{:S(2)}) copy-start(f32[1,6,16,16,128]{4,3,2,1,0:T(8,128)} %adj.1) | copy-start | bytes 2359300
  20.5 41.8 %copy-start.3 = (f32[1,6,16,16,128]{4,3,2,1,0:T(8,128)S(1)}, f32[1,6,16,16,128]{4,3,2,1,0:T(8,128)}, u32[]{:S(2)}) copy-start(f32[1,6,16,16,128]{4,3,2,1,0:T(8,128)} %adj.1) | copy-start | bytes 2359300
  21.4 21.7 %copy-start.16 = (f32[23,4,128]{2,1,0:T(4,128)}, f32[23,4,128]{2,1,0:T(4,128)S(1)}, u32[]{:S(2)}) copy-start(f32[23,4,128]{2,1,0:T(4,128)S(1)} %get-tuple-element.21) | copy-start | bytes 141316
  21.4 21.8 %copy-start.17 = (f32[20,4,128]{2,1,0:T(4,128)}, f32[20,4,128]{2,1,0:T(4,128)S(1)}, u32[]{:S(2)}) copy-start(f32[20,4,128]{2,1,0:T(4,128)S(1)} %get-tuple-element.22) | copy-start | bytes 122884
  21.4 40.9 %collective-permute-start.2 = (f32[6,16,4,128]{3,2,1,0:T(4,128)}, f32[6,16,4,128]{3,2,1,0:T(4,128)}, u32[]{:S(2)}, u32[]{:S(2)}) collective-permute-start(f32[6,16,4,128]{3,2,1,0:T(4,128)} %get-tuple-element.20), channel_id=1, source_target_pairs={{0,1},{1,0},{2,3},{3,2},{4,5},{5,4},{6,7},{7,6},{8,9},{9,8},{10,11... | collective-permute-start | bytes 589832 | tf_op jit(solution)/shard_map/ppermute | solution.py:95
  21.9 40.4 %collective-permute-start = (f32[23,16,128]{2,1,0:T(8,128)}, f32[23,16,128]{2,1,0:T(8,128)}, u32[]{:S(2)}, u32[]{:S(2)}) collective-permute-start(f32[23,16,128]{2,1,0:T(8,128)} %get-tuple-element.18), channel_id=1, source_target_pairs={{0,2},{1,3},{2,4},{3,5},{4,6},{5,7},{6,8},{7,9},{8,10},{9,11},{10,... | collective-permute-start | bytes 565256 | tf_op jit(solution)/shard_map/ppermute | solution.py:93
  27.2 35.0 %collective-permute-start.1 = (f32[20,16,128]{2,1,0:T(8,128)}, f32[20,16,128]{2,1,0:T(8,128)}, u32[]{:S(2)}, u32[]{:S(2)}) collective-permute-start(f32[20,16,128]{2,1,0:T(8,128)} %get-tuple-element.19), channel_id=1, source_target_pairs={{2,0},{3,1},{4,2},{5,3},{6,4},{7,5},{8,6},{9,7},{10,8},{11,9},{12,... | collective-permute-start | bytes 491528 | tf_op jit(solution)/shard_map/ppermute | solution.py:94
  43.8 18.5 %all-to-all-start = ((f32[16,16,128]{2,1,0:T(8,128)}), f32[16,16,128]{2,1,0:T(8,128)}, u32[]{:S(2)}, u32[]{:S(2)}) async-start(f32[16,16,128]{2,1,0:T(8,128)} %copy-done.8), calls=%async_computation | async-start | bytes 262144 | tf_op jit(solution)/shard_map/all_to_all | solution.py:351
  49.8 11.8 %collective-permute-start.3 = (f32[23,4,128]{2,1,0:T(4,128)}, f32[23,4,128]{2,1,0:T(4,128)S(1)}, u32[]{:S(2)}, u32[]{:S(2)}) collective-permute-start(f32[23,4,128]{2,1,0:T(4,128)} %copy-done.16), channel_id=1, source_target_pairs={{0,3},{1,2},{2,5},{3,4},{4,7},{5,6},{6,9},{7,8},{8,11},{9,10},{10,... | collective-permute-start | bytes 141320 | tf_op jit(solution)/shard_map/ppermute | solution.py:96
  54.2 6.7 %collective-permute-start.4 = (f32[20,4,128]{2,1,0:T(4,128)}, f32[20,4,128]{2,1,0:T(4,128)S(1)}, u32[]{:S(2)}, u32[]{:S(2)}) collective-permute-start(f32[20,4,128]{2,1,0:T(4,128)} %copy-done.17), channel_id=1, source_target_pairs={{2,1},{3,0},{4,3},{5,2},{6,5},{7,4},{8,7},{9,6},{10,9},{11,8},{12,... | collective-permute-start | bytes 122888 | tf_op jit(solution)/shard_map/ppermute | solution.py:97
  (5 other events, 3.5 us)

commit v2 on v1

v2 whole, which is shorter than its diff:
```python
import jax
import jax.numpy as jnp
from jax import lax
from jax.experimental import pallas as pl
from jax.experimental.pallas import tpu as pltpu
from jax.sharding import PartitionSpec as P

STEPS = 4
ZREC = 32
STEP_DT = 0.5
HALO = 4
CX = 16
CY = 16
NZ = 128
EX = CX + 2 * HALO
EXP = EX + 4
EY = CY + 2 * HALO
F32 = jnp.float32
HIGHEST = lax.Precision.HIGHEST

COMPS = 14
LOW = [
    (c, x)
    for c in range(COMPS)
    for x in range(CX - HALO + (c in (3, 6, 7, 11)), CX)
]
HIGH = [(c, x) for c in range(COMPS) for x in range(HALO - (c not in (1, 2, 9, 10)))]
VMEM = pl.BlockSpec(memory_space=pltpu.VMEM)
SMEM = pl.BlockSpec(memory_space=pltpu.SMEM)


def shape(*dims):
    return jax.ShapeDtypeStruct(dims, F32)


def params():
    return pltpu.CompilerParams(vmem_limit_bytes=8 * 1024 * 1024)


def plane_of(refs, comp, x):
    fwd, cond_h, cond_v, adj = refs
    if comp < 6:
        return fwd[0, comp, x]
    return adj[0, comp - 8, x] if comp > 7 else (cond_h, cond_v)[comp - 6][x]


def pack_kernel(fwd, cond_h, cond_v, adj, *refs):
    to_next, to_prev, to_side, side_next, side_prev = refs[:5]
    bufs, sem = refs[5:9], refs[9]
    copies = [
        pltpu.make_async_copy(src, dst, sem.at[k])
        for k, (src, dst) in enumerate(zip((fwd, cond_h, cond_v, adj), bufs))
    ]
    for copy in copies:
        copy.start()
    second = lax.axis_index("gy") == 1

    def edge(plane):
        return jnp.where(second, plane[0:HALO], plane[CY - HALO : CY])

    for which, comps in ((0, range(6)), (1, (6,)), (2, (7,)), (3, range(8, COMPS))):
        copies[which].wait()
        for c in comps:
            edges = [edge(plane_of(bufs, c, x)) for x in range(CX)]
            for x in range(CX):
                to_side[c, x] = edges[x]
            for k, (comp, x) in enumerate(LOW):
                if comp == c:
                    to_next[k] = plane_of(bufs, c, x)
                    side_next[k] = edges[x]
            for k, (comp, x) in enumerate(HIGH):
                if comp == c:
                    to_prev[k] = plane_of(bufs, c, x)
                    side_prev[k] = edges[x]


def pack(*arrays):
    return pl.pallas_call(
        pack_kernel,
        out_shape=[
            shape(len(LOW), CY, NZ),
            shape(len(HIGH), CY, NZ),
            shape(COMPS, CX, HALO, NZ),
            shape(len(LOW), HALO, NZ),
            shape(len(HIGH), HALO, NZ),
        ],
        in_specs=[pl.BlockSpec(memory_space=pltpu.HBM)] * 4,
        out_specs=[VMEM] * 5,
        scratch_shapes=[pltpu.VMEM(a.shape, F32) for a in arrays]
        + [pltpu.SemaphoreType.DMA((4,))],
        compiler_params=params(),
        name="pack",
    )(*arrays)


def exchange(to_next, to_prev, to_side, side_next, side_prev):
    size_x = lax.axis_size("gx")
    size_y = lax.axis_size("gy")

    def pairs(dx, swap):
        return [
            (x * size_y + y, (x + dx) * size_y + (1 - y if swap else y))
            for x in range(size_x)
            for y in range(size_y)
            if 0 <= x + dx < size_x
        ]

    both = ("gx", "gy")
    return (
        lax.ppermute(to_next, both, pairs(1, False)),
        lax.ppermute(to_prev, both, pairs(-1, False)),
        lax.ppermute(to_side, both, pairs(0, True)),
        lax.ppermute(side_next, both, pairs(1, True)),
        lax.ppermute(side_prev, both, pairs(-1, True)),
    )


def assemble(own, halos, comps, first):
    from_prev, from_next, from_side, side_prev, side_next = halos
    zero_rows = jnp.zeros((HALO, NZ), F32)
    zero_plane = jnp.zeros((EY, NZ), F32)

    def put(ref, index, i, plane, rows):
        ref[index, i, 0:CY] = plane
        ref[index, i, CY : CY + HALO] = jnp.where(first, rows, zero_rows)
        ref[index, i, CY + HALO : EY] = jnp.where(first, zero_rows, rows)

    for c, (ref, index) in comps.items():
        filled = set()
        for x in range(CX):
            put(ref, index, HALO + x, own(c, x), from_side[c, x])
            filled.add(HALO + x)
        for k, (comp, x) in enumerate(LOW):
            if comp == c:
                i = x - (CX - HALO)
                put(ref, index, i, from_prev[k], side_prev[k])
                filled.add(i)
        for k, (comp, x) in enumerate(HIGH):
            if comp == c:
                i = x + HALO + CX
                put(ref, index, i, from_next[k], side_next[k])
                filled.add(i)
        for i in range(EXP):
            if i not in filled:
                ref[index, i] = zero_plane


def helpers(gy):
    lane = lax.broadcasted_iota(jnp.int32, (EY, NZ), 1)
    row = lax.broadcasted_iota(jnp.int32, (EY, NZ), 0)
    y = jnp.where(row < CY + HALO, row, row - EY) + gy * CY
    inside = (y >= 0) & (y < 2 * CY)
    last, start = lane == NZ - 1, lane == 0

    def z_up(f):
        return jnp.where(last, 0.0, pltpu.roll(f, NZ - 1, 1))

    def z_down(f):
        return jnp.where(start, 0.0, pltpu.roll(f, 1, 1))

    def y_up(f):
        return pltpu.roll(f, EY - 1, 0)

    def y_down(f):
        return pltpu.roll(f, 1, 0)

    return lane, inside, z_up, z_down, y_up, y_down


def in_grid(gx, i):
    x = gx * CX + i - HALO
    return (x >= 0) & (x < 8 * CX)


MODE = "fused"
UNROLL = 8


def sweep(step, gx, elec, mag, coef, tools):
    _, inside, z_up, z_down, y_up, y_down = tools
    half = jnp.where(inside, STEP_DT, 0.0)
    zero = jnp.zeros((EY, NZ), F32)
    turns = -(-(EX - 1 - 2 * step) // UNROLL)

    def magnetic(i, field, after):
        ex, ey, ez = field
        _, ey_next, ez_next = after
        rate = jnp.where(in_grid(gx, i), half, zero)
        hx = mag[0, i] - rate * ((y_up(ez) - ez) - (z_up(ey) - ey))
        hy = mag[1, i] - rate * ((z_up(ex) - ex) - (ez_next - ez))
        hz = mag[2, i] - rate * ((ey_next - ey) - (y_up(ex) - ex))
        return hx, hy, hz

    def electric(i, field, now, before):
        ex, ey, ez = field
        hx, hy, hz = now
        decay_h, drive_h, decay_v, drive_v = (coef[k, i] for k in range(4))
        ex = decay_h * ex + drive_h * ((hz - y_down(hz)) - (hy - z_down(hy)))
        ey = decay_h * ey + drive_h * ((hx - z_down(hx)) - (hz - before[2]))
        ez = decay_v * ez + drive_v * ((hy - before[1]) - (hx - y_down(hx)))
        return ex, ey, ez

    def planes(ref, i, n):
        return [tuple(ref[c, i + k] for c in range(3)) for k in range(n)]

    def put(ref, i, values):
        for k, plane in enumerate(values):
            for c in range(3):
                ref[c, i + k] = plane[c]

    if MODE == "fused":

        def body(turn, carry):
            i = step + turn * UNROLL
            field = planes(elec, i, UNROLL + 1)
            now = [magnetic(i + k, field[k], field[k + 1]) for k in range(UNROLL)]
            put(mag, i, now)
            before = [(None, *carry)] + now[:-1]
            put(elec, i, [electric(i + k, field[k], now[k], before[k]) for k in range(UNROLL)])
            return now[-1][1:]

        lax.fori_loop(0, turns, body, (zero, zero))
    else:

        def body_h(turn, carry):
            i = step + turn * UNROLL
            field = planes(elec, i, UNROLL + 1)
            put(mag, i, [magnetic(i + k, field[k], field[k + 1]) for k in range(UNROLL)])
            return carry

        def body_e(turn, carry):
            i = step + 1 + turn * UNROLL
            field = planes(elec, i, UNROLL)
            now = planes(mag, i - 1, UNROLL + 1)
            put(elec, i, [electric(i + k, field[k], now[k + 1], now[k]) for k in range(UNROLL)])
            return carry

        lax.fori_loop(0, turns, body_h, 0)
        lax.fori_loop(0, -(-(EX - 2 - 2 * step) // UNROLL), body_e, 0)


def forward_kernel(fwd, cond_h, cond_v, *refs):
    halos, refs = refs[:5], refs[5:]
    observed, rec_vec, rec, coef, stored, spread, block, elec, mag, rows = refs
    gx, gy = lax.axis_index("gx"), lax.axis_index("gy")
    tools = helpers(gy)
    lane, inside = tools[0], tools[1]

    comps = {c: (elec, c) if c < 3 else (mag, c - 3) for c in range(6)}
    comps |= {6: (coef, 0), 7: (coef, 2)}
    assemble(lambda c, x: plane_of((fwd, cond_h, cond_v, None), c, x), halos, comps, gy == 0)

    def coefficients(i, carry):
        keep = inside & in_grid(gx, i)
        for k in (0, 2):
            half_rate = 0.25 * coef[k, i]
            inverse = 1.0 / (1.0 + half_rate)
            coef[k, i] = jnp.where(keep, (1.0 - half_rate) * inverse, 0.0)
            coef[k + 1, i] = jnp.where(keep, STEP_DT * inverse, 0.0)
        return carry

    lax.fori_loop(0, EX, coefficients, 0)
    for k in (1, 3):
        coef[k, EX:EXP] = jnp.zeros((EXP - EX, EY, NZ), F32)

    for step in range(STEPS):
        sweep(step, gx, elec, mag, coef, tools)
        stored[step] = elec[:, HALO : HALO + CX, 0:CY]

    for r in range(rec.shape[0]):
        x, y = rec[r] >> 4, rec[r] & 15
        for step in range(STEPS):
            for c in range(2):
                rows[pl.ds((2 * step + c) * 32 + r, 1), :] = stored[step, c, x, pl.ds(y, 1), :]
    pick = (lax.broadcasted_iota(jnp.int32, (8, NZ), 1) == ZREC).astype(F32)
    picked = lax.dot_general(
        pick, rows[...], (((1,), (1,)), ((), ())), precision=HIGHEST, preferred_element_type=F32
    )
    lane8 = lax.broadcasted_iota(jnp.int32, (8, NZ), 1)
    row8 = lax.broadcasted_iota(jnp.int32, (8, NZ), 0)
    own = jnp.where(lane8 // 32 == row8, picked[:, 0:NZ], 0.0)
    own = own + jnp.where(lane8 // 32 + 4 == row8, picked[:, NZ : 2 * NZ], 0.0)
    own = own + pltpu.roll(own, 64, 1)
    own = own + pltpu.roll(own, 32, 1)
    residual = own[:, 0:32] - observed[...]
    misfit = 0.5 * jnp.sum(residual * residual)
    cells = rec_vec[...]
    at_y = ((cells & 15) == lax.broadcasted_iota(jnp.int32, (CY, 32), 0)).astype(F32)
    at_x = (cells >> 4) == lax.broadcasted_iota(jnp.int32, (NZ, 32), 0) // 8
    weighted = jnp.where(at_x, jnp.tile(residual, (16, 1)), 0.0)
    spread_now = lax.dot_general(
        at_y, weighted, (((1,), (1,)), ((), ())), precision=HIGHEST, preferred_element_type=F32
    )
    spread[...] = spread_now
    low_rows, high_rows = spread_now[0:8], spread_now[8:16]
    edges = jnp.where((lane8 < 32) | (lane8 >= 96), low_rows, pltpu.roll(high_rows, 64, 1))
    is_first = gy == 0
    side = jnp.where(is_first, high_rows, low_rows)
    used = row8 // HALO == 1 - gy
    side = jnp.where(used, side, misfit)
    for t in range(16):
        block[t, 0:8] = edges
        block[t, 8:16] = side


def adjoint_kernel(adj, *refs):
    halos, refs = refs[:5], refs[5:]
    coef, stored, spread, blocks, foot, owner, keep, send, elec, mag, inject, grad = refs
    gx, gy = lax.axis_index("gx"), lax.axis_index("gy")
    tools = helpers(gy)
    lane, inside = tools[0], tools[1]

    comps = {8 + c: (elec, c) if c < 3 else (mag, c - 3) for c in range(6)}
    assemble(lambda c, x: adj[0, c - 8, x], halos, comps, gy == 0)

    row8 = lax.broadcasted_iota(jnp.int32, (8, NZ), 0)
    used = row8 // HALO == gy
    for k, dx in enumerate((-1, 0, 1)):
        there = (gx + dx >= 0) & (gx + dx < 8)
        near = jnp.clip(gx + dx, 0, 7)
        if dx == 0:
            inject[k, 0:16] = spread[...]
        else:
            edges = jnp.where(there, blocks[2 * near + gy, 0:8], 0.0)
            inject[k, 0:8] = edges
            inject[k, 8:16] = pltpu.roll(edges, 64, 1)
        side = blocks[2 * near + 1 - gy, 8:16]
        inject[k, 16:24] = jnp.where(used & there, side, 0.0)

    at_depth = lane == ZREC

    for step in range(STEPS):
        when = STEPS - 1 - step

        def add(turn, carry, when=when):
            for k in range(4):
                i = turn * 4 + k
                tile = jnp.where(turn == 0, 0, jnp.where(turn < 5, 1, 2))
                x = (i + CX - HALO) & (CX - 1)
                source = inject[tile]
                shift = (ZREC + NZ - (x * 8 + 2 * when)) & (NZ - 1)
                for c in range(2):
                    moved = pltpu.roll(source, (shift - c) & (NZ - 1), 1)
                    elec[c, i] += jnp.where(at_depth, moved, 0.0)
            return carry

        lax.fori_loop(0, EX // 4, add, 0)
        sweep(step, gx, elec, mag, coef, tools)

        def accumulate(x, carry, when=when, step=step):
            ax, ay, az = (elec[c, HALO + x, 0:CY] for c in range(3))
            horizontal = ax * stored[when, 0, x] + ay * stored[when, 1, x]
            vertical = az * stored[when, 2, x]
            if step:
                horizontal = grad[0, x] + horizontal
                vertical = grad[1, x] + vertical
            grad[0, x] = horizontal
            grad[1, x] = vertical
            return carry

        lax.fori_loop(0, CX, accumulate, 0)

    flag = foot[0].astype(F32)
    misfit = blocks[0, 8:16][0:1]
    for t in range(1, 16):
        top = 0 if t % 2 == 0 else HALO
        misfit = misfit + blocks[t, 8:16][top : top + 1]
    core = lax.axis_index("tx") & 1
    for z in range(8):
        for ref, mine in ((keep, core), (send, 1 - core)):
            row = owner[2 * z + mine]
            ref[32 * z : 32 * z + 16] = grad[0, row] * flag
            ref[32 * z + 16 : 32 * z + 32] = grad[1, row] * flag
    keep[256:264] = jnp.broadcast_to(misfit, (8, NZ))
    send[256:264] = jnp.broadcast_to(misfit, (8, NZ))


def pair_kernel(mine, other, out):
    misfit = mine[256:264] + other[256:264]
    for z in range(8):
        out[z, 0:32] = mine[32 * z : 32 * z + 32] + other[32 * z : 32 * z + 32]
        out[z, 32:40] = misfit


def sum_kernel(blocks, part, misfit):
    total = blocks[0]
    for z in range(1, 8):
        total = total + blocks[z]
    part[0, 0, 0, 0] = total[0:16]
    part[0, 0, 1, 0] = total[16:32]
    misfit[...] = total[32:33, 0:1]


def on_device(cond_h, cond_v, fwd_init, adj_init, observed, footprint, owner, rec_cells):
    halos = exchange(*pack(fwd_init, cond_h, cond_v, adj_init))
    rec = rec_cells.reshape(32)
    coef, stored, spread, block = pl.pallas_call(
        forward_kernel,
        out_shape=[
            shape(4, EXP, EY, NZ),
            shape(STEPS, 3, CX, CY, NZ),
            shape(CY, NZ),
            shape(16, 16, NZ),
        ],
        in_specs=[VMEM] * 10 + [SMEM],
        out_specs=[VMEM] * 4,
        scratch_shapes=[
            pltpu.VMEM((3, EXP, EY, NZ), F32),
            pltpu.VMEM((3, EXP, EY, NZ), F32),
            pltpu.VMEM((256, NZ), F32),
        ],
        compiler_params=params(),
        name="forward",
    )(fwd_init, cond_h, cond_v, *halos, observed.reshape(8, 32), rec.reshape(1, 32), rec)
    blocks = lax.all_to_all(block, ("gx", "gy"), 0, 0, tiled=True)
    keep, send = pl.pallas_call(
        adjoint_kernel,
        out_shape=[shape(264, NZ)] * 2,
        in_specs=[VMEM] * 10 + [SMEM, SMEM],
        out_specs=[VMEM] * 2,
        scratch_shapes=[
            pltpu.VMEM((3, EXP, EY, NZ), F32),
            pltpu.VMEM((3, EXP, EY, NZ), F32),
            pltpu.VMEM((3, EY, NZ), F32),
            pltpu.VMEM((2, CX, CY, NZ), F32),
        ],
        compiler_params=params(),
        name="adjoint",
    )(
        adj_init,
        *halos,
        coef,
        stored,
        spread,
        blocks,
        footprint.reshape(1),
        owner.reshape(16),
    )
    size = lax.axis_size("tx")
    other = lax.ppermute(send, "tx", [(t, t ^ 1) for t in range(size)])
    paired = pl.pallas_call(
        pair_kernel,
        out_shape=shape(8, 40, NZ),
        in_specs=[VMEM] * 2,
        out_specs=VMEM,
        compiler_params=params(),
        name="pair",
    )(keep, other)
    along_z = [list(range(core, size, 2)) for core in range(2)]
    summed = lax.all_to_all(paired, "tx", 0, 0, axis_index_groups=along_z, tiled=True)
    part, misfit = pl.pallas_call(
        sum_kernel,
        out_shape=[shape(1, 1, 2, 1, CY, NZ), shape(1, 1)],
        in_specs=[VMEM],
        out_specs=[VMEM, VMEM],
        compiler_params=params(),
        name="total",
    )(summed)
    return part, misfit.reshape(())


def solution(mesh):
    placed = (
        P("gx", "gy", None),
        P("gx", "gy", None),
        P("tx", None, "gx", "gy", None),
        P("tx", None, "gx", "gy", None),
        P("tx", None, "gx", "gy", None, None),
        P("tx", "gx", "gy"),
        P("gx", "gy", None),
        P("gx", "gy", None),
    )
    return jax.shard_map(
        on_device,
        mesh=mesh,
        in_specs=placed,
        out_specs=(P("gx", "tx", None, None, "gy", None), P()),
        check_vma=False,
    )
```

time: 106 us -> 88.5 us (0.83)
  waiting for transfers between devices: 4.82 us -> 24.5 us
  Pallas kernels: 30.5 us -> 12 us
  starting transfers between devices: 34.4 us -> 24.4 us
  blocking collectives: 26 us -> 16.6 us
  local copies, waits for them, and re-layouts: 7.55 us -> 9.1 us
    pallas_call x4, Pallas kernels: 29.9 us -> 11.4 us  [the longest x1 6.05 us: on_device(): pl.pallas_call(adjoint_kernel, out_shape=[shape(264, NZ)] * 2, in_specs=[...]
    all_to_all x1, blocking collectives: 26 us -> 16.6 us  [on_device(): lax.all_to_all(paired, 'tx', 0, 0, axis_index_groups=along_z, tiled=True)]
    ppermute x2 -> x1, waiting for transfers between devices: 0.01 us -> 7.99 us  [exchange(): lax.ppermute(to_next, both, pairs(1, False))]
    ppermute x2 -> x1, starting transfers between devices: 9.32 us -> 2.32 us  [exchange(): lax.ppermute(to_next, both, pairs(1, False))]
    all_to_all x1, waiting for transfers between devices: 0.01 us -> 6.4 us  [on_device(): blocks = lax.all_to_all(block, ('gx', 'gy'), 0, 0, tiled=True)]
    ppermute x2 -> x1, starting transfers between devices: 9.62 us -> 4.37 us  [exchange(): lax.ppermute(side_next, both, pairs(1, True))]
    ppermute x0 -> x1, starting transfers between devices: none -> 3.06 us  [on_device(): other = lax.ppermute(send, 'tx', [(t, t ^ 1) for t in range(size)])]
    ppermute x2 -> x1, waiting for transfers between devices: 0.01 us -> 2.29 us  [exchange(): lax.ppermute(to_prev, both, pairs(-1, False))]
  transfers between devices with their start and end apart: 11 -> 7, of which waited for: 1 -> 5; matrix products, arithmetic and copies ran while one was open for 0% -> 0% of each run, Pallas kernels for 15% -> 0%
where the time goes in v2:
time: 88.5 us; the launch traced here: 88 us
  waiting for transfers between devices  24.5 us (28%)
  starting transfers between devices  24.4 us (28%)
  blocking collectives  16.6 us (19%)
  Pallas kernels  12 us (14%)
  local copies, waits for them, and re-layouts  9.1 us (10%)
  between operations  1.38 us (2%)
    all_to_all x1, blocking collectives, on_device(): lax.all_to_all(paired, 'tx', 0, 0, axis_index_groups=along_z, tiled=True)  16.6 us
    unnamed x30, local copies, waits for them, and re-layouts  9.1 us
    all_to_all x1, starting transfers between devices, on_device(): blocks = lax.all_to_all(block, ('gx', 'gy'), 0, 0, tiled=True)  8.27 us
    ppermute x1, waiting for transfers between devices, exchange(): lax.ppermute(to_next, both, pairs(1, False))  7.99 us
    ppermute x1, waiting for transfers between devices, exchange(): lax.ppermute(side_prev, both, pairs(-1, True))  6.79 us
    all_to_all x1, waiting for transfers between devices, on_device(): blocks = lax.all_to_all(block, ('gx', 'gy'), 0, 0, tiled=True)  6.4 us
    pallas_call x1, Pallas kernels, on_device(): pl.pallas_call(adjoint_kernel, out_shape=[shape(264, NZ)] * 2, in_specs=[...  6.05 us
    pallas_call x1, Pallas kernels, on_device(): pl.pallas_call(forward_kernel, out_shape=[shape(4, EXP, EY, NZ), shape(ST...  4.67 us
  transfers between devices with their start and end apart: 7, of which 5 were waited for; matrix products, arithmetic and copies ran while one was open for 0% of the time, Pallas kernels for 0%

profile of v2, /device:TPU:1, one launch (start us, length us, event | category | flops | bytes accessed | tf_op | source)
XLA Modules:
  0.0 88.0 jit_solution(13365169029523428032)
XLA Ops:
  0.6 1.1 %copy-done = f32[1,6,16,16,128]{4,3,2,1,0:T(8,128)S(1)} copy-done((f32[1,6,16,16,128]{4,3,2,1,0:T(8,128)S(1)}, f32[1,6,16,16,128]{4,3,2,1,0:T(8,128)}, u32[]{:S(2)}) %copy-start) | copy-done | bytes 786456
  1.8 1.1 %copy-done.2 = f32[1,6,16,16,128]{4,3,2,1,0:T(8,128)S(1)} copy-done((f32[1,6,16,16,128]{4,3,2,1,0:T(8,128)S(1)}, f32[1,6,16,16,128]{4,3,2,1,0:T(8,128)}, u32[]{:S(2)}) %copy-start.2) | copy-done | bytes 786456
  2.9 0.9 %copy-done.7 = f32[16,16,128]{2,1,0:T(8,128)S(1)} copy-done((f32[16,16,128]{2,1,0:T(8,128)S(1)}, f32[16,16,128]{2,1,0:T(8,128)}, u32[]{:S(2)}) %copy-start.7) | copy-done | bytes 131096
  3.8 0.9 %copy-done.8 = f32[16,16,128]{2,1,0:T(8,128)S(1)} copy-done((f32[16,16,128]{2,1,0:T(8,128)S(1)}, f32[16,16,128]{2,1,0:T(8,128)}, u32[]{:S(2)}) %copy-start.8) | copy-done | bytes 131096
  5.4 3.8 %collective-permute-start.2 = (f32[14,16,4,128]{3,2,1,0:T(4,128)S(1)}, f32[14,16,4,128]{3,2,1,0:T(4,128)S(1)}, u32[]{:S(2)}, u32[]{:S(2)}) collective-permute-start(f32[14,16,4,128]{3,2,1,0:T(4,128)S(1)} %get-tuple-element.17), channel_id=1, source_target_pairs={{0,1},{1,0},{2,3},{3,2},{4,5},{5,4},{6,7},{7,6},{8,9},{9,8},{10,11... | collective-permute-start | bytes 1376264 | tf_op jit(solution)/shard_map/ppermute | solution.py:112
  9.2 2.3 %collective-permute-start = (f32[52,16,128]{2,1,0:T(8,128)S(1)}, f32[52,16,128]{2,1,0:T(8,128)S(1)}, u32[]{:S(2)}, u32[]{:S(2)}) collective-permute-start(f32[52,16,128]{2,1,0:T(8,128)S(1)} %get-tuple-element.15), channel_id=1, source_target_pairs={{0,2},{1,3},{2,4},{3,5},{4,6},{5,7},{6,8},{7,9},{8,10},{9,11},{10,... | collective-permute-start | bytes 1277960 | tf_op jit(solution)/shard_map/ppermute | solution.py:110
  11.5 1.3 %collective-permute-start.1 = (f32[46,16,128]{2,1,0:T(8,128)S(1)}, f32[46,16,128]{2,1,0:T(8,128)S(1)}, u32[]{:S(2)}, u32[]{:S(2)}) collective-permute-start(f32[46,16,128]{2,1,0:T(8,128)S(1)} %get-tuple-element.16), channel_id=1, source_target_pairs={{2,0},{3,1},{4,2},{5,3},{6,4},{7,5},{8,6},{9,7},{10,8},{11,9},{12,... | collective-permute-start | bytes 1130504 | tf_op jit(solution)/shard_map/ppermute | solution.py:111
  12.8 4.4 %collective-permute-start.3 = (f32[52,4,128]{2,1,0:T(4,128)S(1)}, f32[52,4,128]{2,1,0:T(4,128)S(1)}, u32[]{:S(2)}, u32[]{:S(2)}) collective-permute-start(f32[52,4,128]{2,1,0:T(4,128)S(1)} %get-tuple-element.18), channel_id=1, source_target_pairs={{0,3},{1,2},{2,5},{3,4},{4,7},{5,6},{6,9},{7,8},{8,11},{9,10},{10,... | collective-permute-start | bytes 319496 | tf_op jit(solution)/shard_map/ppermute | solution.py:113
  17.2 1.3 %collective-permute-start.4 = (f32[46,4,128]{2,1,0:T(4,128)S(1)}, f32[46,4,128]{2,1,0:T(4,128)S(1)}, u32[]{:S(2)}, u32[]{:S(2)}) collective-permute-start(f32[46,4,128]{2,1,0:T(4,128)S(1)} %get-tuple-element.19), channel_id=1, source_target_pairs={{2,1},{3,0},{4,3},{5,2},{6,5},{7,4},{8,7},{9,6},{10,9},{11,8},{12,... | collective-permute-start | bytes 282632 | tf_op jit(solution)/shard_map/ppermute | solution.py:114
  18.5 6.8 %collective-permute-done.4.refs_4_ = f32[46,4,128]{2,1,0:T(4,128)S(1)} collective-permute-done((f32[46,4,128]{2,1,0:T(4,128)S(1)}, f32[46,4,128]{2,1,0:T(4,128)S(1)}, u32[]{:S(2)}, u32[]{:S(2)}) %collective-permute-start.4) | collective-permute-done | bytes 94240 | tf_op jit(solution)/shard_map/ppermute | solution.py:114
  25.3 2.3 %collective-permute-done.1.refs_1_ = f32[46,16,128]{2,1,0:T(8,128)S(1)} collective-permute-done((f32[46,16,128]{2,1,0:T(8,128)S(1)}, f32[46,16,128]{2,1,0:T(8,128)S(1)}, u32[]{:S(2)}, u32[]{:S(2)}) %collective-permute-start.1) | collective-permute-done | bytes 376864 | tf_op jit(solution)/shard_map/ppermute | solution.py:111
  27.6 8.0 %collective-permute-done.refs_0_ = f32[52,16,128]{2,1,0:T(8,128)S(1)} collective-permute-done((f32[52,16,128]{2,1,0:T(8,128)S(1)}, f32[52,16,128]{2,1,0:T(8,128)S(1)}, u32[]{:S(2)}, u32[]{:S(2)}) %collective-permute-start) | collective-permute-done | bytes 426016 | tf_op jit(solution)/shard_map/ppermute | solution.py:110
  35.6 4.7 %forward.1 = (f32[4,28,24,128]{3,2,1,0:T(8,128)S(1)}, f32[4,3,16,16,128]{4,3,2,1,0:T(8,128)S(1)}, f32[16,128]{1,0:T(8,128)S(1)}, f32[16,16,128]{2,1,0:T(8,128)S(1)}) custom-call(f32[1,6,16,16,128]{4,3,2,1,0:T(8,128)S(1)} %copy-done.2, f32[16,16,128]{2,1,0:T(8,128)S(1)} %copy-done.7, f32[16,16,128]{2,1,0:T(8,128)S(1)} %copy-done.8, ...), custom_call_target="tpu_custom_call" | custom-call | tf_op jit(solution)/shard_map/forward/pallas_call | solution.py:397
  40.3 1.1 %copy-done.5 = f32[4,28,24,128]{3,2,1,0:T(8,128)} copy-done((f32[4,28,24,128]{3,2,1,0:T(8,128)}, f32[4,28,24,128]{3,2,1,0:T(8,128)S(1)}, u32[]{:S(2)}) %copy-start.5) | copy-done | bytes 1376280
  41.4 0.6 copy-done.11
  42.1 8.3 %all-to-all-start = ((f32[16,16,128]{2,1,0:T(8,128)}), f32[16,16,128]{2,1,0:T(8,128)S(1)}, u32[]{:S(2)}, u32[]{:S(2)}) async-start(f32[16,16,128]{2,1,0:T(8,128)} %copy-done.11), calls=%async_computation | async-start | bytes 262144 | tf_op jit(solution)/shard_map/all_to_all | solution.py:415
  51.0 6.4 %all-to-all-done.refs_8_ = f32[16,16,128]{2,1,0:T(8,128)S(1)} async-done(((f32[16,16,128]{2,1,0:T(8,128)}), f32[16,16,128]{2,1,0:T(8,128)S(1)}, u32[]{:S(2)}, u32[]{:S(2)}) %all-to-all-start) | async-done | bytes 131104 | tf_op jit(solution)/shard_map/all_to_all | solution.py:415
  57.4 1.0 %copy-done.4 = f32[46,16,128]{2,1,0:T(8,128)S(1)} copy-done((f32[46,16,128]{2,1,0:T(8,128)S(1)}, f32[46,16,128]{2,1,0:T(8,128)}, u32[]{:S(2)}) %copy-start.4) | copy-done | bytes 376856
  58.4 1.3 %copy-done.6 = f32[4,28,24,128]{3,2,1,0:T(8,128)S(1)} copy-done((f32[4,28,24,128]{3,2,1,0:T(8,128)S(1)}, f32[4,28,24,128]{3,2,1,0:T(8,128)}, u32[]{:S(2)}) %copy-start.6) | copy-done | bytes 1376280
  59.7 0.9 %copy-done.10 = f32[46,4,128]{2,1,0:T(4,128)S(1)} copy-done((f32[46,4,128]{2,1,0:T(4,128)S(1)}, f32[46,4,128]{2,1,0:T(4,128)}, u32[]{:S(2)}) %copy-start.10) | copy-done | bytes 94232
  60.6 6.1 %adjoint.1 = (f32[264,128]{1,0:T(8,128)S(1)}, f32[264,128]{1,0:T(8,128)S(1)}) custom-call(f32[1,6,16,16,128]{4,3,2,1,0:T(8,128)S(1)} %copy-done.1, f32[52,16,128]{2,1,0:T(8,128)S(1)} %collective-permute-done.refs_0_, f32[46,16,128]{2,1,0:T(8,128)S(1)} %copy-done.4, f32[14,16,4,128]{3,2,1,0:T(4,128)S(1)} %collective-permute-done.2.refs_2_, ...), custom_call_target="tpu_custom_call" | custom-call | tf_op jit(solution)/shard_map/adjoint/pallas_call | solution.py:416
  66.7 3.1 %collective-permute-start.5 = (f32[264,128]{1,0:T(8,128)S(1)}, f32[264,128]{1,0:T(8,128)S(1)}, u32[]{:S(2)}, u32[]{:S(2)}) collective-permute-start(f32[264,128]{1,0:T(8,128)S(1)} %get-tuple-element.25), channel_id=1, source_target_pairs={{0,16},{16,0},{32,48},{48,32},{64,80},{80,64},{96,112},{112,96},{1... | collective-permute-start | bytes 405512 | tf_op jit(solution)/shard_map/ppermute | solution.py:440
  69.7 1.0 %collective-permute-done.5.other = f32[264,128]{1,0:T(8,128)S(1)} collective-permute-done((f32[264,128]{1,0:T(8,128)S(1)}, f32[264,128]{1,0:T(8,128)S(1)}, u32[]{:S(2)}, u32[]{:S(2)}) %collective-permute-start.5) | collective-permute-done | bytes 135200 | tf_op jit(solution)/shard_map/ppermute | solution.py:440
  70.8 16.6 %all_to_all.10.blocks = f32[8,40,128]{2,1,0:T(8,128)S(1)} all-to-all(f32[8,40,128]{2,1,0:T(8,128)S(1)} %pair.1), channel_id=1, replica_groups={{0,32,64,96,128,160,192,224},{16,48,80,112,144,176,208,240},{1,33,65,97..., dimensions={0} | all-to-all | bytes 327680 | tf_op jit(solution)/shard_map/all_to_all | solution.py:450
  (26 shorter events, 1.3 us)
Async XLA Ops:
  0.6 1.1 %copy-start = (f32[1,6,16,16,128]{4,3,2,1,0:T(8,128)S(1)}, f32[1,6,16,16,128]{4,3,2,1,0:T(8,128)}, u32[]{:S(2)}) copy-start(f32[1,6,16,16,128]{4,3,2,1,0:T(8,128)} %adj.3) | copy-start | bytes 2359300
  1.8 1.1 %copy-start.2 = (f32[1,6,16,16,128]{4,3,2,1,0:T(8,128)S(1)}, f32[1,6,16,16,128]{4,3,2,1,0:T(8,128)}, u32[]{:S(2)}) copy-start(f32[1,6,16,16,128]{4,3,2,1,0:T(8,128)} %fwd.3) | copy-start | bytes 2359300
  2.9 0.9 %copy-start.7 = (f32[16,16,128]{2,1,0:T(8,128)S(1)}, f32[16,16,128]{2,1,0:T(8,128)}, u32[]{:S(2)}) copy-start(f32[16,16,128]{2,1,0:T(8,128)} %cond_h.3) | copy-start | bytes 393220
  3.8 0.9 %copy-start.8 = (f32[16,16,128]{2,1,0:T(8,128)S(1)}, f32[16,16,128]{2,1,0:T(8,128)}, u32[]{:S(2)}) copy-start(f32[16,16,128]{2,1,0:T(8,128)} %cond_v.3) | copy-start | bytes 393220
  4.7 30.9 %copy-start.12 = (f32[1,4,1,1,2,32]{5,4,3,2,1,0:T(2,128)S(1)}, f32[1,4,1,1,2,32]{5,4,3,2,1,0:T(2,128)}, u32[]{:S(2)}) copy-start(f32[1,4,1,1,2,32]{5,4,3,2,1,0:T(2,128)} %param.12) | copy-start | bytes 3076
  4.7 30.9 %copy-start.13 = (s32[1,1,32]{2,1,0:T(1,128)S(1)}, s32[1,1,32]{2,1,0:T(1,128)}, u32[]{:S(2)}) copy-start(s32[1,1,32]{2,1,0:T(1,128)} %param.15) | copy-start | bytes 388
  5.4 52.0 %copy-start.1 = (f32[1,6,16,16,128]{4,3,2,1,0:T(8,128)S(1)}, f32[1,6,16,16,128]{4,3,2,1,0:T(8,128)}, u32[]{:S(2)}) copy-start(f32[1,6,16,16,128]{4,3,2,1,0:T(8,128)} %adj.3) | copy-start | bytes 2359300
  5.4 52.0 %copy-start.14 = (s32[1,1,16]{2,1,0:T(1,128)S(1)}, s32[1,1,16]{2,1,0:T(1,128)}, u32[]{:S(2)}) copy-start(s32[1,1,16]{2,1,0:T(1,128)} %param.14) | copy-start | bytes 196
  5.4 30.2 %collective-permute-start.2 = (f32[14,16,4,128]{3,2,1,0:T(4,128)S(1)}, f32[14,16,4,128]{3,2,1,0:T(4,128)S(1)}, u32[]{:S(2)}, u32[]{:S(2)}) collective-permute-start(f32[14,16,4,128]{3,2,1,0:T(4,128)S(1)} %get-tuple-element.17), channel_id=1, source_target_pairs={{0,1},{1,0},{2,3},{3,2},{4,5},{5,4},{6,7},{7,6},{8,9},{9,8},{10,11... | collective-permute-start | bytes 1376264 | tf_op jit(solution)/shard_map/ppermute | solution.py:112
  9.2 26.4 %collective-permute-start = (f32[52,16,128]{2,1,0:T(8,128)S(1)}, f32[52,16,128]{2,1,0:T(8,128)S(1)}, u32[]{:S(2)}, u32[]{:S(2)}) collective-permute-start(f32[52,16,128]{2,1,0:T(8,128)S(1)} %get-tuple-element.15), channel_id=1, source_target_pairs={{0,2},{1,3},{2,4},{3,5},{4,6},{5,7},{6,8},{7,9},{8,10},{9,11},{10,... | collective-permute-start | bytes 1277960 | tf_op jit(solution)/shard_map/ppermute | solution.py:110
  11.5 16.1 %collective-permute-start.1 = (f32[46,16,128]{2,1,0:T(8,128)S(1)}, f32[46,16,128]{2,1,0:T(8,128)S(1)}, u32[]{:S(2)}, u32[]{:S(2)}) collective-permute-start(f32[46,16,128]{2,1,0:T(8,128)S(1)} %get-tuple-element.16), channel_id=1, source_target_pairs={{2,0},{3,1},{4,2},{5,3},{6,4},{7,5},{8,6},{9,7},{10,8},{11,9},{12,... | collective-permute-start | bytes 1130504 | tf_op jit(solution)/shard_map/ppermute | solution.py:111
  12.8 12.5 %collective-permute-start.3 = (f32[52,4,128]{2,1,0:T(4,128)S(1)}, f32[52,4,128]{2,1,0:T(4,128)S(1)}, u32[]{:S(2)}, u32[]{:S(2)}) collective-permute-start(f32[52,4,128]{2,1,0:T(4,128)S(1)} %get-tuple-element.18), channel_id=1, source_target_pairs={{0,3},{1,2},{2,5},{3,4},{4,7},{5,6},{6,9},{7,8},{8,11},{9,10},{10,... | collective-permute-start | bytes 319496 | tf_op jit(solution)/shard_map/ppermute | solution.py:113
  17.2 8.1 %collective-permute-start.4 = (f32[46,4,128]{2,1,0:T(4,128)S(1)}, f32[46,4,128]{2,1,0:T(4,128)S(1)}, u32[]{:S(2)}, u32[]{:S(2)}) collective-permute-start(f32[46,4,128]{2,1,0:T(4,128)S(1)} %get-tuple-element.19), channel_id=1, source_target_pairs={{2,1},{3,0},{4,3},{5,2},{6,5},{7,4},{8,7},{9,6},{10,9},{11,8},{12,... | collective-permute-start | bytes 282632 | tf_op jit(solution)/shard_map/ppermute | solution.py:114
  25.3 16.8 %copy-start.9 = (f32[46,4,128]{2,1,0:T(4,128)}, f32[46,4,128]{2,1,0:T(4,128)S(1)}, u32[]{:S(2)}) copy-start(f32[46,4,128]{2,1,0:T(4,128)S(1)} %collective-permute-done.4.refs_4_) | copy-start | bytes 282628
  27.6 12.7 %copy-start.3 = (f32[46,16,128]{2,1,0:T(8,128)}, f32[46,16,128]{2,1,0:T(8,128)S(1)}, u32[]{:S(2)}) copy-start(f32[46,16,128]{2,1,0:T(8,128)S(1)} %collective-permute-done.1.refs_1_) | copy-start | bytes 1130500
  40.3 1.1 %copy-start.5 = (f32[4,28,24,128]{3,2,1,0:T(8,128)}, f32[4,28,24,128]{3,2,1,0:T(8,128)S(1)}, u32[]{:S(2)}) copy-start(f32[4,28,24,128]{3,2,1,0:T(8,128)S(1)} %get-tuple-element.20.refs_5_) | copy-start | bytes 4128772
  41.4 0.7 copy-start.11
  42.1 15.3 %all-to-all-start = ((f32[16,16,128]{2,1,0:T(8,128)}), f32[16,16,128]{2,1,0:T(8,128)S(1)}, u32[]{:S(2)}, u32[]{:S(2)}) async-start(f32[16,16,128]{2,1,0:T(8,128)} %copy-done.11), calls=%async_computation | async-start | bytes 262144 | tf_op jit(solution)/shard_map/all_to_all | solution.py:415
  57.4 1.0 %copy-start.4 = (f32[46,16,128]{2,1,0:T(8,128)S(1)}, f32[46,16,128]{2,1,0:T(8,128)}, u32[]{:S(2)}) copy-start(f32[46,16,128]{2,1,0:T(8,128)} %copy-done.3) | copy-start | bytes 1130500
  58.4 1.3 %copy-start.6 = (f32[4,28,24,128]{3,2,1,0:T(8,128)S(1)}, f32[4,28,24,128]{3,2,1,0:T(8,128)}, u32[]{:S(2)}) copy-start(f32[4,28,24,128]{3,2,1,0:T(8,128)} %copy-done.5) | copy-start | bytes 4128772
  59.7 0.9 %copy-start.10 = (f32[46,4,128]{2,1,0:T(4,128)S(1)}, f32[46,4,128]{2,1,0:T(4,128)}, u32[]{:S(2)}) copy-start(f32[46,4,128]{2,1,0:T(4,128)} %copy-done.9) | copy-start | bytes 282628
  66.7 4.1 %collective-permute-start.5 = (f32[264,128]{1,0:T(8,128)S(1)}, f32[264,128]{1,0:T(8,128)S(1)}, u32[]{:S(2)}, u32[]{:S(2)}) collective-permute-start(f32[264,128]{1,0:T(8,128)S(1)} %get-tuple-element.25), channel_id=1, source_target_pairs={{0,16},{16,0},{32,48},{48,32},{64,80},{80,64},{96,112},{112,96},{1... | collective-permute-start | bytes 405512 | tf_op jit(solution)/shard_map/ppermute | solution.py:440

commit v3 on v2

--- a/solution.py
+++ b/solution.py
@@ -18,35 +18,38 @@
 F32 = jnp.float32
 HIGHEST = lax.Precision.HIGHEST
 
-COMPS = 14
-LOW = [
-    (c, x)
-    for c in range(COMPS)
-    for x in range(CX - HALO + (c in (3, 6, 7, 11)), CX)
-]
-HIGH = [(c, x) for c in range(COMPS) for x in range(HALO - (c not in (1, 2, 9, 10)))]
+LOW = [(c, x) for c in range(8) for x in range(CX - HALO + (c in (3, 6, 7)), CX)]
+HIGH = [(c, x) for c in range(8) for x in range(HALO - (c not in (1, 2)))]
+ADJ_LOW = [(c, x) for c, x in LOW if c < 6]
+ADJ_HIGH = [(c, x) for c, x in HIGH if c < 6]
 VMEM = pl.BlockSpec(memory_space=pltpu.VMEM)
 SMEM = pl.BlockSpec(memory_space=pltpu.SMEM)
+HBM = pl.BlockSpec(memory_space=pltpu.HBM)
 
 
 def shape(*dims):
     return jax.ShapeDtypeStruct(dims, F32)
 
 
+def in_hbm(array):
+    return pltpu.with_memory_space_constraint(array, pltpu.HBM)
+
+
 def params():
     return pltpu.CompilerParams(vmem_limit_bytes=8 * 1024 * 1024)
 
 
 def plane_of(refs, comp, x):
-    fwd, cond_h, cond_v, adj = refs
-    if comp < 6:
-        return fwd[0, comp, x]
-    return adj[0, comp - 8, x] if comp > 7 else (cond_h, cond_v)[comp - 6][x]
+    return refs[0][0, comp, x] if comp < 6 else refs[comp - 5][x]
+
+
+def edge_of(plane, second):
+    return jnp.where(second, plane[0:HALO], plane[CY - HALO : CY])
 
 
 def pack_kernel(fwd, cond_h, cond_v, adj, *refs):
-    to_next, to_prev, to_side, side_next, side_prev = refs[:5]
-    bufs, sem = refs[5:9], refs[9]
+    to_next, to_prev, to_side, side_next, side_prev, adj_next, adj_prev = refs[:7]
+    bufs, sem = refs[7:11], refs[11]
     copies = [
         pltpu.make_async_copy(src, dst, sem.at[k])
         for k, (src, dst) in enumerate(zip((fwd, cond_h, cond_v, adj), bufs))
@@ -54,14 +57,10 @@
     for copy in copies:
         copy.start()
     second = lax.axis_index("gy") == 1
-
-    def edge(plane):
-        return jnp.where(second, plane[0:HALO], plane[CY - HALO : CY])
-
-    for which, comps in ((0, range(6)), (1, (6,)), (2, (7,)), (3, range(8, COMPS))):
+    for which, comps in ((0, range(6)), (1, (6,)), (2, (7,))):
         copies[which].wait()
         for c in comps:
-            edges = [edge(plane_of(bufs, c, x)) for x in range(CX)]
+            edges = [edge_of(plane_of(bufs, c, x), second) for x in range(CX)]
             for x in range(CX):
                 to_side[c, x] = edges[x]
             for k, (comp, x) in enumerate(LOW):
@@ -72,6 +71,11 @@
                 if comp == c:
                     to_prev[k] = plane_of(bufs, c, x)
                     side_prev[k] = edges[x]
+    copies[3].wait()
+    for k, (c, x) in enumerate(ADJ_LOW):
+        adj_next[k] = bufs[3][0, c, x]
+    for k, (c, x) in enumerate(ADJ_HIGH):
+        adj_prev[k] = bufs[3][0, c, x]
 
 
 def pack(*arrays):
@@ -80,39 +84,53 @@
         out_shape=[
             shape(len(LOW), CY, NZ),
             shape(len(HIGH), CY, NZ),
-            shape(COMPS, CX, HALO, NZ),
+            shape(8, CX, HALO, NZ),
             shape(len(LOW), HALO, NZ),
             shape(len(HIGH), HALO, NZ),
+            shape(len(ADJ_LOW), CY, NZ),
+            shape(len(ADJ_HIGH), CY, NZ),
         ],
-        in_specs=[pl.BlockSpec(memory_space=pltpu.HBM)] * 4,
-        out_specs=[VMEM] * 5,
+        in_specs=[HBM] * 4,
+        out_specs=[VMEM] * 7,
         scratch_shapes=[pltpu.VMEM(a.shape, F32) for a in arrays]
         + [pltpu.SemaphoreType.DMA((4,))],
         compiler_params=params(),
         name="pack",
-    )(*arrays)
-
-
-def exchange(to_next, to_prev, to_side, side_next, side_prev):
+    )(*(in_hbm(a) for a in arrays))
+
+
+def pack_side_kernel(adj, from_prev, from_next, to_side):
+    second = lax.axis_index("gy") == 1
+    for c in range(6):
+        for x in range(CX):
+            to_side[c, HALO + x] = edge_of(adj[0, c, x], second)
+        filled = set(range(HALO, HALO + CX))
+        for k, (comp, x) in enumerate(ADJ_LOW):
+            if comp == c:
+                to_side[c, x - (CX - HALO)] = edge_of(from_prev[k], second)
+                filled.add(x - (CX - HALO))
+        for k, (comp, x) in enumerate(ADJ_HIGH):
+            if comp == c:
+                to_side[c, x + HALO + CX] = edge_of(from_next[k], second)
+                filled.add(x + HALO + CX)
+        for i in range(EX):
+            if i not in filled:
+                to_side[c, i] = jnp.zeros((HALO, NZ), F32)
+
+
+def pairs(dx, swap):
     size_x = lax.axis_size("gx")
     size_y = lax.axis_size("gy")
-
-    def pairs(dx, swap):
-        return [
-            (x * size_y + y, (x + dx) * size_y + (1 - y if swap else y))
-            for x in range(size_x)
-            for y in range(size_y)
-            if 0 <= x + dx < size_x
-        ]
-
-    both = ("gx", "gy")
-    return (
-        lax.ppermute(to_next, both, pairs(1, False)),
-        lax.ppermute(to_prev, both, pairs(-1, False)),
-        lax.ppermute(to_side, both, pairs(0, True)),
-        lax.ppermute(side_next, both, pairs(1, True)),
-        lax.ppermute(side_prev, both, pairs(-1, True)),
-    )
+    return [
+        (x * size_y + y, (x + dx) * size_y + (1 - y if swap else y))
+        for x in range(size_x)
+        for y in range(size_y)
+        if 0 <= x + dx < size_x
+    ]
+
+
+def send(array, dx, swap):
+    return lax.ppermute(array, ("gx", "gy"), pairs(dx, swap))
 
 
 def assemble(own, halos, comps, first):
@@ -241,7 +259,8 @@
 
 def forward_kernel(fwd, cond_h, cond_v, *refs):
     halos, refs = refs[:5], refs[5:]
-    observed, rec_vec, rec, coef, stored, spread, block, elec, mag, rows = refs
+    observed, rec_vec, rec, coef_out, stored_out, spread, block = refs[:7]
+    coef, stored, elec, mag, rows, sem = refs[7:]
     gx, gy = lax.axis_index("gx"), lax.axis_index("gy")
     tools = helpers(gy)
     lane, inside = tools[0], tools[1]
@@ -263,9 +282,13 @@
     for k in (1, 3):
         coef[k, EX:EXP] = jnp.zeros((EXP - EX, EY, NZ), F32)
 
+    copies = [pltpu.make_async_copy(coef, coef_out, sem.at[STEPS])]
+    copies[0].start()
     for step in range(STEPS):
         sweep(step, gx, elec, mag, coef, tools)
         stored[step] = elec[:, HALO : HALO + CX, 0:CY]
+        copies.append(pltpu.make_async_copy(stored.at[step], stored_out.at[step], sem.at[step]))
+        copies[-1].start()
 
     for r in range(rec.shape[0]):
         x, y = rec[r] >> 4, rec[r] & 15
@@ -301,17 +324,41 @@
     for t in range(16):
         block[t, 0:8] = edges
         block[t, 8:16] = side
-
-
-def adjoint_kernel(adj, *refs):
-    halos, refs = refs[:5], refs[5:]
-    coef, stored, spread, blocks, foot, owner, keep, send, elec, mag, inject, grad = refs
+    for copy in copies:
+        copy.wait()
+
+
+def adjoint_kernel(adj, from_prev, from_next, from_side, coef_in, stored_in, *refs):
+    spread, blocks, foot, owner, keep, away = refs[:6]
+    coef, stored, elec, mag, inject, grad, sem = refs[6:]
     gx, gy = lax.axis_index("gx"), lax.axis_index("gy")
     tools = helpers(gy)
     lane, inside = tools[0], tools[1]
 
-    comps = {8 + c: (elec, c) if c < 3 else (mag, c - 3) for c in range(6)}
-    assemble(lambda c, x: adj[0, c - 8, x], halos, comps, gy == 0)
+    copies = [
+        pltpu.make_async_copy(adj.at[0, 0:3], elec.at[:, HALO : HALO + CX, 0:CY], sem.at[0]),
+        pltpu.make_async_copy(adj.at[0, 3:6], mag.at[:, HALO : HALO + CX, 0:CY], sem.at[1]),
+        pltpu.make_async_copy(coef_in, coef, sem.at[2]),
+        pltpu.make_async_copy(stored_in, stored, sem.at[3]),
+    ]
+    for copy in copies:
+        copy.start()
+    zero_rows = jnp.zeros((HALO, NZ), F32)
+    zero_plane = jnp.zeros((EY, NZ), F32)
+    targets = [(elec, c) for c in range(3)] + [(mag, c) for c in range(3)]
+    for c, (ref, index) in enumerate(targets):
+        filled = set(range(HALO, HALO + CX))
+        for source, planes, base in (
+            (from_prev, ADJ_LOW, HALO - CX),
+            (from_next, ADJ_HIGH, HALO + CX),
+        ):
+            for k, (comp, x) in enumerate(planes):
+                if comp == c:
+                    ref[index, x + base, 0:CY] = source[k]
+                    filled.add(x + base)
+        for i in range(EXP):
+            if i not in filled:
+                ref[index, i] = zero_plane
 
     row8 = lax.broadcasted_iota(jnp.int32, (8, NZ), 0)
     used = row8 // HALO == gy
@@ -327,6 +374,15 @@
         side = blocks[2 * near + 1 - gy, 8:16]
         inject[k, 16:24] = jnp.where(used & there, side, 0.0)
 
+    first = gy == 0
+    for c, (ref, index) in enumerate(targets):
+        for i in range(EX):
+            rows = from_side[c, i]
+            ref[index, i, CY : CY + HALO] = jnp.where(first, rows, zero_rows)
+            ref[index, i, CY + HALO : EY] = jnp.where(first, zero_rows, rows)
+    for copy in copies:
+        copy.wait()
+
     at_depth = lane == ZREC
 
     for step in range(STEPS):
@@ -367,12 +423,12 @@
         misfit = misfit + blocks[t, 8:16][top : top + 1]
     core = lax.axis_index("tx") & 1
     for z in range(8):
-        for ref, mine in ((keep, core), (send, 1 - core)):
+        for ref, mine in ((keep, core), (away, 1 - core)):
             row = owner[2 * z + mine]
             ref[32 * z : 32 * z + 16] = grad[0, row] * flag
             ref[32 * z + 16 : 32 * z + 32] = grad[1, row] * flag
     keep[256:264] = jnp.broadcast_to(misfit, (8, NZ))
-    send[256:264] = jnp.broadcast_to(misfit, (8, NZ))
+    away[256:264] = jnp.broadcast_to(misfit, (8, NZ))
 
 
 def pair_kernel(mine, other, out):
@@ -392,52 +448,79 @@
 
 
 def on_device(cond_h, cond_v, fwd_init, adj_init, observed, footprint, owner, rec_cells):
-    halos = exchange(*pack(fwd_init, cond_h, cond_v, adj_init))
+    packed = pack(fwd_init, cond_h, cond_v, adj_init)
+    to_next, to_prev, to_side, side_next, side_prev, adj_next, adj_prev = packed
+    halos = (
+        send(to_next, 1, False),
+        send(to_prev, -1, False),
+        send(to_side, 0, True),
+        send(side_next, 1, True),
+        send(side_prev, -1, True),
+    )
+    adj_halos = (send(adj_next, 1, False), send(adj_prev, -1, False))
     rec = rec_cells.reshape(32)
     coef, stored, spread, block = pl.pallas_call(
         forward_kernel,
         out_shape=[
-            shape(4, EXP, EY, NZ),
-            shape(STEPS, 3, CX, CY, NZ),
+            pltpu.HBM((4, EXP, EY, NZ), F32),
+            pltpu.HBM((STEPS, 3, CX, CY, NZ), F32),
             shape(CY, NZ),
             shape(16, 16, NZ),
         ],
         in_specs=[VMEM] * 10 + [SMEM],
-        out_specs=[VMEM] * 4,
+        out_specs=[HBM, HBM, VMEM, VMEM],
         scratch_shapes=[
+            pltpu.VMEM((4, EXP, EY, NZ), F32),
+            pltpu.VMEM((STEPS, 3, CX, CY, NZ), F32),
             pltpu.VMEM((3, EXP, EY, NZ), F32),
             pltpu.VMEM((3, EXP, EY, NZ), F32),
             pltpu.VMEM((256, NZ), F32),
+            pltpu.SemaphoreType.DMA((STEPS + 1,)),
         ],
         compiler_params=params(),
         name="forward",
     )(fwd_init, cond_h, cond_v, *halos, observed.reshape(8, 32), rec.reshape(1, 32), rec)
+    block, *adj_ready = lax.optimization_barrier((block, *adj_halos))
+    adj_side = pl.pallas_call(
+        pack_side_kernel,
+        out_shape=shape(6, EX, HALO, NZ),
+        in_specs=[VMEM] * 3,
+        out_specs=VMEM,
+        compiler_params=params(),
+        name="pack_side",
+    )(adj_init, *adj_ready)
+    block, adj_side = lax.optimization_barrier((block, adj_side))
+    from_side = send(adj_side, 0, True)
     blocks = lax.all_to_all(block, ("gx", "gy"), 0, 0, tiled=True)
-    keep, send = pl.pallas_call(
+    keep, away = pl.pallas_call(
         adjoint_kernel,
         out_shape=[shape(264, NZ)] * 2,
-        in_specs=[VMEM] * 10 + [SMEM, SMEM],
+        in_specs=[HBM] + [VMEM] * 3 + [HBM] * 2 + [VMEM] * 2 + [SMEM, SMEM],
         out_specs=[VMEM] * 2,
         scratch_shapes=[
+            pltpu.VMEM((4, EXP, EY, NZ), F32),
+            pltpu.VMEM((STEPS, 3, CX, CY, NZ), F32),
             pltpu.VMEM((3, EXP, EY, NZ), F32),
             pltpu.VMEM((3, EXP, EY, NZ), F32),
             pltpu.VMEM((3, EY, NZ), F32),
             pltpu.VMEM((2, CX, CY, NZ), F32),
+            pltpu.SemaphoreType.DMA((4,)),
         ],
         compiler_params=params(),
         name="adjoint",
     )(
-        adj_init,
-        *halos,
-        coef,
-        stored,
+        in_hbm(adj_init),
+        *adj_halos,
+        from_side,
+        in_hbm(coef),
+        in_hbm(stored),
         spread,
         blocks,
         footprint.reshape(1),
         owner.reshape(16),
     )
     size = lax.axis_size("tx")
-    other = lax.ppermute(send, "tx", [(t, t ^ 1) for t in range(size)])
+    other = lax.ppermute(away, "tx", [(t, t ^ 1) for t in range(size)])
     paired = pl.pallas_call(
         pair_kernel,
         out_shape=shape(8, 40, NZ),

time: 88.5 us -> 77.6 us (0.88)
  waiting for transfers between devices: 24.5 us -> 11.7 us
  local copies, waits for them, and re-layouts: 9.1 us -> 0.03 us
  starting transfers between devices: 24.4 us -> 31.8 us
  Pallas kernels: 12 us -> 15.7 us
    ppermute x6 -> x9, waiting for transfers between devices: 18.1 us -> 5.26 us  [the longest x8 4.26 us: send(): return lax.ppermute(array, ('gx', 'gy'), pairs(dx, swap))]
    unnamed x30 -> x14, local copies, waits for them, and re-layouts: 9.1 us -> 0.03 us
    ppermute x6 -> x9, starting transfers between devices: 16.2 us -> 24.7 us  [the longest x8 20.7 us: send(): return lax.ppermute(array, ('gx', 'gy'), pairs(dx, swap))]
    pallas_call x1, Pallas kernels: 6.05 us -> 7.93 us  [on_device(): pl.pallas_call(adjoint_kernel, out_shape=[shape(264, NZ)] * 2, in_specs=[...]
    all_to_all x1, starting transfers between devices: 8.27 us -> 7.06 us  [on_device(): blocks = lax.all_to_all(block, ('gx', 'gy'), 0, 0, tiled=True)]
    pallas_call x1, Pallas kernels: 0.63 us -> 1.63 us  [pack(): pl.pallas_call(pack_kernel, out_shape=[shape(len(LOW), CY, NZ), shape(len...]
    pallas_call x1 -> x2, Pallas kernels: 4.67 us -> 5.5 us  [the longest x1 5.43 us: on_device(): pl.pallas_call(forward_kernel, out_shape=[pltpu.HBM((4, EXP, EY, NZ), F32...]
  transfers between devices with their start and end apart: 7 -> 10, of which waited for: 5 -> 3; matrix products, arithmetic and copies ran while one was open for 0% -> 0% of each run, Pallas kernels for 0% -> 7%
where the time goes in v3:
time: 77.6 us; the launch traced here: 77.2 us
  starting transfers between devices  31.8 us (41%)
  blocking collectives  16.6 us (21%)
  Pallas kernels  15.7 us (20%)
  waiting for transfers between devices  11.7 us (15%)
  between operations  1.51 us (2%)
    ppermute x8, starting transfers between devices, send(): return lax.ppermute(array, ('gx', 'gy'), pairs(dx, swap))  20.7 us
    all_to_all x1, blocking collectives, on_device(): lax.all_to_all(paired, 'tx', 0, 0, axis_index_groups=along_z, tiled=True)  16.6 us
    pallas_call x1, Pallas kernels, on_device(): pl.pallas_call(adjoint_kernel, out_shape=[shape(264, NZ)] * 2, in_specs=[...  7.93 us
    all_to_all x1, starting transfers between devices, on_device(): blocks = lax.all_to_all(block, ('gx', 'gy'), 0, 0, tiled=True)  7.06 us
    all_to_all x1, waiting for transfers between devices, on_device(): blocks = lax.all_to_all(block, ('gx', 'gy'), 0, 0, tiled=True)  6.4 us
    pallas_call x1, Pallas kernels, on_device(): pl.pallas_call(forward_kernel, out_shape=[pltpu.HBM((4, EXP, EY, NZ), F32...  5.43 us
    ppermute x8, waiting for transfers between devices, send(): return lax.ppermute(array, ('gx', 'gy'), pairs(dx, swap))  4.26 us
    ppermute x1, starting transfers between devices, on_device(): other = lax.ppermute(away, 'tx', [(t, t ^ 1) for t in range(size)])  4.04 us
  transfers between devices with their start and end apart: 10, of which 3 were waited for; matrix products, arithmetic and copies ran while one was open for 0% of the time, Pallas kernels for 7%

profile of v3, /device:TPU:1, one launch (start us, length us, event | category | flops | bytes accessed | tf_op | source)
XLA Modules:
  0.0 77.2 jit_solution(17634536542867818096)
XLA Ops:
  0.6 0.0 copy-start
  0.7 1.6 %pack.1 = (f32[29,16,128]{2,1,0:T(8,128)S(1)}, f32[26,16,128]{2,1,0:T(8,128)S(1)}, f32[8,16,4,128]{3,2,1,0:T(4,128)S(1)}, f32[29,4,128]{2,1,0:T(4,128)S(1)}, f32...) custom-call(f32[1,6,16,16,128]{4,3,2,1,0:T(8,128)} %fwd.3, f32[16,16,128]{2,1,0:T(8,128)} %cond_h.3, ...), custom_call_target="tpu_custom_call" | custom-call | tf_op jit(solution)/shard_map/pack/pallas_call | solution.py:82
  2.3 3.8 %collective-permute-start.4 = (f32[8,16,4,128]{3,2,1,0:T(4,128)S(1)}, f32[8,16,4,128]{3,2,1,0:T(4,128)S(1)}, u32[]{:S(2)}, u32[]{:S(2)}) collective-permute-start(f32[8,16,4,128]{3,2,1,0:T(4,128)S(1)} %get-tuple-element.26), channel_id=1, source_target_pairs={{0,1},{1,0},{2,3},{3,2},{4,5},{5,4},{6,7},{7,6},{8,9},{9,8},{10,11... | collective-permute-start | bytes 786440 | tf_op jit(solution)/shard_map/ppermute | solution.py:133
  6.2 1.3 %collective-permute-start.6 = (f32[26,4,128]{2,1,0:T(4,128)S(1)}, f32[26,4,128]{2,1,0:T(4,128)S(1)}, u32[]{:S(2)}, u32[]{:S(2)}) collective-permute-start(f32[26,4,128]{2,1,0:T(4,128)S(1)} %get-tuple-element.28), channel_id=1, source_target_pairs={{2,1},{3,0},{4,3},{5,2},{6,5},{7,4},{8,7},{9,6},{10,9},{11,8},{12,... | collective-permute-start | bytes 159752 | tf_op jit(solution)/shard_map/ppermute | solution.py:133
  7.5 2.9 %collective-permute-start.2 = (f32[29,16,128]{2,1,0:T(8,128)S(1)}, f32[29,16,128]{2,1,0:T(8,128)S(1)}, u32[]{:S(2)}, u32[]{:S(2)}) collective-permute-start(f32[29,16,128]{2,1,0:T(8,128)S(1)} %get-tuple-element.24), channel_id=1, source_target_pairs={{0,2},{1,3},{2,4},{3,5},{4,6},{5,7},{6,8},{7,9},{8,10},{9,11},{10,... | collective-permute-start | bytes 712712 | tf_op jit(solution)/shard_map/ppermute | solution.py:133
  10.4 4.9 %collective-permute-start.5 = (f32[29,4,128]{2,1,0:T(4,128)S(1)}, f32[29,4,128]{2,1,0:T(4,128)S(1)}, u32[]{:S(2)}, u32[]{:S(2)}) collective-permute-start(f32[29,4,128]{2,1,0:T(4,128)S(1)} %get-tuple-element.27), channel_id=1, source_target_pairs={{0,3},{1,2},{2,5},{3,4},{4,7},{5,6},{6,9},{7,8},{8,11},{9,10},{10,... | collective-permute-start | bytes 178184 | tf_op jit(solution)/shard_map/ppermute | solution.py:133
  15.3 1.3 %collective-permute-start.3 = (f32[26,16,128]{2,1,0:T(8,128)S(1)}, f32[26,16,128]{2,1,0:T(8,128)S(1)}, u32[]{:S(2)}, u32[]{:S(2)}) collective-permute-start(f32[26,16,128]{2,1,0:T(8,128)S(1)} %get-tuple-element.25), channel_id=1, source_target_pairs={{2,0},{3,1},{4,2},{5,3},{6,4},{7,5},{8,6},{9,7},{10,8},{11,9},{12,... | collective-permute-start | bytes 638984 | tf_op jit(solution)/shard_map/ppermute | solution.py:133
  16.6 0.0 collective-permute-done.6.refs_4_
  16.6 4.0 %collective-permute-start = (f32[23,16,128]{2,1,0:T(8,128)S(1)}, f32[23,16,128]{2,1,0:T(8,128)S(1)}, u32[]{:S(2)}, u32[]{:S(2)}) collective-permute-start(f32[23,16,128]{2,1,0:T(8,128)S(1)} %get-tuple-element.22), channel_id=1, source_target_pairs={{0,2},{1,3},{2,4},{3,5},{4,6},{5,7},{6,8},{7,9},{8,10},{9,11},{10,... | collective-permute-start | bytes 565256 | tf_op jit(solution)/shard_map/ppermute | solution.py:133
  20.6 1.3 %collective-permute-start.1 = (f32[20,16,128]{2,1,0:T(8,128)S(1)}, f32[20,16,128]{2,1,0:T(8,128)S(1)}, u32[]{:S(2)}, u32[]{:S(2)}) collective-permute-start(f32[20,16,128]{2,1,0:T(8,128)S(1)} %get-tuple-element.23), channel_id=1, source_target_pairs={{2,0},{3,1},{4,2},{5,3},{6,4},{7,5},{8,6},{9,7},{10,8},{11,9},{12,... | collective-permute-start | bytes 491528 | tf_op jit(solution)/shard_map/ppermute | solution.py:133
  21.9 0.0 collective-permute-done.3.refs_1_
  22.0 0.0 copy-start.6
  22.0 5.4 %forward.1 = (f32[4,28,24,128]{3,2,1,0:T(8,128)}, f32[4,3,16,16,128]{4,3,2,1,0:T(8,128)}, f32[16,128]{1,0:T(8,128)S(1)}, f32[16,16,128]{2,1,0:T(8,128)}) custom-call(f32[1,6,16,16,128]{4,3,2,1,0:T(8,128)S(1)} %copy-done.1, f32[16,16,128]{2,1,0:T(8,128)S(1)} %copy-done.2, f32[16,16,128]{2,1,0:T(8,128)S(1)} %copy-done.3, ...), custom_call_target="tpu_custom_call" | custom-call | tf_op jit(solution)/shard_map/forward/pallas_call | solution.py:462
  27.4 0.0 collective-permute-done.1.from_next
  27.4 4.2 %collective-permute-done.from_prev = f32[23,16,128]{2,1,0:T(8,128)S(1)} collective-permute-done((f32[23,16,128]{2,1,0:T(8,128)S(1)}, f32[23,16,128]{2,1,0:T(8,128)S(1)}, u32[]{:S(2)}, u32[]{:S(2)}) %collective-permute-start) | collective-permute-done | bytes 188448 | tf_op jit(solution)/shard_map/ppermute | solution.py:133
  31.7 0.1 pack_side.1
  31.8 1.2 %collective-permute-start.7 = (f32[6,24,4,128]{3,2,1,0:T(4,128)S(1)}, f32[6,24,4,128]{3,2,1,0:T(4,128)S(1)}, u32[]{:S(2)}, u32[]{:S(2)}) collective-permute-start(f32[6,24,4,128]{3,2,1,0:T(4,128)S(1)} %pack_side.1), channel_id=1, source_target_pairs={{0,1},{1,0},{2,3},{3,2},{4,5},{5,4},{6,7},{7,6},{8,9},{9,8},{10,11... | collective-permute-start | bytes 884744 | tf_op jit(solution)/shard_map/ppermute | solution.py:133
  32.9 7.1 %all-to-all-start = ((f32[16,16,128]{2,1,0:T(8,128)}), f32[16,16,128]{2,1,0:T(8,128)S(1)}, u32[]{:S(2)}, u32[]{:S(2)}) async-start(f32[16,16,128]{2,1,0:T(8,128)} %get-tuple-element.37), calls=%async_computation | async-start | bytes 262144 | tf_op jit(solution)/shard_map/all_to_all | solution.py:494
  40.6 6.4 %all-to-all-done.refs_1_ = f32[16,16,128]{2,1,0:T(8,128)S(1)} async-done(((f32[16,16,128]{2,1,0:T(8,128)}), f32[16,16,128]{2,1,0:T(8,128)S(1)}, u32[]{:S(2)}, u32[]{:S(2)}) %all-to-all-start) | async-done | bytes 131104 | tf_op jit(solution)/shard_map/all_to_all | solution.py:494
  47.0 7.9 %adjoint.1 = (f32[264,128]{1,0:T(8,128)S(1)}, f32[264,128]{1,0:T(8,128)S(1)}) custom-call(f32[1,6,16,16,128]{4,3,2,1,0:T(8,128)} %adj.5, f32[23,16,128]{2,1,0:T(8,128)S(1)} %collective-permute-done.from_prev, f32[20,16,128]{2,1,0:T(8,128)S(1)} %collective-permute-done.1.from_next, f32[6,24,4,128]{3,2,1,0:T(4,128)S(1)} %collective-permute-done.7.from_side, ...), custom_call_target="tpu_custom_call" | custom-call | tf_op jit(solution)/shard_map/adjoint/pallas_call | solution.py:495
  55.0 4.0 %collective-permute-start.8 = (f32[264,128]{1,0:T(8,128)S(1)}, f32[264,128]{1,0:T(8,128)S(1)}, u32[]{:S(2)}, u32[]{:S(2)}) collective-permute-start(f32[264,128]{1,0:T(8,128)S(1)} %get-tuple-element.39), channel_id=1, source_target_pairs={{0,16},{16,0},{32,48},{48,32},{64,80},{80,64},{96,112},{112,96},{1... | collective-permute-start | bytes 405512 | tf_op jit(solution)/shard_map/ppermute | solution.py:523
  59.0 1.0 %collective-permute-done.8.other = f32[264,128]{1,0:T(8,128)S(1)} collective-permute-done((f32[264,128]{1,0:T(8,128)S(1)}, f32[264,128]{1,0:T(8,128)S(1)}, u32[]{:S(2)}, u32[]{:S(2)}) %collective-permute-start.8) | collective-permute-done | bytes 135200 | tf_op jit(solution)/shard_map/ppermute | solution.py:523
  60.0 16.6 %all_to_all.10.blocks = f32[8,40,128]{2,1,0:T(8,128)S(1)} all-to-all(f32[8,40,128]{2,1,0:T(8,128)S(1)} %pair.1), channel_id=1, replica_groups={{0,32,64,96,128,160,192,224},{16,48,80,112,144,176,208,240},{1,33,65,97..., dimensions={0} | all-to-all | bytes 327680 | tf_op jit(solution)/shard_map/all_to_all | solution.py:533
  76.6 0.6 total.1
  (17 shorter events, 0.1 us)
Async XLA Ops:
  0.6 31.1 %copy-start = (f32[1,6,16,16,128]{4,3,2,1,0:T(8,128)S(1)}, f32[1,6,16,16,128]{4,3,2,1,0:T(8,128)}, u32[]{:S(2)}) copy-start(f32[1,6,16,16,128]{4,3,2,1,0:T(8,128)} %adj.5) | copy-start | bytes 2359300
  0.6 21.3 %copy-start.1 = (f32[1,6,16,16,128]{4,3,2,1,0:T(8,128)S(1)}, f32[1,6,16,16,128]{4,3,2,1,0:T(8,128)}, u32[]{:S(2)}) copy-start(f32[1,6,16,16,128]{4,3,2,1,0:T(8,128)} %fwd.3) | copy-start | bytes 2359300
  0.7 21.3 %copy-start.2 = (f32[16,16,128]{2,1,0:T(8,128)S(1)}, f32[16,16,128]{2,1,0:T(8,128)}, u32[]{:S(2)}) copy-start(f32[16,16,128]{2,1,0:T(8,128)} %cond_h.3) | copy-start | bytes 393220
  0.7 21.3 %copy-start.3 = (f32[16,16,128]{2,1,0:T(8,128)S(1)}, f32[16,16,128]{2,1,0:T(8,128)}, u32[]{:S(2)}) copy-start(f32[16,16,128]{2,1,0:T(8,128)} %cond_v.3) | copy-start | bytes 393220
  0.7 21.3 %copy-start.4 = (f32[1,4,1,1,2,32]{5,4,3,2,1,0:T(2,128)S(1)}, f32[1,4,1,1,2,32]{5,4,3,2,1,0:T(2,128)}, u32[]{:S(2)}) copy-start(f32[1,4,1,1,2,32]{5,4,3,2,1,0:T(2,128)} %param.12) | copy-start | bytes 3076
  0.7 21.3 %copy-start.5 = (s32[1,1,32]{2,1,0:T(1,128)S(1)}, s32[1,1,32]{2,1,0:T(1,128)}, u32[]{:S(2)}) copy-start(s32[1,1,32]{2,1,0:T(1,128)} %param.15) | copy-start | bytes 388
  2.3 19.6 %collective-permute-start.4 = (f32[8,16,4,128]{3,2,1,0:T(4,128)S(1)}, f32[8,16,4,128]{3,2,1,0:T(4,128)S(1)}, u32[]{:S(2)}, u32[]{:S(2)}) collective-permute-start(f32[8,16,4,128]{3,2,1,0:T(4,128)S(1)} %get-tuple-element.26), channel_id=1, source_target_pairs={{0,1},{1,0},{2,3},{3,2},{4,5},{5,4},{6,7},{7,6},{8,9},{9,8},{10,11... | collective-permute-start | bytes 786440 | tf_op jit(solution)/shard_map/ppermute | solution.py:133
  6.2 10.4 %collective-permute-start.6 = (f32[26,4,128]{2,1,0:T(4,128)S(1)}, f32[26,4,128]{2,1,0:T(4,128)S(1)}, u32[]{:S(2)}, u32[]{:S(2)}) collective-permute-start(f32[26,4,128]{2,1,0:T(4,128)S(1)} %get-tuple-element.28), channel_id=1, source_target_pairs={{2,1},{3,0},{4,3},{5,2},{6,5},{7,4},{8,7},{9,6},{10,9},{11,8},{12,... | collective-permute-start | bytes 159752 | tf_op jit(solution)/shard_map/ppermute | solution.py:133
  7.5 14.5 %collective-permute-start.2 = (f32[29,16,128]{2,1,0:T(8,128)S(1)}, f32[29,16,128]{2,1,0:T(8,128)S(1)}, u32[]{:S(2)}, u32[]{:S(2)}) collective-permute-start(f32[29,16,128]{2,1,0:T(8,128)S(1)} %get-tuple-element.24), channel_id=1, source_target_pairs={{0,2},{1,3},{2,4},{3,5},{4,6},{5,7},{6,8},{7,9},{8,10},{9,11},{10,... | collective-permute-start | bytes 712712 | tf_op jit(solution)/shard_map/ppermute | solution.py:133
  10.4 10.2 %collective-permute-start.5 = (f32[29,4,128]{2,1,0:T(4,128)S(1)}, f32[29,4,128]{2,1,0:T(4,128)S(1)}, u32[]{:S(2)}, u32[]{:S(2)}) collective-permute-start(f32[29,4,128]{2,1,0:T(4,128)S(1)} %get-tuple-element.27), channel_id=1, source_target_pairs={{0,3},{1,2},{2,5},{3,4},{4,7},{5,6},{6,9},{7,8},{8,11},{9,10},{10,... | collective-permute-start | bytes 178184 | tf_op jit(solution)/shard_map/ppermute | solution.py:133
  15.3 6.6 %collective-permute-start.3 = (f32[26,16,128]{2,1,0:T(8,128)S(1)}, f32[26,16,128]{2,1,0:T(8,128)S(1)}, u32[]{:S(2)}, u32[]{:S(2)}) collective-permute-start(f32[26,16,128]{2,1,0:T(8,128)S(1)} %get-tuple-element.25), channel_id=1, source_target_pairs={{2,0},{3,1},{4,2},{5,3},{6,4},{7,5},{8,6},{9,7},{10,8},{11,9},{12,... | collective-permute-start | bytes 638984 | tf_op jit(solution)/shard_map/ppermute | solution.py:133
  16.6 15.1 %collective-permute-start = (f32[23,16,128]{2,1,0:T(8,128)S(1)}, f32[23,16,128]{2,1,0:T(8,128)S(1)}, u32[]{:S(2)}, u32[]{:S(2)}) collective-permute-start(f32[23,16,128]{2,1,0:T(8,128)S(1)} %get-tuple-element.22), channel_id=1, source_target_pairs={{0,2},{1,3},{2,4},{3,5},{4,6},{5,7},{6,8},{7,9},{8,10},{9,11},{10,... | collective-permute-start | bytes 565256 | tf_op jit(solution)/shard_map/ppermute | solution.py:133
  20.6 6.8 %collective-permute-start.1 = (f32[20,16,128]{2,1,0:T(8,128)S(1)}, f32[20,16,128]{2,1,0:T(8,128)S(1)}, u32[]{:S(2)}, u32[]{:S(2)}) collective-permute-start(f32[20,16,128]{2,1,0:T(8,128)S(1)} %get-tuple-element.23), channel_id=1, source_target_pairs={{2,0},{3,1},{4,2},{5,3},{6,4},{7,5},{8,6},{9,7},{10,8},{11,9},{12,... | collective-permute-start | bytes 491528 | tf_op jit(solution)/shard_map/ppermute | solution.py:133
  22.0 25.1 %copy-start.6 = (s32[1,1,16]{2,1,0:T(1,128)S(1)}, s32[1,1,16]{2,1,0:T(1,128)}, u32[]{:S(2)}) copy-start(s32[1,1,16]{2,1,0:T(1,128)} %param.14) | copy-start | bytes 196
  31.8 15.3 %collective-permute-start.7 = (f32[6,24,4,128]{3,2,1,0:T(4,128)S(1)}, f32[6,24,4,128]{3,2,1,0:T(4,128)S(1)}, u32[]{:S(2)}, u32[]{:S(2)}) collective-permute-start(f32[6,24,4,128]{3,2,1,0:T(4,128)S(1)} %pack_side.1), channel_id=1, source_target_pairs={{0,1},{1,0},{2,3},{3,2},{4,5},{5,4},{6,7},{7,6},{8,9},{9,8},{10,11... | collective-permute-start | bytes 884744 | tf_op jit(solution)/shard_map/ppermute | solution.py:133
  32.9 14.1 %all-to-all-start = ((f32[16,16,128]{2,1,0:T(8,128)}), f32[16,16,128]{2,1,0:T(8,128)S(1)}, u32[]{:S(2)}, u32[]{:S(2)}) async-start(f32[16,16,128]{2,1,0:T(8,128)} %get-tuple-element.37), calls=%async_computation | async-start | bytes 262144 | tf_op jit(solution)/shard_map/all_to_all | solution.py:494
  55.0 5.0 %collective-permute-start.8 = (f32[264,128]{1,0:T(8,128)S(1)}, f32[264,128]{1,0:T(8,128)S(1)}, u32[]{:S(2)}, u32[]{:S(2)}) collective-permute-start(f32[264,128]{1,0:T(8,128)S(1)} %get-tuple-element.39), channel_id=1, source_target_pairs={{0,16},{16,0},{32,48},{48,32},{64,80},{80,64},{96,112},{112,96},{1... | collective-permute-start | bytes 405512 | tf_op jit(solution)/shard_map/ppermute | solution.py:523

commit v4 on v3

--- a/solution.py
+++ b/solution.py
@@ -190,15 +190,16 @@
     return (x >= 0) & (x < 8 * CX)
 
 
-MODE = "fused"
-UNROLL = 8
+UNROLL = 24
 
 
 def sweep(step, gx, elec, mag, coef, tools):
     _, inside, z_up, z_down, y_up, y_down = tools
     half = jnp.where(inside, STEP_DT, 0.0)
     zero = jnp.zeros((EY, NZ), F32)
-    turns = -(-(EX - 1 - 2 * step) // UNROLL)
+    count = EX - 1 - 2 * step
+    unroll = min(UNROLL, count)
+    turns = -(-count // unroll)
 
     def magnetic(i, field, after):
         ex, ey, ez = field
@@ -226,41 +227,30 @@
             for c in range(3):
                 ref[c, i + k] = plane[c]
 
-    if MODE == "fused":
-
-        def body(turn, carry):
-            i = step + turn * UNROLL
-            field = planes(elec, i, UNROLL + 1)
-            now = [magnetic(i + k, field[k], field[k + 1]) for k in range(UNROLL)]
-            put(mag, i, now)
-            before = [(None, *carry)] + now[:-1]
-            put(elec, i, [electric(i + k, field[k], now[k], before[k]) for k in range(UNROLL)])
-            return now[-1][1:]
-
+    def body(turn, carry):
+        i = step + turn * unroll
+        field = planes(elec, i, unroll + 1)
+        now = [magnetic(i + k, field[k], field[k + 1]) for k in range(unroll)]
+        put(mag, i, now)
+        before = [(None, *carry)] + now[:-1]
+        put(elec, i, [electric(i + k, field[k], now[k], before[k]) for k in range(unroll)])
+        return now[-1][1:]
+
+    if turns == 1:
+        body(0, (zero, zero))
+    else:
         lax.fori_loop(0, turns, body, (zero, zero))
-    else:
-
-        def body_h(turn, carry):
-            i = step + turn * UNROLL
-            field = planes(elec, i, UNROLL + 1)
-            put(mag, i, [magnetic(i + k, field[k], field[k + 1]) for k in range(UNROLL)])
-            return carry
-
-        def body_e(turn, carry):
-            i = step + 1 + turn * UNROLL
-            field = planes(elec, i, UNROLL)
-            now = planes(mag, i - 1, UNROLL + 1)
-            put(elec, i, [electric(i + k, field[k], now[k + 1], now[k]) for k in range(UNROLL)])
-            return carry
-
-        lax.fori_loop(0, turns, body_h, 0)
-        lax.fori_loop(0, -(-(EX - 2 - 2 * step) // UNROLL), body_e, 0)
+
+
+def dot(a, b, dim_a, dim_b):
+    dims = (((dim_a,), (dim_b,)), ((), ()))
+    return lax.dot_general(a, b, dims, precision=HIGHEST, preferred_element_type=F32)
 
 
 def forward_kernel(fwd, cond_h, cond_v, *refs):
     halos, refs = refs[:5], refs[5:]
-    observed, rec_vec, rec, coef_out, stored_out, spread, block = refs[:7]
-    coef, stored, elec, mag, rows, sem = refs[7:]
+    observed, rec_vec, coef_out, stored_out, spread, block = refs[:6]
+    coef, stored, elec, mag, sem = refs[6:]
     gx, gy = lax.axis_index("gx"), lax.axis_index("gy")
     tools = helpers(gy)
     lane, inside = tools[0], tools[1]
@@ -269,19 +259,29 @@
     comps |= {6: (coef, 0), 7: (coef, 2)}
     assemble(lambda c, x: plane_of((fwd, cond_h, cond_v, None), c, x), halos, comps, gy == 0)
 
-    def coefficients(i, carry):
-        keep = inside & in_grid(gx, i)
-        for k in (0, 2):
-            half_rate = 0.25 * coef[k, i]
-            inverse = 1.0 / (1.0 + half_rate)
-            coef[k, i] = jnp.where(keep, (1.0 - half_rate) * inverse, 0.0)
-            coef[k + 1, i] = jnp.where(keep, STEP_DT * inverse, 0.0)
+    def coefficients(turn, carry):
+        for i in [turn * 8 + k for k in range(8)]:
+            keep = inside & in_grid(gx, i)
+            for k in (0, 2):
+                half_rate = 0.25 * coef[k, i]
+                inverse = 1.0 / (1.0 + half_rate)
+                coef[k, i] = jnp.where(keep, (1.0 - half_rate) * inverse, 0.0)
+                coef[k + 1, i] = jnp.where(keep, STEP_DT * inverse, 0.0)
         return carry
 
-    lax.fori_loop(0, EX, coefficients, 0)
+    lax.fori_loop(0, EX // 8, coefficients, 0)
     for k in (1, 3):
         coef[k, EX:EXP] = jnp.zeros((EXP - EX, EY, NZ), F32)
 
+    cells = rec_vec[...]
+    at_y = ((cells & 15) == lax.broadcasted_iota(jnp.int32, (CY, 32), 0)).astype(F32)
+    cell_x = ((cells >> 4) == lax.broadcasted_iota(jnp.int32, (CX, 32), 0)).astype(F32)
+    lane_x = lax.broadcasted_iota(jnp.int32, (CX, NZ), 1) >> 3
+    lane_q = lax.broadcasted_iota(jnp.int32, (8, NZ), 1) & 7
+    at_x = dot(cell_x, (lane_x == lax.broadcasted_iota(jnp.int32, (CX, NZ), 0)).astype(F32), 0, 0)
+    target = dot(
+        observed[...], (lane_q == lax.broadcasted_iota(jnp.int32, (8, NZ), 0)).astype(F32), 0, 0
+    )
     copies = [pltpu.make_async_copy(coef, coef_out, sem.at[STEPS])]
     copies[0].start()
     for step in range(STEPS):
@@ -290,30 +290,18 @@
         copies.append(pltpu.make_async_copy(stored.at[step], stored_out.at[step], sem.at[step]))
         copies[-1].start()
 
-    for r in range(rec.shape[0]):
-        x, y = rec[r] >> 4, rec[r] & 15
-        for step in range(STEPS):
-            for c in range(2):
-                rows[pl.ds((2 * step + c) * 32 + r, 1), :] = stored[step, c, x, pl.ds(y, 1), :]
-    pick = (lax.broadcasted_iota(jnp.int32, (8, NZ), 1) == ZREC).astype(F32)
-    picked = lax.dot_general(
-        pick, rows[...], (((1,), (1,)), ((), ())), precision=HIGHEST, preferred_element_type=F32
-    )
+    at_depth = lane[0:CY] == ZREC
+    record = jnp.zeros((CY, NZ), F32)
+    for x in range(CX):
+        for q in range(8):
+            column = jnp.where(at_depth, stored[q // 2, q % 2, x], 0.0)
+            record = record + pltpu.roll(column, (x * 8 + q - ZREC) % NZ, 1)
+    at_receivers = dot(at_y, record, 0, 0)
+    residual = at_x * (at_receivers - target)
+    misfit = 0.5 * jnp.sum(residual * residual)
+    spread_now = dot(at_y, residual, 1, 0)
     lane8 = lax.broadcasted_iota(jnp.int32, (8, NZ), 1)
     row8 = lax.broadcasted_iota(jnp.int32, (8, NZ), 0)
-    own = jnp.where(lane8 // 32 == row8, picked[:, 0:NZ], 0.0)
-    own = own + jnp.where(lane8 // 32 + 4 == row8, picked[:, NZ : 2 * NZ], 0.0)
-    own = own + pltpu.roll(own, 64, 1)
-    own = own + pltpu.roll(own, 32, 1)
-    residual = own[:, 0:32] - observed[...]
-    misfit = 0.5 * jnp.sum(residual * residual)
-    cells = rec_vec[...]
-    at_y = ((cells & 15) == lax.broadcasted_iota(jnp.int32, (CY, 32), 0)).astype(F32)
-    at_x = (cells >> 4) == lax.broadcasted_iota(jnp.int32, (NZ, 32), 0) // 8
-    weighted = jnp.where(at_x, jnp.tile(residual, (16, 1)), 0.0)
-    spread_now = lax.dot_general(
-        at_y, weighted, (((1,), (1,)), ((), ())), precision=HIGHEST, preferred_element_type=F32
-    )
     spread[...] = spread_now
     low_rows, high_rows = spread_now[0:8], spread_now[8:16]
     edges = jnp.where((lane8 < 32) | (lane8 >= 96), low_rows, pltpu.roll(high_rows, 64, 1))
@@ -339,7 +327,9 @@
         pltpu.make_async_copy(adj.at[0, 0:3], elec.at[:, HALO : HALO + CX, 0:CY], sem.at[0]),
         pltpu.make_async_copy(adj.at[0, 3:6], mag.at[:, HALO : HALO + CX, 0:CY], sem.at[1]),
         pltpu.make_async_copy(coef_in, coef, sem.at[2]),
-        pltpu.make_async_copy(stored_in, stored, sem.at[3]),
+    ] + [
+        pltpu.make_async_copy(stored_in.at[k], stored.at[k], sem.at[3 + k])
+        for k in reversed(range(STEPS))
     ]
     for copy in copies:
         copy.start()
@@ -380,7 +370,7 @@
             rows = from_side[c, i]
             ref[index, i, CY : CY + HALO] = jnp.where(first, rows, zero_rows)
             ref[index, i, CY + HALO : EY] = jnp.where(first, zero_rows, rows)
-    for copy in copies:
+    for copy in copies[:3]:
         copy.wait()
 
     at_depth = lane == ZREC
@@ -388,22 +378,16 @@
     for step in range(STEPS):
         when = STEPS - 1 - step
 
-        def add(turn, carry, when=when):
-            for k in range(4):
-                i = turn * 4 + k
-                tile = jnp.where(turn == 0, 0, jnp.where(turn < 5, 1, 2))
-                x = (i + CX - HALO) & (CX - 1)
-                source = inject[tile]
-                shift = (ZREC + NZ - (x * 8 + 2 * when)) & (NZ - 1)
-                for c in range(2):
-                    moved = pltpu.roll(source, (shift - c) & (NZ - 1), 1)
-                    elec[c, i] += jnp.where(at_depth, moved, 0.0)
-            return carry
-
-        lax.fori_loop(0, EX // 4, add, 0)
+        for i in range(step, EX - step):
+            source = inject[0 if i < HALO else 1 if i < HALO + CX else 2]
+            x = (i - HALO) % CX
+            for c in range(2):
+                moved = pltpu.roll(source, (ZREC - (x * 8 + 2 * when + c)) % NZ, 1)
+                elec[c, i] += jnp.where(at_depth, moved, 0.0)
         sweep(step, gx, elec, mag, coef, tools)
 
-        def accumulate(x, carry, when=when, step=step):
+        copies[3 + step].wait()
+        for x in range(CX):
             ax, ay, az = (elec[c, HALO + x, 0:CY] for c in range(3))
             horizontal = ax * stored[when, 0, x] + ay * stored[when, 1, x]
             vertical = az * stored[when, 2, x]
@@ -412,9 +396,6 @@
                 vertical = grad[1, x] + vertical
             grad[0, x] = horizontal
             grad[1, x] = vertical
-            return carry
-
-        lax.fori_loop(0, CX, accumulate, 0)
 
     flag = foot[0].astype(F32)
     misfit = blocks[0, 8:16][0:1]
@@ -458,7 +439,6 @@
         send(side_prev, -1, True),
     )
     adj_halos = (send(adj_next, 1, False), send(adj_prev, -1, False))
-    rec = rec_cells.reshape(32)
     coef, stored, spread, block = pl.pallas_call(
         forward_kernel,
         out_shape=[
@@ -467,19 +447,18 @@
             shape(CY, NZ),
             shape(16, 16, NZ),
         ],
-        in_specs=[VMEM] * 10 + [SMEM],
+        in_specs=[VMEM] * 10,
         out_specs=[HBM, HBM, VMEM, VMEM],
         scratch_shapes=[
             pltpu.VMEM((4, EXP, EY, NZ), F32),
             pltpu.VMEM((STEPS, 3, CX, CY, NZ), F32),
             pltpu.VMEM((3, EXP, EY, NZ), F32),
             pltpu.VMEM((3, EXP, EY, NZ), F32),
-            pltpu.VMEM((256, NZ), F32),
             pltpu.SemaphoreType.DMA((STEPS + 1,)),
         ],
         compiler_params=params(),
         name="forward",
-    )(fwd_init, cond_h, cond_v, *halos, observed.reshape(8, 32), rec.reshape(1, 32), rec)
+    )(fwd_init, cond_h, cond_v, *halos, observed.reshape(8, 32), rec_cells.reshape(1, 32))
     block, *adj_ready = lax.optimization_barrier((block, *adj_halos))
     adj_side = pl.pallas_call(
         pack_side_kernel,
@@ -504,7 +483,7 @@
             pltpu.VMEM((3, EXP, EY, NZ), F32),
             pltpu.VMEM((3, EY, NZ), F32),
             pltpu.VMEM((2, CX, CY, NZ), F32),
-            pltpu.SemaphoreType.DMA((4,)),
+            pltpu.SemaphoreType.DMA((3 + STEPS,)),
         ],
         compiler_params=params(),
         name="adjoint",

time: 77.6 us -> 72.5 us (0.934)
  Pallas kernels: 15.7 us -> 10.5 us
  starting transfers between devices: 31.8 us -> 29.9 us
  waiting for transfers between devices: 11.7 us -> 13.5 us
    pallas_call x1, Pallas kernels: 7.93 us -> 4.53 us  [on_device(): pl.pallas_call(adjoint_kernel, out_shape=[shape(264, NZ)] * 2, in_specs=[...]
    ppermute x1, starting transfers between devices: 4.04 us -> 2.21 us  [on_device(): other = lax.ppermute(away, 'tx', [(t, t ^ 1) for t in range(size)])]
    ppermute x8, waiting for transfers between devices: 4.26 us -> 6.04 us  [send(): return lax.ppermute(array, ('gx', 'gy'), pairs(dx, swap))]
    pallas_call x1, Pallas kernels: 5.43 us -> 3.67 us  [on_device(): pl.pallas_call(forward_kernel, out_shape=[pltpu.HBM((4, EXP, EY, NZ), F32...]
  transfers between devices with their start and end apart: 10 -> 10, of which waited for: 3 -> 4; matrix products, arithmetic and copies ran while one was open for 0% -> 0% of each run, Pallas kernels for 7% -> 5%
where the time goes in v4:
time: 72.5 us; the launch traced here: 72.1 us
  starting transfers between devices  29.9 us (41%)
  blocking collectives  16.6 us (23%)
  waiting for transfers between devices  13.5 us (19%)
  Pallas kernels  10.5 us (14%)
  between operations  1.5 us (2%)
    ppermute x8, starting transfers between devices, send(): return lax.ppermute(array, ('gx', 'gy'), pairs(dx, swap))  20.7 us
    all_to_all x1, blocking collectives, on_device(): lax.all_to_all(paired, 'tx', 0, 0, axis_index_groups=along_z, tiled=True)  16.6 us
    all_to_all x1, starting transfers between devices, on_device(): blocks = lax.all_to_all(block, ('gx', 'gy'), 0, 0, tiled=True)  7.06 us
    all_to_all x1, waiting for transfers between devices, on_device(): blocks = lax.all_to_all(block, ('gx', 'gy'), 0, 0, tiled=True)  6.47 us
    ppermute x8, waiting for transfers between devices, send(): return lax.ppermute(array, ('gx', 'gy'), pairs(dx, swap))  6.04 us
    pallas_call x1, Pallas kernels, on_device(): pl.pallas_call(adjoint_kernel, out_shape=[shape(264, NZ)] * 2, in_specs=[...  4.53 us
    pallas_call x1, Pallas kernels, on_device(): pl.pallas_call(forward_kernel, out_shape=[pltpu.HBM((4, EXP, EY, NZ), F32...  3.67 us
    ppermute x1, starting transfers between devices, on_device(): other = lax.ppermute(away, 'tx', [(t, t ^ 1) for t in range(size)])  2.21 us
  transfers between devices with their start and end apart: 10, of which 4 were waited for; matrix products, arithmetic and copies ran while one was open for 0% of the time, Pallas kernels for 5%

profile of v4, /device:TPU:1, one launch (start us, length us, event | category | flops | bytes accessed | tf_op | source)
XLA Modules:
  0.0 72.1 jit_solution(8334957595123213569)
XLA Ops:
  0.6 0.0 copy-start
  0.7 1.6 %pack.1 = (f32[29,16,128]{2,1,0:T(8,128)S(1)}, f32[26,16,128]{2,1,0:T(8,128)S(1)}, f32[8,16,4,128]{3,2,1,0:T(4,128)S(1)}, f32[29,4,128]{2,1,0:T(4,128)S(1)}, f32...) custom-call(f32[1,6,16,16,128]{4,3,2,1,0:T(8,128)} %fwd.3, f32[16,16,128]{2,1,0:T(8,128)} %cond_h.3, ...), custom_call_target="tpu_custom_call" | custom-call | tf_op jit(solution)/shard_map/pack/pallas_call | solution.py:82
  2.3 3.8 %collective-permute-start.4 = (f32[8,16,4,128]{3,2,1,0:T(4,128)S(1)}, f32[8,16,4,128]{3,2,1,0:T(4,128)S(1)}, u32[]{:S(2)}, u32[]{:S(2)}) collective-permute-start(f32[8,16,4,128]{3,2,1,0:T(4,128)S(1)} %get-tuple-element.26), channel_id=1, source_target_pairs={{0,1},{1,0},{2,3},{3,2},{4,5},{5,4},{6,7},{7,6},{8,9},{9,8},{10,11... | collective-permute-start | bytes 786440 | tf_op jit(solution)/shard_map/ppermute | solution.py:133
  6.2 1.3 %collective-permute-start.6 = (f32[26,4,128]{2,1,0:T(4,128)S(1)}, f32[26,4,128]{2,1,0:T(4,128)S(1)}, u32[]{:S(2)}, u32[]{:S(2)}) collective-permute-start(f32[26,4,128]{2,1,0:T(4,128)S(1)} %get-tuple-element.28), channel_id=1, source_target_pairs={{2,1},{3,0},{4,3},{5,2},{6,5},{7,4},{8,7},{9,6},{10,9},{11,8},{12,... | collective-permute-start | bytes 159752 | tf_op jit(solution)/shard_map/ppermute | solution.py:133
  7.5 2.9 %collective-permute-start.2 = (f32[29,16,128]{2,1,0:T(8,128)S(1)}, f32[29,16,128]{2,1,0:T(8,128)S(1)}, u32[]{:S(2)}, u32[]{:S(2)}) collective-permute-start(f32[29,16,128]{2,1,0:T(8,128)S(1)} %get-tuple-element.24), channel_id=1, source_target_pairs={{0,2},{1,3},{2,4},{3,5},{4,6},{5,7},{6,8},{7,9},{8,10},{9,11},{10,... | collective-permute-start | bytes 712712 | tf_op jit(solution)/shard_map/ppermute | solution.py:133
  10.4 4.9 %collective-permute-start.5 = (f32[29,4,128]{2,1,0:T(4,128)S(1)}, f32[29,4,128]{2,1,0:T(4,128)S(1)}, u32[]{:S(2)}, u32[]{:S(2)}) collective-permute-start(f32[29,4,128]{2,1,0:T(4,128)S(1)} %get-tuple-element.27), channel_id=1, source_target_pairs={{0,3},{1,2},{2,5},{3,4},{4,7},{5,6},{6,9},{7,8},{8,11},{9,10},{10,... | collective-permute-start | bytes 178184 | tf_op jit(solution)/shard_map/ppermute | solution.py:133
  15.3 1.3 %collective-permute-start.3 = (f32[26,16,128]{2,1,0:T(8,128)S(1)}, f32[26,16,128]{2,1,0:T(8,128)S(1)}, u32[]{:S(2)}, u32[]{:S(2)}) collective-permute-start(f32[26,16,128]{2,1,0:T(8,128)S(1)} %get-tuple-element.25), channel_id=1, source_target_pairs={{2,0},{3,1},{4,2},{5,3},{6,4},{7,5},{8,6},{9,7},{10,8},{11,9},{12,... | collective-permute-start | bytes 638984 | tf_op jit(solution)/shard_map/ppermute | solution.py:133
  16.6 0.0 collective-permute-done.6.refs_4_
  16.6 4.0 %collective-permute-start = (f32[23,16,128]{2,1,0:T(8,128)S(1)}, f32[23,16,128]{2,1,0:T(8,128)S(1)}, u32[]{:S(2)}, u32[]{:S(2)}) collective-permute-start(f32[23,16,128]{2,1,0:T(8,128)S(1)} %get-tuple-element.22), channel_id=1, source_target_pairs={{0,2},{1,3},{2,4},{3,5},{4,6},{5,7},{6,8},{7,9},{8,10},{9,11},{10,... | collective-permute-start | bytes 565256 | tf_op jit(solution)/shard_map/ppermute | solution.py:133
  20.6 1.3 %collective-permute-start.1 = (f32[20,16,128]{2,1,0:T(8,128)S(1)}, f32[20,16,128]{2,1,0:T(8,128)S(1)}, u32[]{:S(2)}, u32[]{:S(2)}) collective-permute-start(f32[20,16,128]{2,1,0:T(8,128)S(1)} %get-tuple-element.23), channel_id=1, source_target_pairs={{2,0},{3,1},{4,2},{5,3},{6,4},{7,5},{8,6},{9,7},{10,8},{11,9},{12,... | collective-permute-start | bytes 491528 | tf_op jit(solution)/shard_map/ppermute | solution.py:133
  21.9 0.0 collective-permute-done.3.refs_1_
  22.0 0.0 copy-start.6
  22.0 3.7 %forward.1 = (f32[4,28,24,128]{3,2,1,0:T(8,128)}, f32[4,3,16,16,128]{4,3,2,1,0:T(8,128)}, f32[16,128]{1,0:T(8,128)S(1)}, f32[16,16,128]{2,1,0:T(8,128)}) custom-call(f32[1,6,16,16,128]{4,3,2,1,0:T(8,128)S(1)} %copy-done.1, f32[16,16,128]{2,1,0:T(8,128)S(1)} %copy-done.2, f32[16,16,128]{2,1,0:T(8,128)S(1)} %copy-done.3, ...), custom_call_target="tpu_custom_call" | custom-call | tf_op jit(solution)/shard_map/forward/pallas_call | solution.py:442
  25.7 1.5 %collective-permute-done.1.from_next = f32[20,16,128]{2,1,0:T(8,128)S(1)} collective-permute-done((f32[20,16,128]{2,1,0:T(8,128)S(1)}, f32[20,16,128]{2,1,0:T(8,128)S(1)}, u32[]{:S(2)}, u32[]{:S(2)}) %collective-permute-start.1) | collective-permute-done | bytes 163872 | tf_op jit(solution)/shard_map/ppermute | solution.py:133
  27.2 4.5 %collective-permute-done.from_prev = f32[23,16,128]{2,1,0:T(8,128)S(1)} collective-permute-done((f32[23,16,128]{2,1,0:T(8,128)S(1)}, f32[23,16,128]{2,1,0:T(8,128)S(1)}, u32[]{:S(2)}, u32[]{:S(2)}) %collective-permute-start) | collective-permute-done | bytes 188448 | tf_op jit(solution)/shard_map/ppermute | solution.py:133
  31.7 0.1 pack_side.1
  31.8 1.2 %collective-permute-start.7 = (f32[6,24,4,128]{3,2,1,0:T(4,128)S(1)}, f32[6,24,4,128]{3,2,1,0:T(4,128)S(1)}, u32[]{:S(2)}, u32[]{:S(2)}) collective-permute-start(f32[6,24,4,128]{3,2,1,0:T(4,128)S(1)} %pack_side.1), channel_id=1, source_target_pairs={{0,1},{1,0},{2,3},{3,2},{4,5},{5,4},{6,7},{7,6},{8,9},{9,8},{10,11... | collective-permute-start | bytes 884744 | tf_op jit(solution)/shard_map/ppermute | solution.py:133
  32.9 7.1 %all-to-all-start = ((f32[16,16,128]{2,1,0:T(8,128)}), f32[16,16,128]{2,1,0:T(8,128)S(1)}, u32[]{:S(2)}, u32[]{:S(2)}) async-start(f32[16,16,128]{2,1,0:T(8,128)} %get-tuple-element.37), calls=%async_computation | async-start | bytes 262144 | tf_op jit(solution)/shard_map/all_to_all | solution.py:473
  40.6 6.5 %all-to-all-done.refs_1_ = f32[16,16,128]{2,1,0:T(8,128)S(1)} async-done(((f32[16,16,128]{2,1,0:T(8,128)}), f32[16,16,128]{2,1,0:T(8,128)S(1)}, u32[]{:S(2)}, u32[]{:S(2)}) %all-to-all-start) | async-done | bytes 131104 | tf_op jit(solution)/shard_map/all_to_all | solution.py:473
  47.1 4.5 %adjoint.1 = (f32[264,128]{1,0:T(8,128)S(1)}, f32[264,128]{1,0:T(8,128)S(1)}) custom-call(f32[1,6,16,16,128]{4,3,2,1,0:T(8,128)} %adj.5, f32[23,16,128]{2,1,0:T(8,128)S(1)} %collective-permute-done.from_prev, f32[20,16,128]{2,1,0:T(8,128)S(1)} %collective-permute-done.1.from_next, f32[6,24,4,128]{3,2,1,0:T(4,128)S(1)} %collective-permute-done.7.from_side, ...), custom_call_target="tpu_custom_call" | custom-call | tf_op jit(solution)/shard_map/adjoint/pallas_call | solution.py:474
  51.7 2.2 %collective-permute-start.8 = (f32[264,128]{1,0:T(8,128)S(1)}, f32[264,128]{1,0:T(8,128)S(1)}, u32[]{:S(2)}, u32[]{:S(2)}) collective-permute-start(f32[264,128]{1,0:T(8,128)S(1)} %get-tuple-element.39), channel_id=1, source_target_pairs={{0,16},{16,0},{32,48},{48,32},{64,80},{80,64},{96,112},{112,96},{1... | collective-permute-start | bytes 405512 | tf_op jit(solution)/shard_map/ppermute | solution.py:502
  53.9 1.0 %collective-permute-done.8.other = f32[264,128]{1,0:T(8,128)S(1)} collective-permute-done((f32[264,128]{1,0:T(8,128)S(1)}, f32[264,128]{1,0:T(8,128)S(1)}, u32[]{:S(2)}, u32[]{:S(2)}) %collective-permute-start.8) | collective-permute-done | bytes 135200 | tf_op jit(solution)/shard_map/ppermute | solution.py:502
  54.9 16.6 %all_to_all.10.blocks = f32[8,40,128]{2,1,0:T(8,128)S(1)} all-to-all(f32[8,40,128]{2,1,0:T(8,128)S(1)} %pair.1), channel_id=1, replica_groups={{0,32,64,96,128,160,192,224},{16,48,80,112,144,176,208,240},{1,33,65,97..., dimensions={0} | all-to-all | bytes 327680 | tf_op jit(solution)/shard_map/all_to_all | solution.py:512
  71.5 0.6 total.1
  (17 shorter events, 0.1 us)
Async XLA Ops:
  0.6 31.1 %copy-start = (f32[1,6,16,16,128]{4,3,2,1,0:T(8,128)S(1)}, f32[1,6,16,16,128]{4,3,2,1,0:T(8,128)}, u32[]{:S(2)}) copy-start(f32[1,6,16,16,128]{4,3,2,1,0:T(8,128)} %adj.5) | copy-start | bytes 2359300
  0.6 21.3 %copy-start.1 = (f32[1,6,16,16,128]{4,3,2,1,0:T(8,128)S(1)}, f32[1,6,16,16,128]{4,3,2,1,0:T(8,128)}, u32[]{:S(2)}) copy-start(f32[1,6,16,16,128]{4,3,2,1,0:T(8,128)} %fwd.3) | copy-start | bytes 2359300
  0.7 21.3 %copy-start.2 = (f32[16,16,128]{2,1,0:T(8,128)S(1)}, f32[16,16,128]{2,1,0:T(8,128)}, u32[]{:S(2)}) copy-start(f32[16,16,128]{2,1,0:T(8,128)} %cond_h.3) | copy-start | bytes 393220
  0.7 21.3 %copy-start.3 = (f32[16,16,128]{2,1,0:T(8,128)S(1)}, f32[16,16,128]{2,1,0:T(8,128)}, u32[]{:S(2)}) copy-start(f32[16,16,128]{2,1,0:T(8,128)} %cond_v.3) | copy-start | bytes 393220
  0.7 21.3 %copy-start.4 = (f32[1,4,1,1,2,32]{5,4,3,2,1,0:T(2,128)S(1)}, f32[1,4,1,1,2,32]{5,4,3,2,1,0:T(2,128)}, u32[]{:S(2)}) copy-start(f32[1,4,1,1,2,32]{5,4,3,2,1,0:T(2,128)} %param.12) | copy-start | bytes 3076
  0.7 21.3 %copy-start.5 = (s32[1,1,32]{2,1,0:T(1,128)S(1)}, s32[1,1,32]{2,1,0:T(1,128)}, u32[]{:S(2)}) copy-start(s32[1,1,32]{2,1,0:T(1,128)} %param.15) | copy-start | bytes 388
  2.3 19.6 %collective-permute-start.4 = (f32[8,16,4,128]{3,2,1,0:T(4,128)S(1)}, f32[8,16,4,128]{3,2,1,0:T(4,128)S(1)}, u32[]{:S(2)}, u32[]{:S(2)}) collective-permute-start(f32[8,16,4,128]{3,2,1,0:T(4,128)S(1)} %get-tuple-element.26), channel_id=1, source_target_pairs={{0,1},{1,0},{2,3},{3,2},{4,5},{5,4},{6,7},{7,6},{8,9},{9,8},{10,11... | collective-permute-start | bytes 786440 | tf_op jit(solution)/shard_map/ppermute | solution.py:133
  6.2 10.4 %collective-permute-start.6 = (f32[26,4,128]{2,1,0:T(4,128)S(1)}, f32[26,4,128]{2,1,0:T(4,128)S(1)}, u32[]{:S(2)}, u32[]{:S(2)}) collective-permute-start(f32[26,4,128]{2,1,0:T(4,128)S(1)} %get-tuple-element.28), channel_id=1, source_target_pairs={{2,1},{3,0},{4,3},{5,2},{6,5},{7,4},{8,7},{9,6},{10,9},{11,8},{12,... | collective-permute-start | bytes 159752 | tf_op jit(solution)/shard_map/ppermute | solution.py:133
  7.5 14.5 %collective-permute-start.2 = (f32[29,16,128]{2,1,0:T(8,128)S(1)}, f32[29,16,128]{2,1,0:T(8,128)S(1)}, u32[]{:S(2)}, u32[]{:S(2)}) collective-permute-start(f32[29,16,128]{2,1,0:T(8,128)S(1)} %get-tuple-element.24), channel_id=1, source_target_pairs={{0,2},{1,3},{2,4},{3,5},{4,6},{5,7},{6,8},{7,9},{8,10},{9,11},{10,... | collective-permute-start | bytes 712712 | tf_op jit(solution)/shard_map/ppermute | solution.py:133
  10.4 10.2 %collective-permute-start.5 = (f32[29,4,128]{2,1,0:T(4,128)S(1)}, f32[29,4,128]{2,1,0:T(4,128)S(1)}, u32[]{:S(2)}, u32[]{:S(2)}) collective-permute-start(f32[29,4,128]{2,1,0:T(4,128)S(1)} %get-tuple-element.27), channel_id=1, source_target_pairs={{0,3},{1,2},{2,5},{3,4},{4,7},{5,6},{6,9},{7,8},{8,11},{9,10},{10,... | collective-permute-start | bytes 178184 | tf_op jit(solution)/shard_map/ppermute | solution.py:133
  15.3 6.6 %collective-permute-start.3 = (f32[26,16,128]{2,1,0:T(8,128)S(1)}, f32[26,16,128]{2,1,0:T(8,128)S(1)}, u32[]{:S(2)}, u32[]{:S(2)}) collective-permute-start(f32[26,16,128]{2,1,0:T(8,128)S(1)} %get-tuple-element.25), channel_id=1, source_target_pairs={{2,0},{3,1},{4,2},{5,3},{6,4},{7,5},{8,6},{9,7},{10,8},{11,9},{12,... | collective-permute-start | bytes 638984 | tf_op jit(solution)/shard_map/ppermute | solution.py:133
  16.6 15.1 %collective-permute-start = (f32[23,16,128]{2,1,0:T(8,128)S(1)}, f32[23,16,128]{2,1,0:T(8,128)S(1)}, u32[]{:S(2)}, u32[]{:S(2)}) collective-permute-start(f32[23,16,128]{2,1,0:T(8,128)S(1)} %get-tuple-element.22), channel_id=1, source_target_pairs={{0,2},{1,3},{2,4},{3,5},{4,6},{5,7},{6,8},{7,9},{8,10},{9,11},{10,... | collective-permute-start | bytes 565256 | tf_op jit(solution)/shard_map/ppermute | solution.py:133
  20.6 6.6 %collective-permute-start.1 = (f32[20,16,128]{2,1,0:T(8,128)S(1)}, f32[20,16,128]{2,1,0:T(8,128)S(1)}, u32[]{:S(2)}, u32[]{:S(2)}) collective-permute-start(f32[20,16,128]{2,1,0:T(8,128)S(1)} %get-tuple-element.23), channel_id=1, source_target_pairs={{2,0},{3,1},{4,2},{5,3},{6,4},{7,5},{8,6},{9,7},{10,8},{11,9},{12,... | collective-permute-start | bytes 491528 | tf_op jit(solution)/shard_map/ppermute | solution.py:133
  22.0 25.1 %copy-start.6 = (s32[1,1,16]{2,1,0:T(1,128)S(1)}, s32[1,1,16]{2,1,0:T(1,128)}, u32[]{:S(2)}) copy-start(s32[1,1,16]{2,1,0:T(1,128)} %param.14) | copy-start | bytes 196
  31.8 15.4 %collective-permute-start.7 = (f32[6,24,4,128]{3,2,1,0:T(4,128)S(1)}, f32[6,24,4,128]{3,2,1,0:T(4,128)S(1)}, u32[]{:S(2)}, u32[]{:S(2)}) collective-permute-start(f32[6,24,4,128]{3,2,1,0:T(4,128)S(1)} %pack_side.1), channel_id=1, source_target_pairs={{0,1},{1,0},{2,3},{3,2},{4,5},{5,4},{6,7},{7,6},{8,9},{9,8},{10,11... | collective-permute-start | bytes 884744 | tf_op jit(solution)/shard_map/ppermute | solution.py:133
  32.9 14.2 %all-to-all-start = ((f32[16,16,128]{2,1,0:T(8,128)}), f32[16,16,128]{2,1,0:T(8,128)S(1)}, u32[]{:S(2)}, u32[]{:S(2)}) async-start(f32[16,16,128]{2,1,0:T(8,128)} %get-tuple-element.37), calls=%async_computation | async-start | bytes 262144 | tf_op jit(solution)/shard_map/all_to_all | solution.py:473
  51.7 3.2 %collective-permute-start.8 = (f32[264,128]{1,0:T(8,128)S(1)}, f32[264,128]{1,0:T(8,128)S(1)}, u32[]{:S(2)}, u32[]{:S(2)}) collective-permute-start(f32[264,128]{1,0:T(8,128)S(1)} %get-tuple-element.39), channel_id=1, source_target_pairs={{0,16},{16,0},{32,48},{48,32},{64,80},{80,64},{96,112},{112,96},{1... | collective-permute-start | bytes 405512 | tf_op jit(solution)/shard_map/ppermute | solution.py:502

commit v5 on v4

--- a/solution.py
+++ b/solution.py
@@ -48,8 +48,8 @@
 
 
 def pack_kernel(fwd, cond_h, cond_v, adj, *refs):
-    to_next, to_prev, to_side, side_next, side_prev, adj_next, adj_prev = refs[:7]
-    bufs, sem = refs[7:11], refs[11]
+    to_next, to_prev, to_side, side_next, side_prev, adj_side = refs[:6]
+    bufs, sem = refs[6:10], refs[10]
     copies = [
         pltpu.make_async_copy(src, dst, sem.at[k])
         for k, (src, dst) in enumerate(zip((fwd, cond_h, cond_v, adj), bufs))
@@ -72,50 +72,38 @@
                     to_prev[k] = plane_of(bufs, c, x)
                     side_prev[k] = edges[x]
     copies[3].wait()
-    for k, (c, x) in enumerate(ADJ_LOW):
-        adj_next[k] = bufs[3][0, c, x]
-    for k, (c, x) in enumerate(ADJ_HIGH):
-        adj_prev[k] = bufs[3][0, c, x]
+    for c in range(6):
+        edges = [edge_of(bufs[3][0, c, x], second) for x in range(CX)]
+        for x in range(CX):
+            adj_side[c, x] = edges[x]
+        for k, (comp, x) in enumerate(ADJ_LOW):
+            if comp == c:
+                to_next[len(LOW) + k] = bufs[3][0, c, x]
+                side_next[len(LOW) + k] = edges[x]
+        for k, (comp, x) in enumerate(ADJ_HIGH):
+            if comp == c:
+                to_prev[len(HIGH) + k] = bufs[3][0, c, x]
+                side_prev[len(HIGH) + k] = edges[x]
 
 
 def pack(*arrays):
     return pl.pallas_call(
         pack_kernel,
         out_shape=[
-            shape(len(LOW), CY, NZ),
-            shape(len(HIGH), CY, NZ),
+            shape(len(LOW) + len(ADJ_LOW), CY, NZ),
+            shape(len(HIGH) + len(ADJ_HIGH), CY, NZ),
             shape(8, CX, HALO, NZ),
-            shape(len(LOW), HALO, NZ),
-            shape(len(HIGH), HALO, NZ),
-            shape(len(ADJ_LOW), CY, NZ),
-            shape(len(ADJ_HIGH), CY, NZ),
+            shape(len(LOW) + len(ADJ_LOW), HALO, NZ),
+            shape(len(HIGH) + len(ADJ_HIGH), HALO, NZ),
+            shape(6, CX, HALO, NZ),
         ],
         in_specs=[HBM] * 4,
-        out_specs=[VMEM] * 7,
+        out_specs=[VMEM] * 6,
         scratch_shapes=[pltpu.VMEM(a.shape, F32) for a in arrays]
         + [pltpu.SemaphoreType.DMA((4,))],
         compiler_params=params(),
         name="pack",
     )(*(in_hbm(a) for a in arrays))
-
-
-def pack_side_kernel(adj, from_prev, from_next, to_side):
-    second = lax.axis_index("gy") == 1
-    for c in range(6):
-        for x in range(CX):
-            to_side[c, HALO + x] = edge_of(adj[0, c, x], second)
-        filled = set(range(HALO, HALO + CX))
-        for k, (comp, x) in enumerate(ADJ_LOW):
-            if comp == c:
-                to_side[c, x - (CX - HALO)] = edge_of(from_prev[k], second)
-                filled.add(x - (CX - HALO))
-        for k, (comp, x) in enumerate(ADJ_HIGH):
-            if comp == c:
-                to_side[c, x + HALO + CX] = edge_of(from_next[k], second)
-                filled.add(x + HALO + CX)
-        for i in range(EX):
-            if i not in filled:
-                to_side[c, i] = jnp.zeros((HALO, NZ), F32)
 
 
 def pairs(dx, swap):
@@ -250,11 +238,20 @@
 def forward_kernel(fwd, cond_h, cond_v, *refs):
     halos, refs = refs[:5], refs[5:]
     observed, rec_vec, coef_out, stored_out, spread, block = refs[:6]
-    coef, stored, elec, mag, sem = refs[6:]
+    adj_halos, refs = refs[6:10], refs[10:]
+    coef, stored, elec, mag, sem = refs
     gx, gy = lax.axis_index("gx"), lax.axis_index("gy")
     tools = helpers(gy)
     lane, inside = tools[0], tools[1]
 
+    adjoint_part = (halos[0].at[len(LOW) :], halos[1].at[len(HIGH) :])
+    adjoint_part += (halos[3].at[len(LOW) :], halos[4].at[len(HIGH) :])
+    copies = [
+        pltpu.make_async_copy(src, dst, sem.at[STEPS + 1 + k])
+        for k, (src, dst) in enumerate(zip(adjoint_part, adj_halos))
+    ]
+    for copy in copies:
+        copy.start()
     comps = {c: (elec, c) if c < 3 else (mag, c - 3) for c in range(6)}
     comps |= {6: (coef, 0), 7: (coef, 2)}
     assemble(lambda c, x: plane_of((fwd, cond_h, cond_v, None), c, x), halos, comps, gy == 0)
@@ -282,8 +279,8 @@
     target = dot(
         observed[...], (lane_q == lax.broadcasted_iota(jnp.int32, (8, NZ), 0)).astype(F32), 0, 0
     )
-    copies = [pltpu.make_async_copy(coef, coef_out, sem.at[STEPS])]
-    copies[0].start()
+    copies.append(pltpu.make_async_copy(coef, coef_out, sem.at[STEPS]))
+    copies[-1].start()
     for step in range(STEPS):
         sweep(step, gx, elec, mag, coef, tools)
         stored[step] = elec[:, HALO : HALO + CX, 0:CY]
@@ -316,39 +313,39 @@
         copy.wait()
 
 
-def adjoint_kernel(adj, from_prev, from_next, from_side, coef_in, stored_in, *refs):
-    spread, blocks, foot, owner, keep, away = refs[:6]
-    coef, stored, elec, mag, inject, grad, sem = refs[6:]
+def adjoint_kernel(adj, from_prev, from_next, corner_prev, corner_next, from_side, *refs):
+    coef_in, stored_in, spread, blocks, foot, owner, keep, away = refs[:8]
+    coef, stored, elec, mag, corner_low, corner_high, inject, grad, sem = refs[8:]
     gx, gy = lax.axis_index("gx"), lax.axis_index("gy")
     tools = helpers(gy)
     lane, inside = tools[0], tools[1]
 
+    own = slice(HALO, HALO + CX)
+    moves = [
+        (corner_prev, corner_low),
+        (corner_next, corner_high),
+        (adj.at[0, 0:3], elec.at[:, own, 0:CY]),
+        (adj.at[0, 3:6], mag.at[:, own, 0:CY]),
+    ]
+    targets = [(elec, c) for c in range(3)] + [(mag, c) for c in range(3)]
+    sides = (
+        (from_prev, corner_low, ADJ_LOW, HALO - CX),
+        (from_next, corner_high, ADJ_HIGH, HALO + CX),
+    )
+    for c, (ref, index) in enumerate(targets):
+        for source, _, planes, base in sides:
+            ks = [k for k, (comp, _) in enumerate(planes) if comp == c]
+            i = planes[ks[0]][1] + base
+            moves.append(
+                (source.at[ks[0] : ks[-1] + 1], ref.at[index, i : i + len(ks), 0:CY])
+            )
+    moves.append((coef_in, coef))
+    moves += [(stored_in.at[k], stored.at[k]) for k in reversed(range(STEPS))]
     copies = [
-        pltpu.make_async_copy(adj.at[0, 0:3], elec.at[:, HALO : HALO + CX, 0:CY], sem.at[0]),
-        pltpu.make_async_copy(adj.at[0, 3:6], mag.at[:, HALO : HALO + CX, 0:CY], sem.at[1]),
-        pltpu.make_async_copy(coef_in, coef, sem.at[2]),
-    ] + [
-        pltpu.make_async_copy(stored_in.at[k], stored.at[k], sem.at[3 + k])
-        for k in reversed(range(STEPS))
+        pltpu.make_async_copy(src, dst, sem.at[k]) for k, (src, dst) in enumerate(moves)
     ]
     for copy in copies:
         copy.start()
-    zero_rows = jnp.zeros((HALO, NZ), F32)
-    zero_plane = jnp.zeros((EY, NZ), F32)
-    targets = [(elec, c) for c in range(3)] + [(mag, c) for c in range(3)]
-    for c, (ref, index) in enumerate(targets):
-        filled = set(range(HALO, HALO + CX))
-        for source, planes, base in (
-            (from_prev, ADJ_LOW, HALO - CX),
-            (from_next, ADJ_HIGH, HALO + CX),
-        ):
-            for k, (comp, x) in enumerate(planes):
-                if comp == c:
-                    ref[index, x + base, 0:CY] = source[k]
-                    filled.add(x + base)
-        for i in range(EXP):
-            if i not in filled:
-                ref[index, i] = zero_plane
 
     row8 = lax.broadcasted_iota(jnp.int32, (8, NZ), 0)
     used = row8 // HALO == gy
@@ -365,12 +362,29 @@
         inject[k, 16:24] = jnp.where(used & there, side, 0.0)
 
     first = gy == 0
+    zero_rows = jnp.zeros((HALO, NZ), F32)
+    zero_plane = jnp.zeros((EY, NZ), F32)
+
+    def put_rows(ref, index, i, rows):
+        ref[index, i, CY : CY + HALO] = jnp.where(first, rows, zero_rows)
+        ref[index, i, CY + HALO : EY] = jnp.where(first, zero_rows, rows)
+
     for c, (ref, index) in enumerate(targets):
-        for i in range(EX):
-            rows = from_side[c, i]
-            ref[index, i, CY : CY + HALO] = jnp.where(first, rows, zero_rows)
-            ref[index, i, CY + HALO : EY] = jnp.where(first, zero_rows, rows)
-    for copy in copies[:3]:
+        for x in range(CX):
+            put_rows(ref, index, HALO + x, from_side[c, x])
+    for copy in copies[:2]:
+        copy.wait()
+    for c, (ref, index) in enumerate(targets):
+        filled = set(range(HALO, HALO + CX))
+        for _, corner, planes, base in sides:
+            for k, (comp, x) in enumerate(planes):
+                if comp == c:
+                    put_rows(ref, index, x + base, corner[k])
+                    filled.add(x + base)
+        for i in range(EXP):
+            if i not in filled:
+                ref[index, i] = zero_plane
+    for copy in copies[2:-STEPS]:
         copy.wait()
 
     at_depth = lane == ZREC
@@ -386,7 +400,7 @@
                 elec[c, i] += jnp.where(at_depth, moved, 0.0)
         sweep(step, gx, elec, mag, coef, tools)
 
-        copies[3 + step].wait()
+        copies[step - STEPS].wait()
         for x in range(CX):
             ax, ay, az = (elec[c, HALO + x, 0:CY] for c in range(3))
             horizontal = ax * stored[when, 0, x] + ay * stored[when, 1, x]
@@ -430,7 +444,7 @@
 
 def on_device(cond_h, cond_v, fwd_init, adj_init, observed, footprint, owner, rec_cells):
     packed = pack(fwd_init, cond_h, cond_v, adj_init)
-    to_next, to_prev, to_side, side_next, side_prev, adj_next, adj_prev = packed
+    to_next, to_prev, to_side, side_next, side_prev, adj_side = packed
     halos = (
         send(to_next, 1, False),
         send(to_prev, -1, False),
@@ -438,58 +452,53 @@
         send(side_next, 1, True),
         send(side_prev, -1, True),
     )
-    adj_halos = (send(adj_next, 1, False), send(adj_prev, -1, False))
-    coef, stored, spread, block = pl.pallas_call(
+    from_side = send(adj_side, 0, True)
+    coef, stored, spread, block, *adj_halos = pl.pallas_call(
         forward_kernel,
         out_shape=[
             pltpu.HBM((4, EXP, EY, NZ), F32),
             pltpu.HBM((STEPS, 3, CX, CY, NZ), F32),
             shape(CY, NZ),
             shape(16, 16, NZ),
+            pltpu.HBM((len(ADJ_LOW), CY, NZ), F32),
+            pltpu.HBM((len(ADJ_HIGH), CY, NZ), F32),
+            pltpu.HBM((len(ADJ_LOW), HALO, NZ), F32),
+            pltpu.HBM((len(ADJ_HIGH), HALO, NZ), F32),
         ],
         in_specs=[VMEM] * 10,
-        out_specs=[HBM, HBM, VMEM, VMEM],
+        out_specs=[HBM, HBM, VMEM, VMEM] + [HBM] * 4,
         scratch_shapes=[
             pltpu.VMEM((4, EXP, EY, NZ), F32),
             pltpu.VMEM((STEPS, 3, CX, CY, NZ), F32),
             pltpu.VMEM((3, EXP, EY, NZ), F32),
             pltpu.VMEM((3, EXP, EY, NZ), F32),
-            pltpu.SemaphoreType.DMA((STEPS + 1,)),
+            pltpu.SemaphoreType.DMA((STEPS + 5,)),
         ],
         compiler_params=params(),
         name="forward",
     )(fwd_init, cond_h, cond_v, *halos, observed.reshape(8, 32), rec_cells.reshape(1, 32))
-    block, *adj_ready = lax.optimization_barrier((block, *adj_halos))
-    adj_side = pl.pallas_call(
-        pack_side_kernel,
-        out_shape=shape(6, EX, HALO, NZ),
-        in_specs=[VMEM] * 3,
-        out_specs=VMEM,
-        compiler_params=params(),
-        name="pack_side",
-    )(adj_init, *adj_ready)
-    block, adj_side = lax.optimization_barrier((block, adj_side))
-    from_side = send(adj_side, 0, True)
     blocks = lax.all_to_all(block, ("gx", "gy"), 0, 0, tiled=True)
     keep, away = pl.pallas_call(
         adjoint_kernel,
         out_shape=[shape(264, NZ)] * 2,
-        in_specs=[HBM] + [VMEM] * 3 + [HBM] * 2 + [VMEM] * 2 + [SMEM, SMEM],
+        in_specs=[HBM] * 5 + [VMEM] + [HBM] * 2 + [VMEM] * 2 + [SMEM, SMEM],
         out_specs=[VMEM] * 2,
         scratch_shapes=[
             pltpu.VMEM((4, EXP, EY, NZ), F32),
             pltpu.VMEM((STEPS, 3, CX, CY, NZ), F32),
             pltpu.VMEM((3, EXP, EY, NZ), F32),
             pltpu.VMEM((3, EXP, EY, NZ), F32),
+            pltpu.VMEM((len(ADJ_LOW), HALO, NZ), F32),
+            pltpu.VMEM((len(ADJ_HIGH), HALO, NZ), F32),
             pltpu.VMEM((3, EY, NZ), F32),
             pltpu.VMEM((2, CX, CY, NZ), F32),
-            pltpu.SemaphoreType.DMA((3 + STEPS,)),
+            pltpu.SemaphoreType.DMA((17 + STEPS,)),
         ],
         compiler_params=params(),
         name="adjoint",
     )(
         in_hbm(adj_init),
-        *adj_halos,
+        *(in_hbm(halo) for halo in adj_halos),
         from_side,
         in_hbm(coef),
         in_hbm(stored),

time: 72.5 us -> 74.6 us (1.029)
  waiting for transfers between devices: 13.5 us -> 21.5 us
  starting transfers between devices: 29.9 us -> 23.8 us
    ppermute x8 -> x6, waiting for transfers between devices: 6.04 us -> 14.1 us  [send(): return lax.ppermute(array, ('gx', 'gy'), pairs(dx, swap))]
    ppermute x8 -> x6, starting transfers between devices: 20.7 us -> 15.4 us  [send(): return lax.ppermute(array, ('gx', 'gy'), pairs(dx, swap))]
    all_to_all x1, starting transfers between devices: 7.06 us -> 5.75 us  [on_device(): blocks = lax.all_to_all(block, ('gx', 'gy'), 0, 0, tiled=True)]
    pallas_call x2 -> x1, Pallas kernels: 1.7 us -> 1.63 us  [pack(): pl.pallas_call(pack_kernel, out_shape=[shape(len(LOW) + len(ADJ_LOW), CY,...]
  transfers between devices with their start and end apart: 10 -> 8, of which waited for: 4 -> 4; matrix products, arithmetic and copies ran while one was open for 0% -> 0% of each run, Pallas kernels for 5% -> 5%
where the time goes in v5:
time: 74.6 us; the launch traced here: 74.2 us
  starting transfers between devices  23.8 us (32%)
  waiting for transfers between devices  21.5 us (29%)
  blocking collectives  16.6 us (22%)
  Pallas kernels  10.8 us (14%)
  between operations  1.44 us (2%)
    all_to_all x1, blocking collectives, on_device(): lax.all_to_all(paired, 'tx', 0, 0, axis_index_groups=along_z, tiled=True)  16.6 us
    ppermute x6, starting transfers between devices, send(): return lax.ppermute(array, ('gx', 'gy'), pairs(dx, swap))  15.4 us
    ppermute x6, waiting for transfers between devices, send(): return lax.ppermute(array, ('gx', 'gy'), pairs(dx, swap))  14.1 us
    all_to_all x1, waiting for transfers between devices, on_device(): blocks = lax.all_to_all(block, ('gx', 'gy'), 0, 0, tiled=True)  6.39 us
    all_to_all x1, starting transfers between devices, on_device(): blocks = lax.all_to_all(block, ('gx', 'gy'), 0, 0, tiled=True)  5.75 us
    pallas_call x1, Pallas kernels, on_device(): pl.pallas_call(adjoint_kernel, out_shape=[shape(264, NZ)] * 2, in_specs=[...  4.87 us
    pallas_call x1, Pallas kernels, on_device(): pl.pallas_call(forward_kernel, out_shape=[pltpu.HBM((4, EXP, EY, NZ), F32...  3.71 us
    ppermute x1, starting transfers between devices, on_device(): other = lax.ppermute(away, 'tx', [(t, t ^ 1) for t in range(size)])  2.67 us
  transfers between devices with their start and end apart: 8, of which 4 were waited for; matrix products, arithmetic and copies ran while one was open for 0% of the time, Pallas kernels for 5%

profile of v5, /device:TPU:1, one launch (start us, length us, event | category | flops | bytes accessed | tf_op | source)
XLA Modules:
  0.0 74.2 jit_solution(15618572310244064772)
XLA Ops:
  0.7 1.6 %pack.1 = (f32[52,16,128]{2,1,0:T(8,128)S(1)}, f32[46,16,128]{2,1,0:T(8,128)S(1)}, f32[8,16,4,128]{3,2,1,0:T(4,128)S(1)}, f32[52,4,128]{2,1,0:T(4,128)S(1)}, f32...) custom-call(f32[1,6,16,16,128]{4,3,2,1,0:T(8,128)} %fwd.3, f32[16,16,128]{2,1,0:T(8,128)} %cond_h.3, ...), custom_call_target="tpu_custom_call" | custom-call | tf_op jit(solution)/shard_map/pack/pallas_call | solution.py:90
  2.3 0.0 copy-start.5
  2.3 4.1 %collective-permute-start = (f32[52,16,128]{2,1,0:T(8,128)S(1)}, f32[52,16,128]{2,1,0:T(8,128)S(1)}, u32[]{:S(2)}, u32[]{:S(2)}) collective-permute-start(f32[52,16,128]{2,1,0:T(8,128)S(1)} %get-tuple-element.20), channel_id=1, source_target_pairs={{0,2},{1,3},{2,4},{3,5},{4,6},{5,7},{6,8},{7,9},{8,10},{9,11},{10,... | collective-permute-start | bytes 1277960 | tf_op jit(solution)/shard_map/ppermute | solution.py:121
  6.4 1.3 %collective-permute-start.1 = (f32[46,16,128]{2,1,0:T(8,128)S(1)}, f32[46,16,128]{2,1,0:T(8,128)S(1)}, u32[]{:S(2)}, u32[]{:S(2)}) collective-permute-start(f32[46,16,128]{2,1,0:T(8,128)S(1)} %get-tuple-element.21), channel_id=1, source_target_pairs={{2,0},{3,1},{4,2},{5,3},{6,4},{7,5},{8,6},{9,7},{10,8},{11,9},{12,... | collective-permute-start | bytes 1130504 | tf_op jit(solution)/shard_map/ppermute | solution.py:121
  7.7 2.7 %collective-permute-start.2 = (f32[8,16,4,128]{3,2,1,0:T(4,128)S(1)}, f32[8,16,4,128]{3,2,1,0:T(4,128)S(1)}, u32[]{:S(2)}, u32[]{:S(2)}) collective-permute-start(f32[8,16,4,128]{3,2,1,0:T(4,128)S(1)} %get-tuple-element.22), channel_id=1, source_target_pairs={{0,1},{1,0},{2,3},{3,2},{4,5},{5,4},{6,7},{7,6},{8,9},{9,8},{10,11... | collective-permute-start | bytes 786440 | tf_op jit(solution)/shard_map/ppermute | solution.py:121
  10.4 1.3 %collective-permute-start.4 = (f32[46,4,128]{2,1,0:T(4,128)S(1)}, f32[46,4,128]{2,1,0:T(4,128)S(1)}, u32[]{:S(2)}, u32[]{:S(2)}) collective-permute-start(f32[46,4,128]{2,1,0:T(4,128)S(1)} %get-tuple-element.24), channel_id=1, source_target_pairs={{2,1},{3,0},{4,3},{5,2},{6,5},{7,4},{8,7},{9,6},{10,9},{11,8},{12,... | collective-permute-start | bytes 282632 | tf_op jit(solution)/shard_map/ppermute | solution.py:121
  11.7 5.2 %collective-permute-start.3 = (f32[52,4,128]{2,1,0:T(4,128)S(1)}, f32[52,4,128]{2,1,0:T(4,128)S(1)}, u32[]{:S(2)}, u32[]{:S(2)}) collective-permute-start(f32[52,4,128]{2,1,0:T(4,128)S(1)} %get-tuple-element.23), channel_id=1, source_target_pairs={{0,3},{1,2},{2,5},{3,4},{4,7},{5,6},{6,9},{7,8},{8,11},{9,10},{10,... | collective-permute-start | bytes 319496 | tf_op jit(solution)/shard_map/ppermute | solution.py:121
  16.9 0.0 collective-permute-done.4.refs_4_
  16.9 0.9 %collective-permute-start.5 = (f32[6,16,4,128]{3,2,1,0:T(4,128)S(1)}, f32[6,16,4,128]{3,2,1,0:T(4,128)S(1)}, u32[]{:S(2)}, u32[]{:S(2)}) collective-permute-start(f32[6,16,4,128]{3,2,1,0:T(4,128)S(1)} %get-tuple-element.29), channel_id=1, source_target_pairs={{0,1},{1,0},{2,3},{3,2},{4,5},{5,4},{6,7},{7,6},{8,9},{9,8},{10,11... | collective-permute-start | bytes 589832 | tf_op jit(solution)/shard_map/ppermute | solution.py:121
  17.8 13.2 %collective-permute-done.3.refs_3_ = f32[52,4,128]{2,1,0:T(4,128)S(1)} collective-permute-done((f32[52,4,128]{2,1,0:T(4,128)S(1)}, f32[52,4,128]{2,1,0:T(4,128)S(1)}, u32[]{:S(2)}, u32[]{:S(2)}) %collective-permute-start.3) | collective-permute-done | bytes 106528 | tf_op jit(solution)/shard_map/ppermute | solution.py:121
  31.0 0.9 %collective-permute-done.2.refs_2_ = f32[8,16,4,128]{3,2,1,0:T(4,128)S(1)} collective-permute-done((f32[8,16,4,128]{3,2,1,0:T(4,128)S(1)}, f32[8,16,4,128]{3,2,1,0:T(4,128)S(1)}, u32[]{:S(2)}, u32[]{:S(2)}) %collective-permute-start.2) | collective-permute-done | bytes 262176 | tf_op jit(solution)/shard_map/ppermute | solution.py:121
  31.9 0.0 collective-permute-done.1.refs_1_
  31.9 0.0 collective-permute-done.refs_0_
  31.9 0.0 copy-done
  31.9 3.7 %forward.1 = (f32[4,28,24,128]{3,2,1,0:T(8,128)}, f32[4,3,16,16,128]{4,3,2,1,0:T(8,128)}, f32[16,128]{1,0:T(8,128)S(1)}, f32[16,16,128]{2,1,0:T(8,128)}, f32[23,...) custom-call(f32[1,6,16,16,128]{4,3,2,1,0:T(8,128)S(1)} %copy-done, ...), custom_call_target="tpu_custom_call" | custom-call | tf_op jit(solution)/shard_map/forward/pallas_call | solution.py:456
  35.7 5.7 %all-to-all-start = ((f32[16,16,128]{2,1,0:T(8,128)}), f32[16,16,128]{2,1,0:T(8,128)S(1)}, u32[]{:S(2)}, u32[]{:S(2)}) async-start(f32[16,16,128]{2,1,0:T(8,128)} %get-tuple-element.33), calls=%async_computation | async-start | bytes 262144 | tf_op jit(solution)/shard_map/all_to_all | solution.py:480
  42.1 0.0 collective-permute-done.5.from_side
  42.1 6.4 %all-to-all-done.refs_3_ = f32[16,16,128]{2,1,0:T(8,128)S(1)} async-done(((f32[16,16,128]{2,1,0:T(8,128)}), f32[16,16,128]{2,1,0:T(8,128)S(1)}, u32[]{:S(2)}, u32[]{:S(2)}) %all-to-all-start) | async-done | bytes 131104 | tf_op jit(solution)/shard_map/all_to_all | solution.py:480
  48.4 0.0 copy-done.5
  48.5 4.9 %adjoint.1 = (f32[264,128]{1,0:T(8,128)S(1)}, f32[264,128]{1,0:T(8,128)S(1)}) custom-call(f32[1,6,16,16,128]{4,3,2,1,0:T(8,128)} %adj.3, f32[23,16,128]{2,1,0:T(8,128)} %get-tuple-element.25.from_prev, f32[20,16,128]{2,1,0:T(8,128)} %get-tuple-element.26.from_next, f32[23,4,128]{2,1,0:T(4,128)} %get-tuple-element.27.corner_prev, ...), custom_call_target="tpu_custom_call" | custom-call | tf_op jit(solution)/shard_map/adjoint/pallas_call | solution.py:481
  53.3 2.7 %collective-permute-start.6 = (f32[264,128]{1,0:T(8,128)S(1)}, f32[264,128]{1,0:T(8,128)S(1)}, u32[]{:S(2)}, u32[]{:S(2)}) collective-permute-start(f32[264,128]{1,0:T(8,128)S(1)} %get-tuple-element.35), channel_id=1, source_target_pairs={{0,16},{16,0},{32,48},{48,32},{64,80},{80,64},{96,112},{112,96},{1... | collective-permute-start | bytes 405512 | tf_op jit(solution)/shard_map/ppermute | solution.py:511
  56.0 1.0 %collective-permute-done.6.other = f32[264,128]{1,0:T(8,128)S(1)} collective-permute-done((f32[264,128]{1,0:T(8,128)S(1)}, f32[264,128]{1,0:T(8,128)S(1)}, u32[]{:S(2)}, u32[]{:S(2)}) %collective-permute-start.6) | collective-permute-done | bytes 135200 | tf_op jit(solution)/shard_map/ppermute | solution.py:511
  57.0 16.6 %all_to_all.10.blocks = f32[8,40,128]{2,1,0:T(8,128)S(1)} all-to-all(f32[8,40,128]{2,1,0:T(8,128)S(1)} %pair.1), channel_id=1, replica_groups={{0,32,64,96,128,160,192,224},{16,48,80,112,144,176,208,240},{1,33,65,97..., dimensions={0} | all-to-all | bytes 327680 | tf_op jit(solution)/shard_map/all_to_all | solution.py:521
  73.6 0.6 total.1
  (10 shorter events, 0.0 us)
Async XLA Ops:
  0.6 31.3 %copy-start = (f32[1,6,16,16,128]{4,3,2,1,0:T(8,128)S(1)}, f32[1,6,16,16,128]{4,3,2,1,0:T(8,128)}, u32[]{:S(2)}) copy-start(f32[1,6,16,16,128]{4,3,2,1,0:T(8,128)} %fwd.3) | copy-start | bytes 2359300
  0.6 31.3 %copy-start.1 = (f32[16,16,128]{2,1,0:T(8,128)S(1)}, f32[16,16,128]{2,1,0:T(8,128)}, u32[]{:S(2)}) copy-start(f32[16,16,128]{2,1,0:T(8,128)} %cond_h.3) | copy-start | bytes 393220
  0.7 31.3 %copy-start.2 = (f32[16,16,128]{2,1,0:T(8,128)S(1)}, f32[16,16,128]{2,1,0:T(8,128)}, u32[]{:S(2)}) copy-start(f32[16,16,128]{2,1,0:T(8,128)} %cond_v.3) | copy-start | bytes 393220
  0.7 31.3 %copy-start.3 = (f32[1,4,1,1,2,32]{5,4,3,2,1,0:T(2,128)S(1)}, f32[1,4,1,1,2,32]{5,4,3,2,1,0:T(2,128)}, u32[]{:S(2)}) copy-start(f32[1,4,1,1,2,32]{5,4,3,2,1,0:T(2,128)} %param.12) | copy-start | bytes 3076
  0.7 31.3 %copy-start.4 = (s32[1,1,32]{2,1,0:T(1,128)S(1)}, s32[1,1,32]{2,1,0:T(1,128)}, u32[]{:S(2)}) copy-start(s32[1,1,32]{2,1,0:T(1,128)} %param.15) | copy-start | bytes 388
  2.3 46.1 %copy-start.5 = (s32[1,1,16]{2,1,0:T(1,128)S(1)}, s32[1,1,16]{2,1,0:T(1,128)}, u32[]{:S(2)}) copy-start(s32[1,1,16]{2,1,0:T(1,128)} %param.14) | copy-start | bytes 196
  2.3 29.6 %collective-permute-start = (f32[52,16,128]{2,1,0:T(8,128)S(1)}, f32[52,16,128]{2,1,0:T(8,128)S(1)}, u32[]{:S(2)}, u32[]{:S(2)}) collective-permute-start(f32[52,16,128]{2,1,0:T(8,128)S(1)} %get-tuple-element.20), channel_id=1, source_target_pairs={{0,2},{1,3},{2,4},{3,5},{4,6},{5,7},{6,8},{7,9},{8,10},{9,11},{10,... | collective-permute-start | bytes 1277960 | tf_op jit(solution)/shard_map/ppermute | solution.py:121
  6.4 25.5 %collective-permute-start.1 = (f32[46,16,128]{2,1,0:T(8,128)S(1)}, f32[46,16,128]{2,1,0:T(8,128)S(1)}, u32[]{:S(2)}, u32[]{:S(2)}) collective-permute-start(f32[46,16,128]{2,1,0:T(8,128)S(1)} %get-tuple-element.21), channel_id=1, source_target_pairs={{2,0},{3,1},{4,2},{5,3},{6,4},{7,5},{8,6},{9,7},{10,8},{11,9},{12,... | collective-permute-start | bytes 1130504 | tf_op jit(solution)/shard_map/ppermute | solution.py:121
  7.7 24.2 %collective-permute-start.2 = (f32[8,16,4,128]{3,2,1,0:T(4,128)S(1)}, f32[8,16,4,128]{3,2,1,0:T(4,128)S(1)}, u32[]{:S(2)}, u32[]{:S(2)}) collective-permute-start(f32[8,16,4,128]{3,2,1,0:T(4,128)S(1)} %get-tuple-element.22), channel_id=1, source_target_pairs={{0,1},{1,0},{2,3},{3,2},{4,5},{5,4},{6,7},{7,6},{8,9},{9,8},{10,11... | collective-permute-start | bytes 786440 | tf_op jit(solution)/shard_map/ppermute | solution.py:121
  10.4 6.5 %collective-permute-start.4 = (f32[46,4,128]{2,1,0:T(4,128)S(1)}, f32[46,4,128]{2,1,0:T(4,128)S(1)}, u32[]{:S(2)}, u32[]{:S(2)}) collective-permute-start(f32[46,4,128]{2,1,0:T(4,128)S(1)} %get-tuple-element.24), channel_id=1, source_target_pairs={{2,1},{3,0},{4,3},{5,2},{6,5},{7,4},{8,7},{9,6},{10,9},{11,8},{12,... | collective-permute-start | bytes 282632 | tf_op jit(solution)/shard_map/ppermute | solution.py:121
  11.7 19.3 %collective-permute-start.3 = (f32[52,4,128]{2,1,0:T(4,128)S(1)}, f32[52,4,128]{2,1,0:T(4,128)S(1)}, u32[]{:S(2)}, u32[]{:S(2)}) collective-permute-start(f32[52,4,128]{2,1,0:T(4,128)S(1)} %get-tuple-element.23), channel_id=1, source_target_pairs={{0,3},{1,2},{2,5},{3,4},{4,7},{5,6},{6,9},{7,8},{8,11},{9,10},{10,... | collective-permute-start | bytes 319496 | tf_op jit(solution)/shard_map/ppermute | solution.py:121
  16.9 25.1 %collective-permute-start.5 = (f32[6,16,4,128]{3,2,1,0:T(4,128)S(1)}, f32[6,16,4,128]{3,2,1,0:T(4,128)S(1)}, u32[]{:S(2)}, u32[]{:S(2)}) collective-permute-start(f32[6,16,4,128]{3,2,1,0:T(4,128)S(1)} %get-tuple-element.29), channel_id=1, source_target_pairs={{0,1},{1,0},{2,3},{3,2},{4,5},{5,4},{6,7},{7,6},{8,9},{9,8},{10,11... | collective-permute-start | bytes 589832 | tf_op jit(solution)/shard_map/ppermute | solution.py:121
  35.7 12.8 %all-to-all-start = ((f32[16,16,128]{2,1,0:T(8,128)}), f32[16,16,128]{2,1,0:T(8,128)S(1)}, u32[]{:S(2)}, u32[]{:S(2)}) async-start(f32[16,16,128]{2,1,0:T(8,128)} %get-tuple-element.33), calls=%async_computation | async-start | bytes 262144 | tf_op jit(solution)/shard_map/all_to_all | solution.py:480
  53.3 3.7 %collective-permute-start.6 = (f32[264,128]{1,0:T(8,128)S(1)}, f32[264,128]{1,0:T(8,128)S(1)}, u32[]{:S(2)}, u32[]{:S(2)}) collective-permute-start(f32[264,128]{1,0:T(8,128)S(1)} %get-tuple-element.35), channel_id=1, source_target_pairs={{0,16},{16,0},{32,48},{48,32},{64,80},{80,64},{96,112},{112,96},{1... | collective-permute-start | bytes 405512 | tf_op jit(solution)/shard_map/ppermute | solution.py:511

commit v6 on v4

--- a/solution.py
+++ b/solution.py
@@ -47,12 +47,38 @@
     return jnp.where(second, plane[0:HALO], plane[CY - HALO : CY])
 
 
-def pack_kernel(fwd, cond_h, cond_v, adj, *refs):
-    to_next, to_prev, to_side, side_next, side_prev, adj_next, adj_prev = refs[:7]
-    bufs, sem = refs[7:11], refs[11]
+def pack_adjoint_kernel(adj, to_next, to_prev, sem):
+    copies = []
+    for ref, planes in ((to_next, ADJ_LOW), (to_prev, ADJ_HIGH)):
+        for c in range(6):
+            ks = [k for k, (comp, _) in enumerate(planes) if comp == c]
+            x = planes[ks[0]][1]
+            src, dst = adj.at[0, c, x : x + len(ks)], ref.at[ks[0] : ks[-1] + 1]
+            copies.append(pltpu.make_async_copy(src, dst, sem.at[len(copies)]))
+    for copy in copies:
+        copy.start()
+    for copy in copies:
+        copy.wait()
+
+
+def pack_adjoint(adj):
+    return pl.pallas_call(
+        pack_adjoint_kernel,
+        out_shape=[shape(len(ADJ_LOW), CY, NZ), shape(len(ADJ_HIGH), CY, NZ)],
+        in_specs=[HBM],
+        out_specs=[VMEM] * 2,
+        scratch_shapes=[pltpu.SemaphoreType.DMA((12,))],
+        compiler_params=params(),
+        name="pack_adjoint",
+    )(in_hbm(adj))
+
+
+def pack_kernel(fwd, cond_h, cond_v, *refs):
+    to_next, to_prev, to_side, side_next, side_prev = refs[:5]
+    bufs, sem = refs[5:8], refs[8]
     copies = [
         pltpu.make_async_copy(src, dst, sem.at[k])
-        for k, (src, dst) in enumerate(zip((fwd, cond_h, cond_v, adj), bufs))
+        for k, (src, dst) in enumerate(zip((fwd, cond_h, cond_v), bufs))
     ]
     for copy in copies:
         copy.start()
@@ -71,11 +97,6 @@
                 if comp == c:
                     to_prev[k] = plane_of(bufs, c, x)
                     side_prev[k] = edges[x]
-    copies[3].wait()
-    for k, (c, x) in enumerate(ADJ_LOW):
-        adj_next[k] = bufs[3][0, c, x]
-    for k, (c, x) in enumerate(ADJ_HIGH):
-        adj_prev[k] = bufs[3][0, c, x]
 
 
 def pack(*arrays):
@@ -87,13 +108,11 @@
             shape(8, CX, HALO, NZ),
             shape(len(LOW), HALO, NZ),
             shape(len(HIGH), HALO, NZ),
-            shape(len(ADJ_LOW), CY, NZ),
-            shape(len(ADJ_HIGH), CY, NZ),
         ],
-        in_specs=[HBM] * 4,
-        out_specs=[VMEM] * 7,
+        in_specs=[HBM] * 3,
+        out_specs=[VMEM] * 5,
         scratch_shapes=[pltpu.VMEM(a.shape, F32) for a in arrays]
-        + [pltpu.SemaphoreType.DMA((4,))],
+        + [pltpu.SemaphoreType.DMA((3,))],
         compiler_params=params(),
         name="pack",
     )(*(in_hbm(a) for a in arrays))
@@ -429,8 +448,8 @@
 
 
 def on_device(cond_h, cond_v, fwd_init, adj_init, observed, footprint, owner, rec_cells):
-    packed = pack(fwd_init, cond_h, cond_v, adj_init)
-    to_next, to_prev, to_side, side_next, side_prev, adj_next, adj_prev = packed
+    to_next, to_prev, to_side, side_next, side_prev = pack(fwd_init, cond_h, cond_v)
+    adj_next, adj_prev = pack_adjoint(adj_init)
     halos = (
         send(to_next, 1, False),
         send(to_prev, -1, False),
@@ -468,7 +487,6 @@
         compiler_params=params(),
         name="pack_side",
     )(adj_init, *adj_ready)
-    block, adj_side = lax.optimization_barrier((block, adj_side))
     from_side = send(adj_side, 0, True)
     blocks = lax.all_to_all(block, ("gx", "gy"), 0, 0, tiled=True)
     keep, away = pl.pallas_call(

time: 72.5 us -> 72.3 us (level)
  waiting for transfers between devices: 13.5 us -> 10.4 us
  starting transfers between devices: 29.9 us -> 32 us
    ppermute x8, waiting for transfers between devices: 6.04 us -> 2.91 us  [send(): return lax.ppermute(array, ('gx', 'gy'), pairs(dx, swap))]
    all_to_all x1, starting transfers between devices: 7.06 us -> 8.88 us  [on_device(): blocks = lax.all_to_all(block, ('gx', 'gy'), 0, 0, tiled=True)]
    ppermute x1, starting transfers between devices: 2.21 us -> 3.54 us  [on_device(): other = lax.ppermute(away, 'tx', [(t, t ^ 1) for t in range(size)])]
    ppermute x8, starting transfers between devices: 20.7 us -> 19.6 us  [send(): return lax.ppermute(array, ('gx', 'gy'), pairs(dx, swap))]
    pallas_call x0 -> x1, Pallas kernels: none -> 1.01 us  [pack_adjoint(): pl.pallas_call(pack_adjoint_kernel, out_shape=[shape(len(ADJ_LOW), CY, NZ...]
  transfers between devices with their start and end apart: 10 -> 10, of which waited for: 4 -> 4; matrix products, arithmetic and copies ran while one was open for 0% -> 0% of each run, Pallas kernels for 5% -> 7%
where the time goes in v6:
time: 72.3 us; the launch traced here: 71.8 us
  starting transfers between devices  32 us (44%)
  blocking collectives  16.6 us (23%)
  Pallas kernels  11.2 us (15%)
  waiting for transfers between devices  10.4 us (14%)
  between operations  1.52 us (2%)
    ppermute x8, starting transfers between devices, send(): return lax.ppermute(array, ('gx', 'gy'), pairs(dx, swap))  19.6 us
    all_to_all x1, blocking collectives, on_device(): lax.all_to_all(paired, 'tx', 0, 0, axis_index_groups=along_z, tiled=True)  16.6 us
    all_to_all x1, starting transfers between devices, on_device(): blocks = lax.all_to_all(block, ('gx', 'gy'), 0, 0, tiled=True)  8.88 us
    all_to_all x1, waiting for transfers between devices, on_device(): blocks = lax.all_to_all(block, ('gx', 'gy'), 0, 0, tiled=True)  6.5 us
    pallas_call x1, Pallas kernels, on_device(): pl.pallas_call(adjoint_kernel, out_shape=[shape(264, NZ)] * 2, in_specs=[...  4.53 us
    pallas_call x1, Pallas kernels, on_device(): pl.pallas_call(forward_kernel, out_shape=[pltpu.HBM((4, EXP, EY, NZ), F32...  3.66 us
    ppermute x1, starting transfers between devices, on_device(): other = lax.ppermute(away, 'tx', [(t, t ^ 1) for t in range(size)])  3.54 us
    ppermute x8, waiting for transfers between devices, send(): return lax.ppermute(array, ('gx', 'gy'), pairs(dx, swap))  2.91 us
  transfers between devices with their start and end apart: 10, of which 4 were waited for; matrix products, arithmetic and copies ran while one was open for 0% of the time, Pallas kernels for 7%

profile of v6, /device:TPU:1, one launch (start us, length us, event | category | flops | bytes accessed | tf_op | source)
XLA Modules:
  0.0 71.8 jit_solution(2779057552946812800)
XLA Ops:
  0.7 1.3 %pack.1 = (f32[29,16,128]{2,1,0:T(8,128)S(1)}, f32[26,16,128]{2,1,0:T(8,128)S(1)}, f32[8,16,4,128]{3,2,1,0:T(4,128)S(1)}, f32[29,4,128]{2,1,0:T(4,128)S(1)}, f32[26,4,128]{2,1,0:T(4,128)S(1)}) custom-call(f32[1,6,16,16,128]{4,3,2,1,0:T(8,128)} %fwd.3, f32[16,16,128]{2,1,0:T(8,128)} %cond_h.3, f32[16,16,128]{2,1,0:T(8,128)} %cond_v.3), custom_call_target="tpu_custom_call" | custom-call | tf_op jit(solution)/shard_map/pack/pallas_call | solution.py:103
  2.0 0.0 copy-start
  2.0 3.8 %collective-permute-start.4 = (f32[8,16,4,128]{3,2,1,0:T(4,128)S(1)}, f32[8,16,4,128]{3,2,1,0:T(4,128)S(1)}, u32[]{:S(2)}, u32[]{:S(2)}) collective-permute-start(f32[8,16,4,128]{3,2,1,0:T(4,128)S(1)} %get-tuple-element.24), channel_id=1, source_target_pairs={{0,1},{1,0},{2,3},{3,2},{4,5},{5,4},{6,7},{7,6},{8,9},{9,8},{10,11... | collective-permute-start | bytes 786440 | tf_op jit(solution)/shard_map/ppermute | solution.py:152
  5.9 1.3 %collective-permute-start.6 = (f32[26,4,128]{2,1,0:T(4,128)S(1)}, f32[26,4,128]{2,1,0:T(4,128)S(1)}, u32[]{:S(2)}, u32[]{:S(2)}) collective-permute-start(f32[26,4,128]{2,1,0:T(4,128)S(1)} %get-tuple-element.26), channel_id=1, source_target_pairs={{2,1},{3,0},{4,3},{5,2},{6,5},{7,4},{8,7},{9,6},{10,9},{11,8},{12,... | collective-permute-start | bytes 159752 | tf_op jit(solution)/shard_map/ppermute | solution.py:152
  7.1 2.9 %collective-permute-start.2 = (f32[29,16,128]{2,1,0:T(8,128)S(1)}, f32[29,16,128]{2,1,0:T(8,128)S(1)}, u32[]{:S(2)}, u32[]{:S(2)}) collective-permute-start(f32[29,16,128]{2,1,0:T(8,128)S(1)} %get-tuple-element.22), channel_id=1, source_target_pairs={{0,2},{1,3},{2,4},{3,5},{4,6},{5,7},{6,8},{7,9},{8,10},{9,11},{10,... | collective-permute-start | bytes 712712 | tf_op jit(solution)/shard_map/ppermute | solution.py:152
  10.1 4.9 %collective-permute-start.5 = (f32[29,4,128]{2,1,0:T(4,128)S(1)}, f32[29,4,128]{2,1,0:T(4,128)S(1)}, u32[]{:S(2)}, u32[]{:S(2)}) collective-permute-start(f32[29,4,128]{2,1,0:T(4,128)S(1)} %get-tuple-element.25), channel_id=1, source_target_pairs={{0,3},{1,2},{2,5},{3,4},{4,7},{5,6},{6,9},{7,8},{8,11},{9,10},{10,... | collective-permute-start | bytes 178184 | tf_op jit(solution)/shard_map/ppermute | solution.py:152
  15.0 1.3 %collective-permute-start.3 = (f32[26,16,128]{2,1,0:T(8,128)S(1)}, f32[26,16,128]{2,1,0:T(8,128)S(1)}, u32[]{:S(2)}, u32[]{:S(2)}) collective-permute-start(f32[26,16,128]{2,1,0:T(8,128)S(1)} %get-tuple-element.23), channel_id=1, source_target_pairs={{2,0},{3,1},{4,2},{5,3},{6,4},{7,5},{8,6},{9,7},{10,8},{11,9},{12,... | collective-permute-start | bytes 638984 | tf_op jit(solution)/shard_map/ppermute | solution.py:152
  16.3 1.0 %pack_adjoint.1 = (f32[23,16,128]{2,1,0:T(8,128)S(1)}, f32[20,16,128]{2,1,0:T(8,128)S(1)}) custom-call(f32[1,6,16,16,128]{4,3,2,1,0:T(8,128)} %adj.5), custom_call_target="tpu_custom_call" | custom-call | tf_op jit(solution)/shard_map/pack_adjoint/pallas_call | solution.py:65
  17.3 0.0 collective-permute-done.6.refs_4_
  17.3 4.0 %collective-permute-start = (f32[23,16,128]{2,1,0:T(8,128)S(1)}, f32[23,16,128]{2,1,0:T(8,128)S(1)}, u32[]{:S(2)}, u32[]{:S(2)}) collective-permute-start(f32[23,16,128]{2,1,0:T(8,128)S(1)} %get-tuple-element.20), channel_id=1, source_target_pairs={{0,2},{1,3},{2,4},{3,5},{4,6},{5,7},{6,8},{7,9},{8,10},{9,11},{10,... | collective-permute-start | bytes 565256 | tf_op jit(solution)/shard_map/ppermute | solution.py:152
  21.3 1.3 %collective-permute-start.1 = (f32[20,16,128]{2,1,0:T(8,128)S(1)}, f32[20,16,128]{2,1,0:T(8,128)S(1)}, u32[]{:S(2)}, u32[]{:S(2)}) collective-permute-start(f32[20,16,128]{2,1,0:T(8,128)S(1)} %get-tuple-element.21), channel_id=1, source_target_pairs={{2,0},{3,1},{4,2},{5,3},{6,4},{7,5},{8,6},{9,7},{10,8},{11,9},{12,... | collective-permute-start | bytes 491528 | tf_op jit(solution)/shard_map/ppermute | solution.py:152
  22.7 0.0 copy-start.6
  22.7 3.7 %forward.1 = (f32[4,28,24,128]{3,2,1,0:T(8,128)}, f32[4,3,16,16,128]{4,3,2,1,0:T(8,128)}, f32[16,128]{1,0:T(8,128)S(1)}, f32[16,16,128]{2,1,0:T(8,128)}) custom-call(f32[1,6,16,16,128]{4,3,2,1,0:T(8,128)S(1)} %copy-done.1, f32[16,16,128]{2,1,0:T(8,128)S(1)} %copy-done.2, f32[16,16,128]{2,1,0:T(8,128)S(1)} %copy-done.3, ...), custom_call_target="tpu_custom_call" | custom-call | tf_op jit(solution)/shard_map/forward/pallas_call | solution.py:461
  26.4 1.5 %collective-permute-done.1.from_next = f32[20,16,128]{2,1,0:T(8,128)S(1)} collective-permute-done((f32[20,16,128]{2,1,0:T(8,128)S(1)}, f32[20,16,128]{2,1,0:T(8,128)S(1)}, u32[]{:S(2)}, u32[]{:S(2)}) %collective-permute-start.1) | collective-permute-done | bytes 163872 | tf_op jit(solution)/shard_map/ppermute | solution.py:152
  27.9 1.4 %collective-permute-done.from_prev = f32[23,16,128]{2,1,0:T(8,128)S(1)} collective-permute-done((f32[23,16,128]{2,1,0:T(8,128)S(1)}, f32[23,16,128]{2,1,0:T(8,128)S(1)}, u32[]{:S(2)}, u32[]{:S(2)}) %collective-permute-start) | collective-permute-done | bytes 188448 | tf_op jit(solution)/shard_map/ppermute | solution.py:152
  29.3 0.1 pack_side.1
  29.3 0.1 collective-permute-start.7
  29.4 8.9 %all-to-all-start = ((f32[16,16,128]{2,1,0:T(8,128)}), f32[16,16,128]{2,1,0:T(8,128)S(1)}, u32[]{:S(2)}, u32[]{:S(2)}) async-start(f32[16,16,128]{2,1,0:T(8,128)} %get-tuple-element.33), calls=%async_computation | async-start | bytes 262144 | tf_op jit(solution)/shard_map/all_to_all | solution.py:491
  39.0 6.5 %all-to-all-done.refs_1_ = f32[16,16,128]{2,1,0:T(8,128)S(1)} async-done(((f32[16,16,128]{2,1,0:T(8,128)}), f32[16,16,128]{2,1,0:T(8,128)S(1)}, u32[]{:S(2)}, u32[]{:S(2)}) %all-to-all-start) | async-done | bytes 131104 | tf_op jit(solution)/shard_map/all_to_all | solution.py:491
  45.5 4.5 %adjoint.1 = (f32[264,128]{1,0:T(8,128)S(1)}, f32[264,128]{1,0:T(8,128)S(1)}) custom-call(f32[1,6,16,16,128]{4,3,2,1,0:T(8,128)} %adj.5, f32[23,16,128]{2,1,0:T(8,128)S(1)} %collective-permute-done.from_prev, f32[20,16,128]{2,1,0:T(8,128)S(1)} %collective-permute-done.1.from_next, f32[6,24,4,128]{3,2,1,0:T(4,128)S(1)} %collective-permute-done.7.from_side, ...), custom_call_target="tpu_custom_call" | custom-call | tf_op jit(solution)/shard_map/adjoint/pallas_call | solution.py:492
  50.0 3.5 %collective-permute-start.8 = (f32[264,128]{1,0:T(8,128)S(1)}, f32[264,128]{1,0:T(8,128)S(1)}, u32[]{:S(2)}, u32[]{:S(2)}) collective-permute-start(f32[264,128]{1,0:T(8,128)S(1)} %get-tuple-element.35), channel_id=1, source_target_pairs={{0,16},{16,0},{32,48},{48,32},{64,80},{80,64},{96,112},{112,96},{1... | collective-permute-start | bytes 405512 | tf_op jit(solution)/shard_map/ppermute | solution.py:520
  53.6 1.0 %collective-permute-done.8.other = f32[264,128]{1,0:T(8,128)S(1)} collective-permute-done((f32[264,128]{1,0:T(8,128)S(1)}, f32[264,128]{1,0:T(8,128)S(1)}, u32[]{:S(2)}, u32[]{:S(2)}) %collective-permute-start.8) | collective-permute-done | bytes 135200 | tf_op jit(solution)/shard_map/ppermute | solution.py:520
  54.6 16.6 %all_to_all.10.blocks = f32[8,40,128]{2,1,0:T(8,128)S(1)} all-to-all(f32[8,40,128]{2,1,0:T(8,128)S(1)} %pair.1), channel_id=1, replica_groups={{0,32,64,96,128,160,192,224},{16,48,80,112,144,176,208,240},{1,33,65,97..., dimensions={0} | all-to-all | bytes 327680 | tf_op jit(solution)/shard_map/all_to_all | solution.py:530
  71.2 0.6 total.1
  (18 shorter events, 0.1 us)
Async XLA Ops:
  0.6 22.0 %copy-start.1 = (f32[1,6,16,16,128]{4,3,2,1,0:T(8,128)S(1)}, f32[1,6,16,16,128]{4,3,2,1,0:T(8,128)}, u32[]{:S(2)}) copy-start(f32[1,6,16,16,128]{4,3,2,1,0:T(8,128)} %fwd.3) | copy-start | bytes 2359300
  0.6 22.0 %copy-start.2 = (f32[16,16,128]{2,1,0:T(8,128)S(1)}, f32[16,16,128]{2,1,0:T(8,128)}, u32[]{:S(2)}) copy-start(f32[16,16,128]{2,1,0:T(8,128)} %cond_h.3) | copy-start | bytes 393220
  0.7 22.0 %copy-start.3 = (f32[16,16,128]{2,1,0:T(8,128)S(1)}, f32[16,16,128]{2,1,0:T(8,128)}, u32[]{:S(2)}) copy-start(f32[16,16,128]{2,1,0:T(8,128)} %cond_v.3) | copy-start | bytes 393220
  0.7 22.0 %copy-start.4 = (f32[1,4,1,1,2,32]{5,4,3,2,1,0:T(2,128)S(1)}, f32[1,4,1,1,2,32]{5,4,3,2,1,0:T(2,128)}, u32[]{:S(2)}) copy-start(f32[1,4,1,1,2,32]{5,4,3,2,1,0:T(2,128)} %param.12) | copy-start | bytes 3076
  0.7 22.0 %copy-start.5 = (s32[1,1,32]{2,1,0:T(1,128)S(1)}, s32[1,1,32]{2,1,0:T(1,128)}, u32[]{:S(2)}) copy-start(s32[1,1,32]{2,1,0:T(1,128)} %param.15) | copy-start | bytes 388
  2.0 27.3 %copy-start = (f32[1,6,16,16,128]{4,3,2,1,0:T(8,128)S(1)}, f32[1,6,16,16,128]{4,3,2,1,0:T(8,128)}, u32[]{:S(2)}) copy-start(f32[1,6,16,16,128]{4,3,2,1,0:T(8,128)} %adj.5) | copy-start | bytes 2359300
  2.0 20.6 %collective-permute-start.4 = (f32[8,16,4,128]{3,2,1,0:T(4,128)S(1)}, f32[8,16,4,128]{3,2,1,0:T(4,128)S(1)}, u32[]{:S(2)}, u32[]{:S(2)}) collective-permute-start(f32[8,16,4,128]{3,2,1,0:T(4,128)S(1)} %get-tuple-element.24), channel_id=1, source_target_pairs={{0,1},{1,0},{2,3},{3,2},{4,5},{5,4},{6,7},{7,6},{8,9},{9,8},{10,11... | collective-permute-start | bytes 786440 | tf_op jit(solution)/shard_map/ppermute | solution.py:152
  5.9 11.4 %collective-permute-start.6 = (f32[26,4,128]{2,1,0:T(4,128)S(1)}, f32[26,4,128]{2,1,0:T(4,128)S(1)}, u32[]{:S(2)}, u32[]{:S(2)}) collective-permute-start(f32[26,4,128]{2,1,0:T(4,128)S(1)} %get-tuple-element.26), channel_id=1, source_target_pairs={{2,1},{3,0},{4,3},{5,2},{6,5},{7,4},{8,7},{9,6},{10,9},{11,8},{12,... | collective-permute-start | bytes 159752 | tf_op jit(solution)/shard_map/ppermute | solution.py:152
  7.1 15.5 %collective-permute-start.2 = (f32[29,16,128]{2,1,0:T(8,128)S(1)}, f32[29,16,128]{2,1,0:T(8,128)S(1)}, u32[]{:S(2)}, u32[]{:S(2)}) collective-permute-start(f32[29,16,128]{2,1,0:T(8,128)S(1)} %get-tuple-element.22), channel_id=1, source_target_pairs={{0,2},{1,3},{2,4},{3,5},{4,6},{5,7},{6,8},{7,9},{8,10},{9,11},{10,... | collective-permute-start | bytes 712712 | tf_op jit(solution)/shard_map/ppermute | solution.py:152
  10.1 11.2 %collective-permute-start.5 = (f32[29,4,128]{2,1,0:T(4,128)S(1)}, f32[29,4,128]{2,1,0:T(4,128)S(1)}, u32[]{:S(2)}, u32[]{:S(2)}) collective-permute-start(f32[29,4,128]{2,1,0:T(4,128)S(1)} %get-tuple-element.25), channel_id=1, source_target_pairs={{0,3},{1,2},{2,5},{3,4},{4,7},{5,6},{6,9},{7,8},{8,11},{9,10},{10,... | collective-permute-start | bytes 178184 | tf_op jit(solution)/shard_map/ppermute | solution.py:152
  15.0 7.6 %collective-permute-start.3 = (f32[26,16,128]{2,1,0:T(8,128)S(1)}, f32[26,16,128]{2,1,0:T(8,128)S(1)}, u32[]{:S(2)}, u32[]{:S(2)}) collective-permute-start(f32[26,16,128]{2,1,0:T(8,128)S(1)} %get-tuple-element.23), channel_id=1, source_target_pairs={{2,0},{3,1},{4,2},{5,3},{6,4},{7,5},{8,6},{9,7},{10,8},{11,9},{12,... | collective-permute-start | bytes 638984 | tf_op jit(solution)/shard_map/ppermute | solution.py:152
  17.3 12.0 %collective-permute-start = (f32[23,16,128]{2,1,0:T(8,128)S(1)}, f32[23,16,128]{2,1,0:T(8,128)S(1)}, u32[]{:S(2)}, u32[]{:S(2)}) collective-permute-start(f32[23,16,128]{2,1,0:T(8,128)S(1)} %get-tuple-element.20), channel_id=1, source_target_pairs={{0,2},{1,3},{2,4},{3,5},{4,6},{5,7},{6,8},{7,9},{8,10},{9,11},{10,... | collective-permute-start | bytes 565256 | tf_op jit(solution)/shard_map/ppermute | solution.py:152
  21.3 6.6 %collective-permute-start.1 = (f32[20,16,128]{2,1,0:T(8,128)S(1)}, f32[20,16,128]{2,1,0:T(8,128)S(1)}, u32[]{:S(2)}, u32[]{:S(2)}) collective-permute-start(f32[20,16,128]{2,1,0:T(8,128)S(1)} %get-tuple-element.21), channel_id=1, source_target_pairs={{2,0},{3,1},{4,2},{5,3},{6,4},{7,5},{8,6},{9,7},{10,8},{11,9},{12,... | collective-permute-start | bytes 491528 | tf_op jit(solution)/shard_map/ppermute | solution.py:152
  22.7 22.8 %copy-start.6 = (s32[1,1,16]{2,1,0:T(1,128)S(1)}, s32[1,1,16]{2,1,0:T(1,128)}, u32[]{:S(2)}) copy-start(s32[1,1,16]{2,1,0:T(1,128)} %param.14) | copy-start | bytes 196
  29.3 16.1 %collective-permute-start.7 = (f32[6,24,4,128]{3,2,1,0:T(4,128)S(1)}, f32[6,24,4,128]{3,2,1,0:T(4,128)S(1)}, u32[]{:S(2)}, u32[]{:S(2)}) collective-permute-start(f32[6,24,4,128]{3,2,1,0:T(4,128)S(1)} %pack_side.1), channel_id=1, source_target_pairs={{0,1},{1,0},{2,3},{3,2},{4,5},{5,4},{6,7},{7,6},{8,9},{9,8},{10,11... | collective-permute-start | bytes 884744 | tf_op jit(solution)/shard_map/ppermute | solution.py:152
  29.4 16.0 %all-to-all-start = ((f32[16,16,128]{2,1,0:T(8,128)}), f32[16,16,128]{2,1,0:T(8,128)S(1)}, u32[]{:S(2)}, u32[]{:S(2)}) async-start(f32[16,16,128]{2,1,0:T(8,128)} %get-tuple-element.33), calls=%async_computation | async-start | bytes 262144 | tf_op jit(solution)/shard_map/all_to_all | solution.py:491
  50.0 4.5 %collective-permute-start.8 = (f32[264,128]{1,0:T(8,128)S(1)}, f32[264,128]{1,0:T(8,128)S(1)}, u32[]{:S(2)}, u32[]{:S(2)}) collective-permute-start(f32[264,128]{1,0:T(8,128)S(1)} %get-tuple-element.35), channel_id=1, source_target_pairs={{0,16},{16,0},{32,48},{48,32},{64,80},{80,64},{96,112},{112,96},{1... | collective-permute-start | bytes 405512 | tf_op jit(solution)/shard_map/ppermute | solution.py:520

commit v7 on v6

--- a/solution.py
+++ b/solution.py
@@ -76,14 +76,15 @@
 def pack_kernel(fwd, cond_h, cond_v, *refs):
     to_next, to_prev, to_side, side_next, side_prev = refs[:5]
     bufs, sem = refs[5:8], refs[8]
+    moves = [(fwd.at[0, 0:3], bufs[0].at[0, 0:3]), (fwd.at[0, 3:6], bufs[0].at[0, 3:6])]
+    moves += [(cond_h, bufs[1]), (cond_v, bufs[2])]
     copies = [
-        pltpu.make_async_copy(src, dst, sem.at[k])
-        for k, (src, dst) in enumerate(zip((fwd, cond_h, cond_v), bufs))
+        pltpu.make_async_copy(src, dst, sem.at[k]) for k, (src, dst) in enumerate(moves)
     ]
     for copy in copies:
         copy.start()
     second = lax.axis_index("gy") == 1
-    for which, comps in ((0, range(6)), (1, (6,)), (2, (7,))):
+    for which, comps in ((0, range(3)), (1, range(3, 6)), (2, (6,)), (3, (7,))):
         copies[which].wait()
         for c in comps:
             edges = [edge_of(plane_of(bufs, c, x), second) for x in range(CX)]
@@ -112,7 +113,7 @@
         in_specs=[HBM] * 3,
         out_specs=[VMEM] * 5,
         scratch_shapes=[pltpu.VMEM(a.shape, F32) for a in arrays]
-        + [pltpu.SemaphoreType.DMA((3,))],
+        + [pltpu.SemaphoreType.DMA((4,))],
         compiler_params=params(),
         name="pack",
     )(*(in_hbm(a) for a in arrays))
@@ -389,9 +390,7 @@
             rows = from_side[c, i]
             ref[index, i, CY : CY + HALO] = jnp.where(first, rows, zero_rows)
             ref[index, i, CY + HALO : EY] = jnp.where(first, zero_rows, rows)
-    for copy in copies[:3]:
-        copy.wait()
-
+    copies[0].wait()
     at_depth = lane == ZREC
 
     for step in range(STEPS):
@@ -403,6 +402,9 @@
             for c in range(2):
                 moved = pltpu.roll(source, (ZREC - (x * 8 + 2 * when + c)) % NZ, 1)
                 elec[c, i] += jnp.where(at_depth, moved, 0.0)
+        if step == 0:
+            copies[1].wait()
+            copies[2].wait()
         sweep(step, gx, elec, mag, coef, tools)
 
         copies[3 + step].wait()

time: 72.3 us -> 72.1 us (level)
  no operation moved by 1% of the time
where the time goes in v7:
time: 72.1 us; the launch traced here: 71.6 us
  starting transfers between devices  32 us (44%)
  blocking collectives  16.6 us (23%)
  Pallas kernels  11 us (15%)
  waiting for transfers between devices  10.4 us (14%)
  between operations  1.52 us (2%)
    ppermute x8, starting transfers between devices, send(): return lax.ppermute(array, ('gx', 'gy'), pairs(dx, swap))  19.6 us
    all_to_all x1, blocking collectives, on_device(): lax.all_to_all(paired, 'tx', 0, 0, axis_index_groups=along_z, tiled=True)  16.6 us
    all_to_all x1, starting transfers between devices, on_device(): blocks = lax.all_to_all(block, ('gx', 'gy'), 0, 0, tiled=True)  8.88 us
    all_to_all x1, waiting for transfers between devices, on_device(): blocks = lax.all_to_all(block, ('gx', 'gy'), 0, 0, tiled=True)  6.5 us
    pallas_call x1, Pallas kernels, on_device(): pl.pallas_call(adjoint_kernel, out_shape=[shape(264, NZ)] * 2, in_specs=[...  4.36 us
    pallas_call x1, Pallas kernels, on_device(): pl.pallas_call(forward_kernel, out_shape=[pltpu.HBM((4, EXP, EY, NZ), F32...  3.66 us
    ppermute x1, starting transfers between devices, on_device(): other = lax.ppermute(away, 'tx', [(t, t ^ 1) for t in range(size)])  3.54 us
    ppermute x8, waiting for transfers between devices, send(): return lax.ppermute(array, ('gx', 'gy'), pairs(dx, swap))  2.91 us
  transfers between devices with their start and end apart: 10, of which 4 were waited for; matrix products, arithmetic and copies ran while one was open for 0% of the time, Pallas kernels for 7%

profile of v7, /device:TPU:1, one launch (start us, length us, event | category | flops | bytes accessed | tf_op | source)
XLA Modules:
  0.0 71.6 jit_solution(8946983663973834250)
XLA Ops:
  0.7 1.3 %pack.1 = (f32[29,16,128]{2,1,0:T(8,128)S(1)}, f32[26,16,128]{2,1,0:T(8,128)S(1)}, f32[8,16,4,128]{3,2,1,0:T(4,128)S(1)}, f32[29,4,128]{2,1,0:T(4,128)S(1)}, f32[26,4,128]{2,1,0:T(4,128)S(1)}) custom-call(f32[1,6,16,16,128]{4,3,2,1,0:T(8,128)} %fwd.3, f32[16,16,128]{2,1,0:T(8,128)} %cond_h.3, f32[16,16,128]{2,1,0:T(8,128)} %cond_v.3), custom_call_target="tpu_custom_call" | custom-call | tf_op jit(solution)/shard_map/pack/pallas_call | solution.py:104
  2.0 0.0 copy-start
  2.0 3.8 %collective-permute-start.4 = (f32[8,16,4,128]{3,2,1,0:T(4,128)S(1)}, f32[8,16,4,128]{3,2,1,0:T(4,128)S(1)}, u32[]{:S(2)}, u32[]{:S(2)}) collective-permute-start(f32[8,16,4,128]{3,2,1,0:T(4,128)S(1)} %get-tuple-element.24), channel_id=1, source_target_pairs={{0,1},{1,0},{2,3},{3,2},{4,5},{5,4},{6,7},{7,6},{8,9},{9,8},{10,11... | collective-permute-start | bytes 786440 | tf_op jit(solution)/shard_map/ppermute | solution.py:153
  5.8 1.3 %collective-permute-start.6 = (f32[26,4,128]{2,1,0:T(4,128)S(1)}, f32[26,4,128]{2,1,0:T(4,128)S(1)}, u32[]{:S(2)}, u32[]{:S(2)}) collective-permute-start(f32[26,4,128]{2,1,0:T(4,128)S(1)} %get-tuple-element.26), channel_id=1, source_target_pairs={{2,1},{3,0},{4,3},{5,2},{6,5},{7,4},{8,7},{9,6},{10,9},{11,8},{12,... | collective-permute-start | bytes 159752 | tf_op jit(solution)/shard_map/ppermute | solution.py:153
  7.1 2.9 %collective-permute-start.2 = (f32[29,16,128]{2,1,0:T(8,128)S(1)}, f32[29,16,128]{2,1,0:T(8,128)S(1)}, u32[]{:S(2)}, u32[]{:S(2)}) collective-permute-start(f32[29,16,128]{2,1,0:T(8,128)S(1)} %get-tuple-element.22), channel_id=1, source_target_pairs={{0,2},{1,3},{2,4},{3,5},{4,6},{5,7},{6,8},{7,9},{8,10},{9,11},{10,... | collective-permute-start | bytes 712712 | tf_op jit(solution)/shard_map/ppermute | solution.py:153
  10.1 4.9 %collective-permute-start.5 = (f32[29,4,128]{2,1,0:T(4,128)S(1)}, f32[29,4,128]{2,1,0:T(4,128)S(1)}, u32[]{:S(2)}, u32[]{:S(2)}) collective-permute-start(f32[29,4,128]{2,1,0:T(4,128)S(1)} %get-tuple-element.25), channel_id=1, source_target_pairs={{0,3},{1,2},{2,5},{3,4},{4,7},{5,6},{6,9},{7,8},{8,11},{9,10},{10,... | collective-permute-start | bytes 178184 | tf_op jit(solution)/shard_map/ppermute | solution.py:153
  14.9 1.3 %collective-permute-start.3 = (f32[26,16,128]{2,1,0:T(8,128)S(1)}, f32[26,16,128]{2,1,0:T(8,128)S(1)}, u32[]{:S(2)}, u32[]{:S(2)}) collective-permute-start(f32[26,16,128]{2,1,0:T(8,128)S(1)} %get-tuple-element.23), channel_id=1, source_target_pairs={{2,0},{3,1},{4,2},{5,3},{6,4},{7,5},{8,6},{9,7},{10,8},{11,9},{12,... | collective-permute-start | bytes 638984 | tf_op jit(solution)/shard_map/ppermute | solution.py:153
  16.2 1.0 %pack_adjoint.1 = (f32[23,16,128]{2,1,0:T(8,128)S(1)}, f32[20,16,128]{2,1,0:T(8,128)S(1)}) custom-call(f32[1,6,16,16,128]{4,3,2,1,0:T(8,128)} %adj.5), custom_call_target="tpu_custom_call" | custom-call | tf_op jit(solution)/shard_map/pack_adjoint/pallas_call | solution.py:65
  17.3 4.0 %collective-permute-start = (f32[23,16,128]{2,1,0:T(8,128)S(1)}, f32[23,16,128]{2,1,0:T(8,128)S(1)}, u32[]{:S(2)}, u32[]{:S(2)}) collective-permute-start(f32[23,16,128]{2,1,0:T(8,128)S(1)} %get-tuple-element.20), channel_id=1, source_target_pairs={{0,2},{1,3},{2,4},{3,5},{4,6},{5,7},{6,8},{7,9},{8,10},{9,11},{10,... | collective-permute-start | bytes 565256 | tf_op jit(solution)/shard_map/ppermute | solution.py:153
  21.3 0.0 collective-permute-done.5.refs_3_
  21.3 1.3 %collective-permute-start.1 = (f32[20,16,128]{2,1,0:T(8,128)S(1)}, f32[20,16,128]{2,1,0:T(8,128)S(1)}, u32[]{:S(2)}, u32[]{:S(2)}) collective-permute-start(f32[20,16,128]{2,1,0:T(8,128)S(1)} %get-tuple-element.21), channel_id=1, source_target_pairs={{2,0},{3,1},{4,2},{5,3},{6,4},{7,5},{8,6},{9,7},{10,8},{11,9},{12,... | collective-permute-start | bytes 491528 | tf_op jit(solution)/shard_map/ppermute | solution.py:153
  22.7 0.0 copy-start.6
  22.7 3.7 %forward.1 = (f32[4,28,24,128]{3,2,1,0:T(8,128)}, f32[4,3,16,16,128]{4,3,2,1,0:T(8,128)}, f32[16,128]{1,0:T(8,128)S(1)}, f32[16,16,128]{2,1,0:T(8,128)}) custom-call(f32[1,6,16,16,128]{4,3,2,1,0:T(8,128)S(1)} %copy-done.1, f32[16,16,128]{2,1,0:T(8,128)S(1)} %copy-done.2, f32[16,16,128]{2,1,0:T(8,128)S(1)} %copy-done.3, ...), custom_call_target="tpu_custom_call" | custom-call | tf_op jit(solution)/shard_map/forward/pallas_call | solution.py:463
  26.4 1.5 %collective-permute-done.1.from_next = f32[20,16,128]{2,1,0:T(8,128)S(1)} collective-permute-done((f32[20,16,128]{2,1,0:T(8,128)S(1)}, f32[20,16,128]{2,1,0:T(8,128)S(1)}, u32[]{:S(2)}, u32[]{:S(2)}) %collective-permute-start.1) | collective-permute-done | bytes 163872 | tf_op jit(solution)/shard_map/ppermute | solution.py:153
  27.9 1.4 %collective-permute-done.from_prev = f32[23,16,128]{2,1,0:T(8,128)S(1)} collective-permute-done((f32[23,16,128]{2,1,0:T(8,128)S(1)}, f32[23,16,128]{2,1,0:T(8,128)S(1)}, u32[]{:S(2)}, u32[]{:S(2)}) %collective-permute-start) | collective-permute-done | bytes 188448 | tf_op jit(solution)/shard_map/ppermute | solution.py:153
  29.2 0.1 pack_side.1
  29.3 0.1 collective-permute-start.7
  29.4 8.9 %all-to-all-start = ((f32[16,16,128]{2,1,0:T(8,128)}), f32[16,16,128]{2,1,0:T(8,128)S(1)}, u32[]{:S(2)}, u32[]{:S(2)}) async-start(f32[16,16,128]{2,1,0:T(8,128)} %get-tuple-element.33), calls=%async_computation | async-start | bytes 262144 | tf_op jit(solution)/shard_map/all_to_all | solution.py:493
  39.0 6.5 %all-to-all-done.refs_1_ = f32[16,16,128]{2,1,0:T(8,128)S(1)} async-done(((f32[16,16,128]{2,1,0:T(8,128)}), f32[16,16,128]{2,1,0:T(8,128)S(1)}, u32[]{:S(2)}, u32[]{:S(2)}) %all-to-all-start) | async-done | bytes 131104 | tf_op jit(solution)/shard_map/all_to_all | solution.py:493
  45.5 4.4 %adjoint.1 = (f32[264,128]{1,0:T(8,128)S(1)}, f32[264,128]{1,0:T(8,128)S(1)}) custom-call(f32[1,6,16,16,128]{4,3,2,1,0:T(8,128)} %adj.5, f32[23,16,128]{2,1,0:T(8,128)S(1)} %collective-permute-done.from_prev, f32[20,16,128]{2,1,0:T(8,128)S(1)} %collective-permute-done.1.from_next, f32[6,24,4,128]{3,2,1,0:T(4,128)S(1)} %collective-permute-done.7.from_side, ...), custom_call_target="tpu_custom_call" | custom-call | tf_op jit(solution)/shard_map/adjoint/pallas_call | solution.py:494
  49.8 3.5 %collective-permute-start.8 = (f32[264,128]{1,0:T(8,128)S(1)}, f32[264,128]{1,0:T(8,128)S(1)}, u32[]{:S(2)}, u32[]{:S(2)}) collective-permute-start(f32[264,128]{1,0:T(8,128)S(1)} %get-tuple-element.35), channel_id=1, source_target_pairs={{0,16},{16,0},{32,48},{48,32},{64,80},{80,64},{96,112},{112,96},{1... | collective-permute-start | bytes 405512 | tf_op jit(solution)/shard_map/ppermute | solution.py:522
  53.4 1.0 %collective-permute-done.8.other = f32[264,128]{1,0:T(8,128)S(1)} collective-permute-done((f32[264,128]{1,0:T(8,128)S(1)}, f32[264,128]{1,0:T(8,128)S(1)}, u32[]{:S(2)}, u32[]{:S(2)}) %collective-permute-start.8) | collective-permute-done | bytes 135200 | tf_op jit(solution)/shard_map/ppermute | solution.py:522
  54.4 16.6 %all_to_all.10.blocks = f32[8,40,128]{2,1,0:T(8,128)S(1)} all-to-all(f32[8,40,128]{2,1,0:T(8,128)S(1)} %pair.1), channel_id=1, replica_groups={{0,32,64,96,128,160,192,224},{16,48,80,112,144,176,208,240},{1,33,65,97..., dimensions={0} | all-to-all | bytes 327680 | tf_op jit(solution)/shard_map/all_to_all | solution.py:532
  71.0 0.6 total.1
  (18 shorter events, 0.1 us)
Async XLA Ops:
  0.6 22.0 %copy-start.1 = (f32[1,6,16,16,128]{4,3,2,1,0:T(8,128)S(1)}, f32[1,6,16,16,128]{4,3,2,1,0:T(8,128)}, u32[]{:S(2)}) copy-start(f32[1,6,16,16,128]{4,3,2,1,0:T(8,128)} %fwd.3) | copy-start | bytes 2359300
  0.6 22.0 %copy-start.2 = (f32[16,16,128]{2,1,0:T(8,128)S(1)}, f32[16,16,128]{2,1,0:T(8,128)}, u32[]{:S(2)}) copy-start(f32[16,16,128]{2,1,0:T(8,128)} %cond_h.3) | copy-start | bytes 393220
  0.7 22.0 %copy-start.3 = (f32[16,16,128]{2,1,0:T(8,128)S(1)}, f32[16,16,128]{2,1,0:T(8,128)}, u32[]{:S(2)}) copy-start(f32[16,16,128]{2,1,0:T(8,128)} %cond_v.3) | copy-start | bytes 393220
  0.7 22.0 %copy-start.4 = (f32[1,4,1,1,2,32]{5,4,3,2,1,0:T(2,128)S(1)}, f32[1,4,1,1,2,32]{5,4,3,2,1,0:T(2,128)}, u32[]{:S(2)}) copy-start(f32[1,4,1,1,2,32]{5,4,3,2,1,0:T(2,128)} %param.12) | copy-start | bytes 3076
  0.7 22.0 %copy-start.5 = (s32[1,1,32]{2,1,0:T(1,128)S(1)}, s32[1,1,32]{2,1,0:T(1,128)}, u32[]{:S(2)}) copy-start(s32[1,1,32]{2,1,0:T(1,128)} %param.15) | copy-start | bytes 388
  2.0 27.3 %copy-start = (f32[1,6,16,16,128]{4,3,2,1,0:T(8,128)S(1)}, f32[1,6,16,16,128]{4,3,2,1,0:T(8,128)}, u32[]{:S(2)}) copy-start(f32[1,6,16,16,128]{4,3,2,1,0:T(8,128)} %adj.5) | copy-start | bytes 2359300
  2.0 20.6 %collective-permute-start.4 = (f32[8,16,4,128]{3,2,1,0:T(4,128)S(1)}, f32[8,16,4,128]{3,2,1,0:T(4,128)S(1)}, u32[]{:S(2)}, u32[]{:S(2)}) collective-permute-start(f32[8,16,4,128]{3,2,1,0:T(4,128)S(1)} %get-tuple-element.24), channel_id=1, source_target_pairs={{0,1},{1,0},{2,3},{3,2},{4,5},{5,4},{6,7},{7,6},{8,9},{9,8},{10,11... | collective-permute-start | bytes 786440 | tf_op jit(solution)/shard_map/ppermute | solution.py:153
  5.8 11.4 %collective-permute-start.6 = (f32[26,4,128]{2,1,0:T(4,128)S(1)}, f32[26,4,128]{2,1,0:T(4,128)S(1)}, u32[]{:S(2)}, u32[]{:S(2)}) collective-permute-start(f32[26,4,128]{2,1,0:T(4,128)S(1)} %get-tuple-element.26), channel_id=1, source_target_pairs={{2,1},{3,0},{4,3},{5,2},{6,5},{7,4},{8,7},{9,6},{10,9},{11,8},{12,... | collective-permute-start | bytes 159752 | tf_op jit(solution)/shard_map/ppermute | solution.py:153
  7.1 15.5 %collective-permute-start.2 = (f32[29,16,128]{2,1,0:T(8,128)S(1)}, f32[29,16,128]{2,1,0:T(8,128)S(1)}, u32[]{:S(2)}, u32[]{:S(2)}) collective-permute-start(f32[29,16,128]{2,1,0:T(8,128)S(1)} %get-tuple-element.22), channel_id=1, source_target_pairs={{0,2},{1,3},{2,4},{3,5},{4,6},{5,7},{6,8},{7,9},{8,10},{9,11},{10,... | collective-permute-start | bytes 712712 | tf_op jit(solution)/shard_map/ppermute | solution.py:153
  10.1 11.2 %collective-permute-start.5 = (f32[29,4,128]{2,1,0:T(4,128)S(1)}, f32[29,4,128]{2,1,0:T(4,128)S(1)}, u32[]{:S(2)}, u32[]{:S(2)}) collective-permute-start(f32[29,4,128]{2,1,0:T(4,128)S(1)} %get-tuple-element.25), channel_id=1, source_target_pairs={{0,3},{1,2},{2,5},{3,4},{4,7},{5,6},{6,9},{7,8},{8,11},{9,10},{10,... | collective-permute-start | bytes 178184 | tf_op jit(solution)/shard_map/ppermute | solution.py:153
  14.9 7.6 %collective-permute-start.3 = (f32[26,16,128]{2,1,0:T(8,128)S(1)}, f32[26,16,128]{2,1,0:T(8,128)S(1)}, u32[]{:S(2)}, u32[]{:S(2)}) collective-permute-start(f32[26,16,128]{2,1,0:T(8,128)S(1)} %get-tuple-element.23), channel_id=1, source_target_pairs={{2,0},{3,1},{4,2},{5,3},{6,4},{7,5},{8,6},{9,7},{10,8},{11,9},{12,... | collective-permute-start | bytes 638984 | tf_op jit(solution)/shard_map/ppermute | solution.py:153
  17.3 12.0 %collective-permute-start = (f32[23,16,128]{2,1,0:T(8,128)S(1)}, f32[23,16,128]{2,1,0:T(8,128)S(1)}, u32[]{:S(2)}, u32[]{:S(2)}) collective-permute-start(f32[23,16,128]{2,1,0:T(8,128)S(1)} %get-tuple-element.20), channel_id=1, source_target_pairs={{0,2},{1,3},{2,4},{3,5},{4,6},{5,7},{6,8},{7,9},{8,10},{9,11},{10,... | collective-permute-start | bytes 565256 | tf_op jit(solution)/shard_map/ppermute | solution.py:153
  21.3 6.6 %collective-permute-start.1 = (f32[20,16,128]{2,1,0:T(8,128)S(1)}, f32[20,16,128]{2,1,0:T(8,128)S(1)}, u32[]{:S(2)}, u32[]{:S(2)}) collective-permute-start(f32[20,16,128]{2,1,0:T(8,128)S(1)} %get-tuple-element.21), channel_id=1, source_target_pairs={{2,0},{3,1},{4,2},{5,3},{6,4},{7,5},{8,6},{9,7},{10,8},{11,9},{12,... | collective-permute-start | bytes 491528 | tf_op jit(solution)/shard_map/ppermute | solution.py:153
  22.7 22.8 %copy-start.6 = (s32[1,1,16]{2,1,0:T(1,128)S(1)}, s32[1,1,16]{2,1,0:T(1,128)}, u32[]{:S(2)}) copy-start(s32[1,1,16]{2,1,0:T(1,128)} %param.14) | copy-start | bytes 196
  29.3 16.1 %collective-permute-start.7 = (f32[6,24,4,128]{3,2,1,0:T(4,128)S(1)}, f32[6,24,4,128]{3,2,1,0:T(4,128)S(1)}, u32[]{:S(2)}, u32[]{:S(2)}) collective-permute-start(f32[6,24,4,128]{3,2,1,0:T(4,128)S(1)} %pack_side.1), channel_id=1, source_target_pairs={{0,1},{1,0},{2,3},{3,2},{4,5},{5,4},{6,7},{7,6},{8,9},{9,8},{10,11... | collective-permute-start | bytes 884744 | tf_op jit(solution)/shard_map/ppermute | solution.py:153
  29.4 16.0 %all-to-all-start = ((f32[16,16,128]{2,1,0:T(8,128)}), f32[16,16,128]{2,1,0:T(8,128)S(1)}, u32[]{:S(2)}, u32[]{:S(2)}) async-start(f32[16,16,128]{2,1,0:T(8,128)} %get-tuple-element.33), calls=%async_computation | async-start | bytes 262144 | tf_op jit(solution)/shard_map/all_to_all | solution.py:493
  49.8 4.5 %collective-permute-start.8 = (f32[264,128]{1,0:T(8,128)S(1)}, f32[264,128]{1,0:T(8,128)S(1)}, u32[]{:S(2)}, u32[]{:S(2)}) collective-permute-start(f32[264,128]{1,0:T(8,128)S(1)} %get-tuple-element.35), channel_id=1, source_target_pairs={{0,16},{16,0},{32,48},{48,32},{64,80},{80,64},{96,112},{112,96},{1... | collective-permute-start | bytes 405512 | tf_op jit(solution)/shard_map/ppermute | solution.py:522
